TPU v7x, 256 devices: a whole 4x4x8 slice. The times are simulated.
256 devices in a mesh: dp: 8 (over z), expert: 32 (over y, x, core).
Axes of the slice: x: 4, y: 4, z: 8, core: 2. Of those that a mesh axis runs over, the one named last changes fastest.
Arguments:
- x_routed: bfloat16 [32, 1024, 2048], P(None, 'dp', 'expert'), may hold values from -10 to 10
- grad_out: bfloat16 [32, 1024, 768], P(None, 'dp'), may hold values from -15 to 15
- block_counts: int32 [8, 32], P('dp'), may hold values from 1 to 8, as said below
Outputs:
- update: bfloat16 [32, 2048, 768], P(None, 'expert')
Inputs may be any that keep to these rules, and one draw needn't show every extreme that they name: Rows of replica r beyond 16 * block_counts[r, e] of expert e are padding; on every replica one expert has all 128 rows live.
All inputs are finite; a program needn't handle non-finite values.
Results may differ from a plain program's by a relative error of at most 0.0065.
Values may be sent and summed in bfloat16 or wider, within the bound.
No kernel may reach another device: no remote copies, remote signals or barrier semaphores. Data moves between devices by JAX's collectives and lax.ppermute only.
A program may use at most 64 MiB of HBM per device.

v0:
```python
import functools
import math

import jax
import jax.numpy as jnp
from jax import lax
from jax.experimental import pallas as pl
from jax.experimental.pallas import tpu as pltpu
from jax.sharding import Mesh, PartitionSpec as P

BLK = 16
NEWTON_FIRST = 3.4445
NEWTON_SECOND = -4.775
NEWTON_THIRD = 2.0315
EPSILON = 1e-07


NZ, NY, NX, NC = 8, 4, 4, 2
COLS, CAP = 64, 128
SIDES = (0, 1, 3, 2)

VMEM = pl.BlockSpec(memory_space=pltpu.VMEM)
SMEM = pl.BlockSpec(memory_space=pltpu.SMEM)
ANY = pl.BlockSpec(memory_space=pl.ANY)


def shift(n, k):
    return [(i, (i + k) % n) for i in range(n)]


def near(*arrays):
    return [pltpu.with_memory_space_constraint(a, pltpu.VMEM) for a in arrays]


def dot(a, b):
    return jnp.dot(a, b, preferred_element_type=jnp.float32)


def gram_of(rows):
    return lax.dot_general(rows, rows, (((0,), (0,)), ((), ())), preferred_element_type=jnp.float32)


def pack_kernel(count_ref, x_ref, g_ref, *refs):
    x_outs, g_out, sems = refs[:NY], refs[NY], refs[NY + 1]
    y = lax.axis_index("y")
    block = NC * lax.axis_index("x") + lax.axis_index("c")
    copies = [pltpu.make_async_copy(g_ref.at[y, :, block], g_out, sems.at[NY])]
    for k, dy in enumerate(SIDES):
        source = x_ref.at[lax.rem(y + dy, NY)]
        copies.append(pltpu.make_async_copy(source, x_outs[k], sems.at[k]))
    for copy in copies:
        copy.start()
    for copy in copies:
        copy.wait()
    for plane in range(NZ):

        @pl.when(block >= count_ref[0, NZ * y + plane])
        def _():
            g_out[plane] = jnp.zeros(g_out.shape[1:], g_out.dtype)


def grad_kernel(xt_ref, *refs):
    pieces, out_ref, rows = refs[:-2], refs[-2], refs[-1]
    x, c = lax.axis_index("x"), lax.axis_index("c")
    half = NZ // 2
    for core in range(NC):
        own, right, left, far_a, far_b = pieces[5 * core : 5 * core + 5]
        for offset, ref, first in (
            (0, own, 0),
            (3, right, 0),
            (1, left, 0),
            (2, far_a, 0),
            (2, far_b, half),
        ):
            block = NC * lax.rem(x + offset, NX) + (c if core == 0 else 1 - c)
            for r in range(ref.shape[0]):
                rows[first + r, block] = ref[r]
    total = None
    for r in range(0, NZ, 2):
        lhs = jnp.concatenate(
            [xt_ref[r].reshape(NY * COLS, CAP), xt_ref[r + 1].reshape(NY * COLS, CAP)], axis=1
        )
        part = dot(lhs, rows[r : r + 2].reshape(2 * CAP, rows.shape[-1]))
        total = part if total is None else total + part
    out_ref[...] = total.astype(jnp.bfloat16)


def newton_kernel(scale, mine_ref, other_ref, far_a_ref, far_b_ref, grad_ref, *out_refs):
    far = jnp.concatenate([far_a_ref[...], far_b_ref[...]], axis=0)
    raw = mine_ref[...] + other_ref[...] + gram_of(far)
    n = raw.shape[0]
    diagonal = lax.broadcasted_iota(jnp.int32, (n, n), 0) == lax.broadcasted_iota(
        jnp.int32, (n, n), 1
    )
    norm = jnp.sqrt(jnp.sum(jnp.where(diagonal, raw, 0.0), keepdims=True))
    inverse = 1.0 / (norm + EPSILON)
    gram = raw * inverse * inverse
    gram16 = gram.astype(jnp.bfloat16)
    first = (NEWTON_SECOND * gram + NEWTON_THIRD * dot(gram16, gram16)).astype(jnp.bfloat16)
    grad = grad_ref[...]
    current = inverse * (NEWTON_FIRST * grad.astype(jnp.float32) + dot(grad, first))
    half = NEWTON_FIRST * gram + dot(first, gram16)
    gram = NEWTON_FIRST * half + dot(half.astype(jnp.bfloat16), first)
    gram16 = gram.astype(jnp.bfloat16)
    second = (NEWTON_SECOND * gram + NEWTON_THIRD * dot(gram16, gram16)).astype(jnp.bfloat16)
    out = NEWTON_FIRST * current + dot(current.astype(jnp.bfloat16), second)
    out = (scale * out).astype(jnp.bfloat16)
    for k in range(NY):
        out_refs[k][...] = out[COLS * k : COLS * (k + 1)].reshape(out_refs[k].shape)


def place_kernel(places, n, aliased, *refs):
    pieces, (out_ref, sems) = refs[:n], refs[n + aliased :]
    y, z = lax.axis_index("y"), lax.axis_index("z")
    copies = []
    for piece, (dys, dz, row) in zip(pieces, places):
        for index, dy in enumerate(dys):
            target = out_ref.at[
                lax.rem(y + dy, NY), lax.rem(z + dz + NZ, NZ), pl.ds(row, piece.shape[1])
            ]
            copies.append(pltpu.make_async_copy(piece.at[index], target, sems.at[len(copies)]))
            copies[-1].start()
    for copy in copies:
        copy.wait()


def place(out, width, items):
    pieces = near(*(piece for piece, _ in items))
    places = [where for _, where in items]
    n = len(pieces)
    aliased = out is not None
    return pl.pallas_call(
        functools.partial(place_kernel, places, n, int(aliased)),
        out_shape=jax.ShapeDtypeStruct((NY, NZ, COLS, width), jnp.bfloat16),
        in_specs=[VMEM] * n + [ANY] * aliased,
        out_specs=ANY,
        scratch_shapes=[pltpu.SemaphoreType.DMA((sum(len(w[0]) for w in places),))],
        input_output_aliases={n: 0} if aliased else {},
        compiler_params=pltpu.CompilerParams(vmem_limit_bytes=4 << 20),
    )(*pieces, *([out] if aliased else []))


def move(value, axis, size, by):
    return lax.ppermute(value, axis, shift(size, by))


def body(x, g, counts):
    width = g.shape[2]

    far_hbm = functools.partial(pltpu.with_memory_space_constraint, memory_space=pltpu.HBM)
    *sides, mine = pl.pallas_call(
        pack_kernel,
        out_shape=[pltpu.VMEM((NZ, COLS, CAP), jnp.bfloat16)] * NY
        + [pltpu.VMEM((NZ, BLK, width), jnp.bfloat16)],
        in_specs=[SMEM, ANY, ANY],
        out_specs=[VMEM] * (NY + 1),
        scratch_shapes=[pltpu.SemaphoreType.DMA((NY + 1,))],
        compiler_params=pltpu.CompilerParams(vmem_limit_bytes=2 << 20),
        name="pack",
    )(
        counts,
        far_hbm(x.transpose(0, 2, 1).reshape(NY, NZ, COLS, CAP)),
        far_hbm(g.reshape(NY, NZ, CAP // BLK, BLK, width)),
    )
    sides = [sides[0]] + [move(sides[k], "y", NY, SIDES[k]) for k in range(1, NY)]
    own = lax.all_to_all(mine, "z", 0, 0, tiled=True)
    xz = lax.all_to_all(jnp.stack(sides, axis=1), "z", 0, 0, tiled=True)

    right = move(own, "x", NX, 1)
    left = move(own, "x", NX, -1)
    far_a = move(right[: NZ // 2], "x", NX, 1)
    far_b = move(left[NZ // 2 :], "x", NX, -1)
    pieces = [own, right, left, far_a, far_b]
    pieces = pieces + [move(p, "c", NC, 1) for p in pieces]

    grad = pl.pallas_call(
        grad_kernel,
        out_shape=pltpu.VMEM((NY * COLS, width), jnp.bfloat16),
        in_specs=[VMEM] * 11,
        out_specs=VMEM,
        scratch_shapes=[pltpu.VMEM((NZ, CAP // BLK, BLK, width), jnp.bfloat16)],
        compiler_params=pltpu.CompilerParams(vmem_limit_bytes=12 << 20),
        name="grad",
    )(*near(xz, *pieces))

    mid = NY * COLS // 2
    right = move(grad, "x", NX, 1)
    left = move(grad, "x", NX, -1)
    total = gram_of(grad)
    far_a = move(right[:mid], "x", NX, 1)
    far_b = move(left[mid:], "x", NX, -1)
    total = total + (gram_of(right) + gram_of(left))
    other = move(total, "c", NC, 1)
    other_far_a = move(far_a, "c", NC, 1)
    other_far_b = move(far_b, "c", NC, 1)
    total = total + (gram_of(far_a) + gram_of(far_b))

    pieces = pl.pallas_call(
        functools.partial(newton_kernel, math.sqrt(2048)),
        out_shape=[pltpu.VMEM((1, COLS, width), jnp.bfloat16)] * NY,
        in_specs=[VMEM] * 5,
        out_specs=[VMEM] * NY,
        compiler_params=pltpu.CompilerParams(vmem_limit_bytes=32 << 20),
        name="newton",
    )(*near(total, other, other_far_a, other_far_b, grad))

    moved = [move(pieces[k], "y", NY, -SIDES[k]) for k in range(1, NY)]
    half = COLS // 2
    a_dys, b_dys = (0,), SIDES[1:]

    def step(right, left):
        return [move(right, "z", NZ, 1), move(left, "z", NZ, -1)]

    def halves(right, left):
        return step(right[:, :half], left[:, half:])

    a1 = step(pieces[0], pieces[0])
    a2 = step(*a1)
    *moved, a2[0], a2[1] = lax.optimization_barrier((*moved, *a2))
    moved = jnp.stack([m[0] for m in moved])
    a3 = step(*a2)
    b1 = step(moved, moved)
    *a3, b1[0], b1[1] = lax.optimization_barrier((*a3, *b1))
    a4 = halves(*a3)
    b2 = step(*b1)
    *a4, b2[0], b2[1] = lax.optimization_barrier((*a4, *b2))
    b3 = step(*b2)
    b4 = halves(*b3)

    def items(pair, dys, n):
        if n == 4:
            return [(pair[0], (dys, 4, 0)), (pair[1], (dys, 4, half))]
        return [(pair[0], (dys, -n, 0)), (pair[1], (dys, n, 0))]

    out = place(
        None,
        width,
        [(pieces[0], (a_dys, 0, 0)), (moved, (b_dys, 0, 0))]
        + items(a1, a_dys, 1)
        + items(a2, a_dys, 2)
        + items(a3, a_dys, 3)
        + items(b1, b_dys, 1),
    )
    out = place(out, width, items(a4, a_dys, 4) + items(b2, b_dys, 2) + items(b3, b_dys, 3))
    out = place(out, width, items(b4, b_dys, 4))
    return out.reshape(NY * NZ, COLS, width)


def solution(mesh):
    fine = Mesh(mesh.devices.reshape(NZ, NY, NX, NC), ("z", "y", "x", "c"))
    return jax.shard_map(
        body,
        mesh=fine,
        in_specs=(P(None, "z", ("y", "x", "c")), P(None, "z", None), P("z", None)),
        out_specs=P(None, ("y", "x", "c"), None),
        check_vma=False,
    )
```

profile of v0, /device:TPU:8, one launch (start us, length us, event | category | flops | bytes accessed | tf_op | source)
XLA Modules:
  0.0 133.9 jit_solution(8671626617422892423)
XLA Ops:
  0.0 0.7 copy-done
  0.7 2.5 %pack.1 = (bf16[8,64,128]{2,1,0:T(8,128)(2,1)S(1)}, bf16[8,64,128]{2,1,0:T(8,128)(2,1)S(1)}, bf16[8,64,128]{2,1,0:T(8,128)(2,1)S(1)}, bf16[8,64,128]{2,1,0:T(8,128)(2,1)S(1)}, bf16[8,16,768]{2,1,0:T(8,128)(2,1)}) custom-call(s32[1,32]{1,0:T(1,128)S(1)} %copy-done, bf16[4,8,64,128]{3,2,1,0:T(8,128)(2,1)} %bitcast.21, bf16[4,8,8,16,768]{4,3,2,1,0:T(8,128)(2,1)} %bitcast.20), custom_call_target="tpu_custom_call" | custom-call | tf_op jit(solution)/shard_map/pack/pallas_call | solution.py:151
  3.1 8.5 %all-to-all-start.1 = ((bf16[8,16,768]{2,1,0:T(8,128)(2,1)}), bf16[8,16,768]{2,1,0:T(8,128)(2,1)S(1)}, u32[]{:S(2)}, u32[]{:S(2)}) async-start(bf16[8,16,768]{2,1,0:T(8,128)(2,1)} %get-tuple-element.31), calls=%async_computation.1 | async-start | bytes 393216 | tf_op jit(solution)/shard_map/all_to_all | solution.py:166
  11.6 1.6 %collective-permute-start = (bf16[8,64,128]{2,1,0:T(8,128)(2,1)S(1)}, bf16[8,64,128]{2,1,0:T(8,128)(2,1)S(1)}, u32[]{:S(2)}, u32[]{:S(2)}) collective-permute-start(bf16[8,64,128]{2,1,0:T(8,128)(2,1)S(1)} %get-tuple-element.28), channel_id=1, source_target_pairs={{0,8},{8,16},{16,24},{24,0},{1,9},{9,17},{17,25},{25,1},{2,10},{10... | collective-permute-start | bytes 393224 | tf_op jit(solution)/shard_map/ppermute | solution.py:144
  13.6 2.3 %collective-permute-start.2 = (bf16[8,64,128]{2,1,0:T(8,128)(2,1)S(1)}, bf16[8,64,128]{2,1,0:T(8,128)(2,1)S(1)}, u32[]{:S(2)}, u32[]{:S(2)}) collective-permute-start(bf16[8,64,128]{2,1,0:T(8,128)(2,1)S(1)} %get-tuple-element.30), channel_id=1, source_target_pairs={{0,16},{8,24},{16,0},{24,8},{1,17},{9,25},{17,1},{25,9},{2,18},{10... | collective-permute-start | bytes 393224 | tf_op jit(solution)/shard_map/ppermute | solution.py:144
  15.9 0.6 collective-permute-done
  16.6 2.8 %collective-permute-done.1 = bf16[8,64,128]{2,1,0:T(8,128)(2,1)S(1)} collective-permute-done((bf16[8,64,128]{2,1,0:T(8,128)(2,1)S(1)}, bf16[8,64,128]{2,1,0:T(8,128)(2,1)S(1)}, u32[]{:S(2)}, u32[]{:S(2)}) %collective-permute-start.1) | collective-permute-done | bytes 131104 | tf_op jit(solution)/shard_map/ppermute | solution.py:144
  19.4 2.0 %collective-permute-done.2 = bf16[8,64,128]{2,1,0:T(8,128)(2,1)S(1)} collective-permute-done((bf16[8,64,128]{2,1,0:T(8,128)(2,1)S(1)}, bf16[8,64,128]{2,1,0:T(8,128)(2,1)S(1)}, u32[]{:S(2)}, u32[]{:S(2)}) %collective-permute-start.2) | collective-permute-done | bytes 131104 | tf_op jit(solution)/shard_map/ppermute | solution.py:144
  21.4 0.9 pad_maximum_fusion
  22.3 6.9 %all-to-all-start = ((bf16[8,4,64,128]{3,2,1,0:T(8,128)(2,1)}), bf16[8,4,64,128]{3,2,1,0:T(8,128)(2,1)S(1)}, u32[]{:S(2)}, u32[]{:S(2)}) async-start(bf16[8,4,64,128]{3,2,1,0:T(8,128)(2,1)} %pad_maximum_fusion), calls=%async_computation | async-start | bytes 1048576 | tf_op jit(solution)/shard_map/all_to_all | solution.py:167
  29.2 2.8 %collective-permute-start.4 = (bf16[8,16,768]{2,1,0:T(8,128)(2,1)S(1)}, bf16[8,16,768]{2,1,0:T(8,128)(2,1)S(1)}, u32[]{:S(2)}, u32[]{:S(2)}) collective-permute-start(bf16[8,16,768]{2,1,0:T(8,128)(2,1)S(1)} %all-to-all-done.1.refs_0_), channel_id=1, source_target_pairs={{0,6},{2,0},{4,2},{6,4},{1,7},{3,1},{5,3},{7,5},{8,14},{10,8},{12,... | collective-permute-start | bytes 589832 | tf_op jit(solution)/shard_map/ppermute | solution.py:144
  32.0 3.2 %collective-permute-done.4.refs_2_ = bf16[8,16,768]{2,1,0:T(8,128)(2,1)S(1)} collective-permute-done((bf16[8,16,768]{2,1,0:T(8,128)(2,1)S(1)}, bf16[8,16,768]{2,1,0:T(8,128)(2,1)S(1)}, u32[]{:S(2)}, u32[]{:S(2)}) %collective-permute-start.4) | collective-permute-done | bytes 196640 | tf_op jit(solution)/shard_map/ppermute | solution.py:144
  35.2 3.8 %collective-permute-start.6 = (bf16[4,16,768]{2,1,0:T(8,128)(2,1)S(1)}, bf16[4,16,768]{2,1,0:T(8,128)(2,1)S(1)}, u32[]{:S(2)}, u32[]{:S(2)}) collective-permute-start(bf16[4,16,768]{2,1,0:T(8,128)(2,1)S(1)} %slice.33), channel_id=1, source_target_pairs={{0,6},{2,0},{4,2},{6,4},{1,7},{3,1},{5,3},{7,5},{8,14},{10,8},{12,... | collective-permute-start | bytes 294920 | tf_op jit(solution)/shard_map/ppermute | solution.py:144
  39.7 1.5 %collective-permute-done.6.refs_4_ = bf16[4,16,768]{2,1,0:T(8,128)(2,1)S(1)} collective-permute-done((bf16[4,16,768]{2,1,0:T(8,128)(2,1)S(1)}, bf16[4,16,768]{2,1,0:T(8,128)(2,1)S(1)}, u32[]{:S(2)}, u32[]{:S(2)}) %collective-permute-start.6) | collective-permute-done | bytes 98336 | tf_op jit(solution)/shard_map/ppermute | solution.py:144
  41.2 3.7 %collective-permute-done.5.refs_3_ = bf16[4,16,768]{2,1,0:T(8,128)(2,1)S(1)} collective-permute-done((bf16[4,16,768]{2,1,0:T(8,128)(2,1)S(1)}, bf16[4,16,768]{2,1,0:T(8,128)(2,1)S(1)}, u32[]{:S(2)}, u32[]{:S(2)}) %collective-permute-start.5) | collective-permute-done | bytes 98336 | tf_op jit(solution)/shard_map/ppermute | solution.py:144
  44.9 1.3 collective-permute-done.10.refs_8_
  46.2 0.7 grad.1.grad_ref
  47.0 3.2 %collective-permute-start.13 = (bf16[256,768]{1,0:T(8,128)(2,1)S(1)}, bf16[256,768]{1,0:T(8,128)(2,1)S(1)}, u32[]{:S(2)}, u32[]{:S(2)}) collective-permute-start(bf16[256,768]{1,0:T(8,128)(2,1)S(1)} %grad.1.grad_ref), channel_id=1, source_target_pairs={{0,6},{2,0},{4,2},{6,4},{1,7},{3,1},{5,3},{7,5},{8,14},{10,8},{12,... | collective-permute-start | bytes 1179656 | tf_op jit(solution)/shard_map/ppermute | solution.py:144
  50.2 9.1 %collective-permute-done.12 = bf16[256,768]{1,0:T(8,128)(2,1)S(1)} collective-permute-done((bf16[256,768]{1,0:T(8,128)(2,1)S(1)}, bf16[256,768]{1,0:T(8,128)(2,1)S(1)}, u32[]{:S(2)}, u32[]{:S(2)}) %collective-permute-start.12) | collective-permute-done | bytes 393248 | tf_op jit(solution)/shard_map/ppermute | solution.py:144
  59.3 0.5 fusion
  59.9 0.5 fusion.1
  60.4 0.5 add_add_fusion.1
  61.2 2.5 %collective-permute-start.15 = (bf16[128,768]{1,0:T(8,128)(2,1)S(1)}, bf16[128,768]{1,0:T(8,128)(2,1)S(1)}, u32[]{:S(2)}, u32[]{:S(2)}) collective-permute-start(bf16[128,768]{1,0:T(8,128)(2,1)S(1)} %slice.35), channel_id=1, source_target_pairs={{0,6},{2,0},{4,2},{6,4},{1,7},{3,1},{5,3},{7,5},{8,14},{10,8},{12,... | collective-permute-start | bytes 589832 | tf_op jit(solution)/shard_map/ppermute | solution.py:144
  63.8 4.8 %collective-permute-done.15 = bf16[128,768]{1,0:T(8,128)(2,1)S(1)} collective-permute-done((bf16[128,768]{1,0:T(8,128)(2,1)S(1)}, bf16[128,768]{1,0:T(8,128)(2,1)S(1)}, u32[]{:S(2)}, u32[]{:S(2)}) %collective-permute-start.15) | collective-permute-done | bytes 196640 | tf_op jit(solution)/shard_map/ppermute | solution.py:144
  68.6 3.5 %collective-permute-done.14 = bf16[128,768]{1,0:T(8,128)(2,1)S(1)} collective-permute-done((bf16[128,768]{1,0:T(8,128)(2,1)S(1)}, bf16[128,768]{1,0:T(8,128)(2,1)S(1)}, u32[]{:S(2)}, u32[]{:S(2)}) %collective-permute-start.14) | collective-permute-done | bytes 196640 | tf_op jit(solution)/shard_map/ppermute | solution.py:144
  72.5 0.5 add_add_fusion.mine_ref
  73.5 5.6 %newton.1 = (bf16[1,64,768]{2,1,0:T(8,128)(2,1)S(1)}, bf16[1,64,768]{2,1,0:T(8,128)(2,1)S(1)}, bf16[1,64,768]{2,1,0:T(8,128)(2,1)S(1)}, bf16[1,64,768]{2,1,0:T(8,128)(2,1)S(1)}) custom-call(f32[768,768]{1,0:T(8,128)S(1)} %add_add_fusion.mine_ref, f32[768,768]{1,0:T(8,128)S(1)} %collective-permute-done.16.other_ref, ...), custom_call_target="tpu_custom_call" | custom-call | tf_op jit(solution)/shard_map/newton/pallas_call | solution.py:198
  79.1 3.3 %collective-permute-start.24 = (bf16[1,64,768]{2,1,0:T(8,128)(2,1)S(1)}, bf16[1,64,768]{2,1,0:T(8,128)(2,1)S(1)}, u32[]{:S(2)}, u32[]{:S(2)}) collective-permute-start(bf16[1,64,768]{2,1,0:T(8,128)(2,1)S(1)} %get-tuple-element.35.refs_0_), channel_id=1, source_target_pairs={{0,224},{32,0},{64,32},{96,64},{128,96},{160,128},{192,160},{224,1... | collective-permute-start | bytes 294920 | tf_op jit(solution)/shard_map/ppermute | solution.py:144
  82.4 1.2 collective-permute-start.19
  83.5 0.9 collective-permute-start.20
  84.4 3.1 %collective-permute-start.21 = (bf16[1,64,768]{2,1,0:T(8,128)(2,1)S(1)}, bf16[1,64,768]{2,1,0:T(8,128)(2,1)S(1)}, u32[]{:S(2)}, u32[]{:S(2)}) collective-permute-start(bf16[1,64,768]{2,1,0:T(8,128)(2,1)S(1)} %get-tuple-element.34), channel_id=1, source_target_pairs={{0,16},{8,24},{16,0},{24,8},{1,17},{9,25},{17,1},{25,9},{2,18},{10... | collective-permute-start | bytes 294920 | tf_op jit(solution)/shard_map/ppermute | solution.py:144
  87.5 3.2 %collective-permute-start.25 = (bf16[1,64,768]{2,1,0:T(8,128)(2,1)S(1)}, bf16[1,64,768]{2,1,0:T(8,128)(2,1)S(1)}, u32[]{:S(2)}, u32[]{:S(2)}) collective-permute-start(bf16[1,64,768]{2,1,0:T(8,128)(2,1)S(1)} %collective-permute-done.24.refs_3_), channel_id=1, source_target_pairs={{0,224},{32,0},{64,32},{96,64},{128,96},{160,128},{192,160},{224,1... | collective-permute-start | bytes 294920 | tf_op jit(solution)/shard_map/ppermute | solution.py:144
  90.8 2.2 %collective-permute-done.25.refs_5_ = bf16[1,64,768]{2,1,0:T(8,128)(2,1)S(1)} collective-permute-done((bf16[1,64,768]{2,1,0:T(8,128)(2,1)S(1)}, bf16[1,64,768]{2,1,0:T(8,128)(2,1)S(1)}, u32[]{:S(2)}, u32[]{:S(2)}) %collective-permute-start.25) | collective-permute-done | bytes 98336 | tf_op jit(solution)/shard_map/ppermute | solution.py:144
  93.0 3.6 %collective-permute-done.23.refs_4_ = bf16[1,64,768]{2,1,0:T(8,128)(2,1)S(1)} collective-permute-done((bf16[1,64,768]{2,1,0:T(8,128)(2,1)S(1)}, bf16[1,64,768]{2,1,0:T(8,128)(2,1)S(1)}, u32[]{:S(2)}, u32[]{:S(2)}) %collective-permute-start.23) | collective-permute-done | bytes 98336 | tf_op jit(solution)/shard_map/ppermute | solution.py:144
  96.7 2.0 %collective-permute-start.28 = (bf16[3,64,768]{2,1,0:T(8,128)(2,1)S(1)}, bf16[3,64,768]{2,1,0:T(8,128)(2,1)S(1)}, u32[]{:S(2)}, u32[]{:S(2)}) collective-permute-start(bf16[3,64,768]{2,1,0:T(8,128)(2,1)S(1)} %constant_dynamic-update-slice_fusion.refs_1_), channel_id=1, source_target_pairs={{0,32},{32,64},{64,96},{96,128},{128,160},{160,192},{192,224},{224... | collective-permute-start | bytes 884744 | tf_op jit(solution)/shard_map/ppermute | solution.py:144
  98.8 3.2 %collective-permute-start.27 = (bf16[1,64,768]{2,1,0:T(8,128)(2,1)S(1)}, bf16[1,64,768]{2,1,0:T(8,128)(2,1)S(1)}, u32[]{:S(2)}, u32[]{:S(2)}) collective-permute-start(bf16[1,64,768]{2,1,0:T(8,128)(2,1)S(1)} %collective-permute-done.25.refs_5_), channel_id=1, source_target_pairs={{0,224},{32,0},{64,32},{96,64},{128,96},{160,128},{192,160},{224,1... | collective-permute-start | bytes 294920 | tf_op jit(solution)/shard_map/ppermute | solution.py:144
  102.0 4.4 %collective-permute-done.26.refs_6_ = bf16[1,64,768]{2,1,0:T(8,128)(2,1)S(1)} collective-permute-done((bf16[1,64,768]{2,1,0:T(8,128)(2,1)S(1)}, bf16[1,64,768]{2,1,0:T(8,128)(2,1)S(1)}, u32[]{:S(2)}, u32[]{:S(2)}) %collective-permute-start.26) | collective-permute-done | bytes 98336 | tf_op jit(solution)/shard_map/ppermute | solution.py:144
  106.4 1.6 %collective-permute-start.32 = (bf16[3,64,768]{2,1,0:T(8,128)(2,1)S(1)}, bf16[3,64,768]{2,1,0:T(8,128)(2,1)S(1)}, u32[]{:S(2)}, u32[]{:S(2)}) collective-permute-start(bf16[3,64,768]{2,1,0:T(8,128)(2,1)S(1)} %collective-permute-done.28.refs_8_), channel_id=1, source_target_pairs={{0,32},{32,64},{64,96},{96,128},{128,160},{160,192},{192,224},{224... | collective-permute-start | bytes 884744 | tf_op jit(solution)/shard_map/ppermute | solution.py:144
  107.9 1.8 %collective-permute-start.33 = (bf16[3,64,768]{2,1,0:T(8,128)(2,1)S(1)}, bf16[3,64,768]{2,1,0:T(8,128)(2,1)S(1)}, u32[]{:S(2)}, u32[]{:S(2)}) collective-permute-start(bf16[3,64,768]{2,1,0:T(8,128)(2,1)S(1)} %collective-permute-done.29.refs_9_), channel_id=1, source_target_pairs={{0,224},{32,0},{64,32},{96,64},{128,96},{160,128},{192,160},{224,1... | collective-permute-start | bytes 884744 | tf_op jit(solution)/shard_map/ppermute | solution.py:144
  109.9 1.9 %collective-permute-start.30 = (bf16[1,32,768]{2,1,0:T(8,128)(2,1)S(1)}, bf16[1,32,768]{2,1,0:T(8,128)(2,1)S(1)}, u32[]{:S(2)}, u32[]{:S(2)}) collective-permute-start(bf16[1,32,768]{2,1,0:T(8,128)(2,1)S(1)} %slice.28), channel_id=1, source_target_pairs={{0,32},{32,64},{64,96},{96,128},{128,160},{160,192},{192,224},{224... | collective-permute-start | bytes 147464 | tf_op jit(solution)/shard_map/ppermute | solution.py:144
  111.8 5.6 %collective-permute-done.31.refs_1_ = bf16[1,32,768]{2,1,0:T(8,128)(2,1)S(1)} collective-permute-done((bf16[1,32,768]{2,1,0:T(8,128)(2,1)S(1)}, bf16[1,32,768]{2,1,0:T(8,128)(2,1)S(1)}, u32[]{:S(2)}, u32[]{:S(2)}) %collective-permute-start.31) | collective-permute-done | bytes 49184 | tf_op jit(solution)/shard_map/ppermute | solution.py:144
  117.5 3.2 %collective-permute-start.36 = (bf16[3,64,768]{2,1,0:T(8,128)(2,1)S(1)}, bf16[3,64,768]{2,1,0:T(8,128)(2,1)S(1)}, u32[]{:S(2)}, u32[]{:S(2)}) collective-permute-start(bf16[3,64,768]{2,1,0:T(8,128)(2,1)S(1)} %collective-permute-done.33.refs_3_), channel_id=1, source_target_pairs={{0,224},{32,0},{64,32},{96,64},{128,96},{160,128},{192,160},{224,1... | collective-permute-start | bytes 884744 | tf_op jit(solution)/shard_map/ppermute | solution.py:144
  120.7 5.8 %collective-permute-done.34.refs_4_ = bf16[3,64,768]{2,1,0:T(8,128)(2,1)S(1)} collective-permute-done((bf16[3,64,768]{2,1,0:T(8,128)(2,1)S(1)}, bf16[3,64,768]{2,1,0:T(8,128)(2,1)S(1)}, u32[]{:S(2)}, u32[]{:S(2)}) %collective-permute-start.34) | collective-permute-done | bytes 294944 | tf_op jit(solution)/shard_map/ppermute | solution.py:144
  126.7 3.3 %collective-permute-start.37 = (bf16[3,32,768]{2,1,0:T(8,128)(2,1)S(1)}, bf16[3,32,768]{2,1,0:T(8,128)(2,1)S(1)}, u32[]{:S(2)}, u32[]{:S(2)}) collective-permute-start(bf16[3,32,768]{2,1,0:T(8,128)(2,1)S(1)} %slice.37), channel_id=1, source_target_pairs={{0,224},{32,0},{64,32},{96,64},{128,96},{160,128},{192,160},{224,1... | collective-permute-start | bytes 442376 | tf_op jit(solution)/shard_map/ppermute | solution.py:144
  129.9 1.3 shard_map.37.refs_6_
  131.2 1.2 shard_map.38.refs_2_
  132.4 0.6 collective-permute-done.35.refs_0_
  133.0 0.8 shard_map.39
  (57 shorter events, 3.2 us)
Async XLA Ops:
  0.0 0.7 copy-start
  3.1 19.1 %all-to-all-start.1 = ((bf16[8,16,768]{2,1,0:T(8,128)(2,1)}), bf16[8,16,768]{2,1,0:T(8,128)(2,1)S(1)}, u32[]{:S(2)}, u32[]{:S(2)}) async-start(bf16[8,16,768]{2,1,0:T(8,128)(2,1)} %get-tuple-element.31), calls=%async_computation.1 | async-start | bytes 393216 | tf_op jit(solution)/shard_map/all_to_all | solution.py:166
  11.6 5.0 %collective-permute-start = (bf16[8,64,128]{2,1,0:T(8,128)(2,1)S(1)}, bf16[8,64,128]{2,1,0:T(8,128)(2,1)S(1)}, u32[]{:S(2)}, u32[]{:S(2)}) collective-permute-start(bf16[8,64,128]{2,1,0:T(8,128)(2,1)S(1)} %get-tuple-element.28), channel_id=1, source_target_pairs={{0,8},{8,16},{16,24},{24,0},{1,9},{9,17},{17,25},{25,1},{2,10},{10... | collective-permute-start | bytes 393224 | tf_op jit(solution)/shard_map/ppermute | solution.py:144
  13.2 6.2 %collective-permute-start.1 = (bf16[8,64,128]{2,1,0:T(8,128)(2,1)S(1)}, bf16[8,64,128]{2,1,0:T(8,128)(2,1)S(1)}, u32[]{:S(2)}, u32[]{:S(2)}) collective-permute-start(bf16[8,64,128]{2,1,0:T(8,128)(2,1)S(1)} %get-tuple-element.29), channel_id=1, source_target_pairs={{0,24},{8,0},{16,8},{24,16},{1,25},{9,1},{17,9},{25,17},{2,26},{10... | collective-permute-start | bytes 393224 | tf_op jit(solution)/shard_map/ppermute | solution.py:144
  13.6 7.8 %collective-permute-start.2 = (bf16[8,64,128]{2,1,0:T(8,128)(2,1)S(1)}, bf16[8,64,128]{2,1,0:T(8,128)(2,1)S(1)}, u32[]{:S(2)}, u32[]{:S(2)}) collective-permute-start(bf16[8,64,128]{2,1,0:T(8,128)(2,1)S(1)} %get-tuple-element.30), channel_id=1, source_target_pairs={{0,16},{8,24},{16,0},{24,8},{1,17},{9,25},{17,1},{25,9},{2,18},{10... | collective-permute-start | bytes 393224 | tf_op jit(solution)/shard_map/ppermute | solution.py:144
  22.3 23.9 %all-to-all-start = ((bf16[8,4,64,128]{3,2,1,0:T(8,128)(2,1)}), bf16[8,4,64,128]{3,2,1,0:T(8,128)(2,1)S(1)}, u32[]{:S(2)}, u32[]{:S(2)}) async-start(bf16[8,4,64,128]{3,2,1,0:T(8,128)(2,1)} %pad_maximum_fusion), calls=%async_computation | async-start | bytes 1048576 | tf_op jit(solution)/shard_map/all_to_all | solution.py:167
  29.2 6.0 %collective-permute-start.4 = (bf16[8,16,768]{2,1,0:T(8,128)(2,1)S(1)}, bf16[8,16,768]{2,1,0:T(8,128)(2,1)S(1)}, u32[]{:S(2)}, u32[]{:S(2)}) collective-permute-start(bf16[8,16,768]{2,1,0:T(8,128)(2,1)S(1)} %all-to-all-done.1.refs_0_), channel_id=1, source_target_pairs={{0,6},{2,0},{4,2},{6,4},{1,7},{3,1},{5,3},{7,5},{8,14},{10,8},{12,... | collective-permute-start | bytes 589832 | tf_op jit(solution)/shard_map/ppermute | solution.py:144
  32.0 7.0 %collective-permute-start.3 = (bf16[8,16,768]{2,1,0:T(8,128)(2,1)S(1)}, bf16[8,16,768]{2,1,0:T(8,128)(2,1)S(1)}, u32[]{:S(2)}, u32[]{:S(2)}) collective-permute-start(bf16[8,16,768]{2,1,0:T(8,128)(2,1)S(1)} %all-to-all-done.1.refs_0_), channel_id=1, source_target_pairs={{0,2},{2,4},{4,6},{6,0},{1,3},{3,5},{5,7},{7,1},{8,10},{10,12},{12... | collective-permute-start | bytes 589832 | tf_op jit(solution)/shard_map/ppermute | solution.py:144
  32.0 12.9 %collective-permute-start.7 = (bf16[8,16,768]{2,1,0:T(8,128)(2,1)S(1)}, bf16[8,16,768]{2,1,0:T(8,128)(2,1)S(1)}, u32[]{:S(2)}, u32[]{:S(2)}) collective-permute-start(bf16[8,16,768]{2,1,0:T(8,128)(2,1)S(1)} %all-to-all-done.1.refs_0_), channel_id=1, source_target_pairs={{0,1},{1,0},{2,3},{3,2},{4,5},{5,4},{6,7},{7,6},{8,9},{9,8},{10,11... | collective-permute-start | bytes 589832 | tf_op jit(solution)/shard_map/ppermute | solution.py:144
  35.2 6.0 %collective-permute-start.6 = (bf16[4,16,768]{2,1,0:T(8,128)(2,1)S(1)}, bf16[4,16,768]{2,1,0:T(8,128)(2,1)S(1)}, u32[]{:S(2)}, u32[]{:S(2)}) collective-permute-start(bf16[4,16,768]{2,1,0:T(8,128)(2,1)S(1)} %slice.33), channel_id=1, source_target_pairs={{0,6},{2,0},{4,2},{6,4},{1,7},{3,1},{5,3},{7,5},{8,14},{10,8},{12,... | collective-permute-start | bytes 294920 | tf_op jit(solution)/shard_map/ppermute | solution.py:144
  39.0 5.9 %collective-permute-start.5 = (bf16[4,16,768]{2,1,0:T(8,128)(2,1)S(1)}, bf16[4,16,768]{2,1,0:T(8,128)(2,1)S(1)}, u32[]{:S(2)}, u32[]{:S(2)}) collective-permute-start(bf16[4,16,768]{2,1,0:T(8,128)(2,1)S(1)} %slice.32), channel_id=1, source_target_pairs={{0,2},{2,4},{4,6},{6,0},{1,3},{3,5},{5,7},{7,1},{8,10},{10,12},{12... | collective-permute-start | bytes 294920 | tf_op jit(solution)/shard_map/ppermute | solution.py:144
  39.1 5.8 %collective-permute-start.9 = (bf16[8,16,768]{2,1,0:T(8,128)(2,1)S(1)}, bf16[8,16,768]{2,1,0:T(8,128)(2,1)S(1)}, u32[]{:S(2)}, u32[]{:S(2)}) collective-permute-start(bf16[8,16,768]{2,1,0:T(8,128)(2,1)S(1)} %collective-permute-done.4.refs_2_), channel_id=1, source_target_pairs={{0,1},{1,0},{2,3},{3,2},{4,5},{5,4},{6,7},{7,6},{8,9},{9,8},{10,11... | collective-permute-start | bytes 589832 | tf_op jit(solution)/shard_map/ppermute | solution.py:144
  39.2 7.0 %collective-permute-start.8 = (bf16[8,16,768]{2,1,0:T(8,128)(2,1)S(1)}, bf16[8,16,768]{2,1,0:T(8,128)(2,1)S(1)}, u32[]{:S(2)}, u32[]{:S(2)}) collective-permute-start(bf16[8,16,768]{2,1,0:T(8,128)(2,1)S(1)} %collective-permute-done.3.refs_1_), channel_id=1, source_target_pairs={{0,1},{1,0},{2,3},{3,2},{4,5},{5,4},{6,7},{7,6},{8,9},{9,8},{10,11... | collective-permute-start | bytes 589832 | tf_op jit(solution)/shard_map/ppermute | solution.py:144
  41.2 3.7 %collective-permute-start.11 = (bf16[4,16,768]{2,1,0:T(8,128)(2,1)S(1)}, bf16[4,16,768]{2,1,0:T(8,128)(2,1)S(1)}, u32[]{:S(2)}, u32[]{:S(2)}) collective-permute-start(bf16[4,16,768]{2,1,0:T(8,128)(2,1)S(1)} %collective-permute-done.6.refs_4_), channel_id=1, source_target_pairs={{0,1},{1,0},{2,3},{3,2},{4,5},{5,4},{6,7},{7,6},{8,9},{9,8},{10,11... | collective-permute-start | bytes 294920 | tf_op jit(solution)/shard_map/ppermute | solution.py:144
  44.9 1.3 collective-permute-start.10
  46.9 12.5 %collective-permute-start.12 = (bf16[256,768]{1,0:T(8,128)(2,1)S(1)}, bf16[256,768]{1,0:T(8,128)(2,1)S(1)}, u32[]{:S(2)}, u32[]{:S(2)}) collective-permute-start(bf16[256,768]{1,0:T(8,128)(2,1)S(1)} %grad.1.grad_ref), channel_id=1, source_target_pairs={{0,2},{2,4},{4,6},{6,0},{1,3},{3,5},{5,7},{7,1},{8,10},{10,12},{12... | collective-permute-start | bytes 1179656 | tf_op jit(solution)/shard_map/ppermute | solution.py:144
  47.0 12.9 %collective-permute-start.13 = (bf16[256,768]{1,0:T(8,128)(2,1)S(1)}, bf16[256,768]{1,0:T(8,128)(2,1)S(1)}, u32[]{:S(2)}, u32[]{:S(2)}) collective-permute-start(bf16[256,768]{1,0:T(8,128)(2,1)S(1)} %grad.1.grad_ref), channel_id=1, source_target_pairs={{0,6},{2,0},{4,2},{6,4},{1,7},{3,1},{5,3},{7,5},{8,14},{10,8},{12,... | collective-permute-start | bytes 1179656 | tf_op jit(solution)/shard_map/ppermute | solution.py:144
  60.9 12.6 %collective-permute-start.16 = (f32[768,768]{1,0:T(8,128)S(1)}, f32[768,768]{1,0:T(8,128)S(1)}, u32[]{:S(2)}, u32[]{:S(2)}) collective-permute-start(f32[768,768]{1,0:T(8,128)S(1)} %add_add_fusion.1), channel_id=1, source_target_pairs={{0,1},{1,0},{2,3},{3,2},{4,5},{5,4},{6,7},{7,6},{8,9},{9,8},{10,11... | collective-permute-start | bytes 7077896 | tf_op jit(solution)/shard_map/ppermute | solution.py:144
  61.2 7.4 %collective-permute-start.15 = (bf16[128,768]{1,0:T(8,128)(2,1)S(1)}, bf16[128,768]{1,0:T(8,128)(2,1)S(1)}, u32[]{:S(2)}, u32[]{:S(2)}) collective-permute-start(bf16[128,768]{1,0:T(8,128)(2,1)S(1)} %slice.35), channel_id=1, source_target_pairs={{0,6},{2,0},{4,2},{6,4},{1,7},{3,1},{5,3},{7,5},{8,14},{10,8},{12,... | collective-permute-start | bytes 589832 | tf_op jit(solution)/shard_map/ppermute | solution.py:144
  63.7 8.3 %collective-permute-start.14 = (bf16[128,768]{1,0:T(8,128)(2,1)S(1)}, bf16[128,768]{1,0:T(8,128)(2,1)S(1)}, u32[]{:S(2)}, u32[]{:S(2)}) collective-permute-start(bf16[128,768]{1,0:T(8,128)(2,1)S(1)} %slice.34), channel_id=1, source_target_pairs={{0,2},{2,4},{4,6},{6,0},{1,3},{3,5},{5,7},{7,1},{8,10},{10,12},{12... | collective-permute-start | bytes 589832 | tf_op jit(solution)/shard_map/ppermute | solution.py:144
  68.6 4.5 %collective-permute-start.18 = (bf16[128,768]{1,0:T(8,128)(2,1)S(1)}, bf16[128,768]{1,0:T(8,128)(2,1)S(1)}, u32[]{:S(2)}, u32[]{:S(2)}) collective-permute-start(bf16[128,768]{1,0:T(8,128)(2,1)S(1)} %collective-permute-done.15), channel_id=1, source_target_pairs={{0,1},{1,0},{2,3},{3,2},{4,5},{5,4},{6,7},{7,6},{8,9},{9,8},{10,11... | collective-permute-start | bytes 589832 | tf_op jit(solution)/shard_map/ppermute | solution.py:144
  72.0 1.4 %collective-permute-start.17 = (bf16[128,768]{1,0:T(8,128)(2,1)S(1)}, bf16[128,768]{1,0:T(8,128)(2,1)S(1)}, u32[]{:S(2)}, u32[]{:S(2)}) collective-permute-start(bf16[128,768]{1,0:T(8,128)(2,1)S(1)} %collective-permute-done.14), channel_id=1, source_target_pairs={{0,1},{1,0},{2,3},{3,2},{4,5},{5,4},{6,7},{7,6},{8,9},{9,8},{10,11... | collective-permute-start | bytes 589832 | tf_op jit(solution)/shard_map/ppermute | solution.py:144
  79.1 8.5 %collective-permute-start.24 = (bf16[1,64,768]{2,1,0:T(8,128)(2,1)S(1)}, bf16[1,64,768]{2,1,0:T(8,128)(2,1)S(1)}, u32[]{:S(2)}, u32[]{:S(2)}) collective-permute-start(bf16[1,64,768]{2,1,0:T(8,128)(2,1)S(1)} %get-tuple-element.35.refs_0_), channel_id=1, source_target_pairs={{0,224},{32,0},{64,32},{96,64},{128,96},{160,128},{192,160},{224,1... | collective-permute-start | bytes 294920 | tf_op jit(solution)/shard_map/ppermute | solution.py:144
  82.4 8.4 %collective-permute-start.22 = (bf16[1,64,768]{2,1,0:T(8,128)(2,1)S(1)}, bf16[1,64,768]{2,1,0:T(8,128)(2,1)S(1)}, u32[]{:S(2)}, u32[]{:S(2)}) collective-permute-start(bf16[1,64,768]{2,1,0:T(8,128)(2,1)S(1)} %get-tuple-element.35.refs_0_), channel_id=1, source_target_pairs={{0,32},{32,64},{64,96},{96,128},{128,160},{160,192},{192,224},{224... | collective-permute-start | bytes 294920 | tf_op jit(solution)/shard_map/ppermute | solution.py:144
  82.4 8.4 %collective-permute-start.19 = (bf16[1,64,768]{2,1,0:T(8,128)(2,1)S(1)}, bf16[1,64,768]{2,1,0:T(8,128)(2,1)S(1)}, u32[]{:S(2)}, u32[]{:S(2)}) collective-permute-start(bf16[1,64,768]{2,1,0:T(8,128)(2,1)S(1)} %get-tuple-element.32), channel_id=1, source_target_pairs={{0,24},{8,0},{16,8},{24,16},{1,25},{9,1},{17,9},{25,17},{2,26},{10... | collective-permute-start | bytes 294920 | tf_op jit(solution)/shard_map/ppermute | solution.py:144
  83.5 7.2 %collective-permute-start.20 = (bf16[1,64,768]{2,1,0:T(8,128)(2,1)S(1)}, bf16[1,64,768]{2,1,0:T(8,128)(2,1)S(1)}, u32[]{:S(2)}, u32[]{:S(2)}) collective-permute-start(bf16[1,64,768]{2,1,0:T(8,128)(2,1)S(1)} %get-tuple-element.33), channel_id=1, source_target_pairs={{0,8},{8,16},{16,24},{24,0},{1,9},{9,17},{17,25},{25,1},{2,10},{10... | collective-permute-start | bytes 294920 | tf_op jit(solution)/shard_map/ppermute | solution.py:144
  84.4 6.4 %collective-permute-start.21 = (bf16[1,64,768]{2,1,0:T(8,128)(2,1)S(1)}, bf16[1,64,768]{2,1,0:T(8,128)(2,1)S(1)}, u32[]{:S(2)}, u32[]{:S(2)}) collective-permute-start(bf16[1,64,768]{2,1,0:T(8,128)(2,1)S(1)} %get-tuple-element.34), channel_id=1, source_target_pairs={{0,16},{8,24},{16,0},{24,8},{1,17},{9,25},{17,1},{25,9},{2,18},{10... | collective-permute-start | bytes 294920 | tf_op jit(solution)/shard_map/ppermute | solution.py:144
  87.5 5.4 %collective-permute-start.25 = (bf16[1,64,768]{2,1,0:T(8,128)(2,1)S(1)}, bf16[1,64,768]{2,1,0:T(8,128)(2,1)S(1)}, u32[]{:S(2)}, u32[]{:S(2)}) collective-permute-start(bf16[1,64,768]{2,1,0:T(8,128)(2,1)S(1)} %collective-permute-done.24.refs_3_), channel_id=1, source_target_pairs={{0,224},{32,0},{64,32},{96,64},{128,96},{160,128},{192,160},{224,1... | collective-permute-start | bytes 294920 | tf_op jit(solution)/shard_map/ppermute | solution.py:144
  90.8 5.8 %collective-permute-start.23 = (bf16[1,64,768]{2,1,0:T(8,128)(2,1)S(1)}, bf16[1,64,768]{2,1,0:T(8,128)(2,1)S(1)}, u32[]{:S(2)}, u32[]{:S(2)}) collective-permute-start(bf16[1,64,768]{2,1,0:T(8,128)(2,1)S(1)} %collective-permute-done.22.refs_2_), channel_id=1, source_target_pairs={{0,32},{32,64},{64,96},{96,128},{128,160},{160,192},{192,224},{224... | collective-permute-start | bytes 294920 | tf_op jit(solution)/shard_map/ppermute | solution.py:144
  96.7 9.7 %collective-permute-start.29 = (bf16[3,64,768]{2,1,0:T(8,128)(2,1)S(1)}, bf16[3,64,768]{2,1,0:T(8,128)(2,1)S(1)}, u32[]{:S(2)}, u32[]{:S(2)}) collective-permute-start(bf16[3,64,768]{2,1,0:T(8,128)(2,1)S(1)} %constant_dynamic-update-slice_fusion.refs_1_), channel_id=1, source_target_pairs={{0,224},{32,0},{64,32},{96,64},{128,96},{160,128},{192,160},{224,1... | collective-permute-start | bytes 884744 | tf_op jit(solution)/shard_map/ppermute | solution.py:144
  96.7 9.6 %collective-permute-start.28 = (bf16[3,64,768]{2,1,0:T(8,128)(2,1)S(1)}, bf16[3,64,768]{2,1,0:T(8,128)(2,1)S(1)}, u32[]{:S(2)}, u32[]{:S(2)}) collective-permute-start(bf16[3,64,768]{2,1,0:T(8,128)(2,1)S(1)} %constant_dynamic-update-slice_fusion.refs_1_), channel_id=1, source_target_pairs={{0,32},{32,64},{64,96},{96,128},{128,160},{160,192},{192,224},{224... | collective-permute-start | bytes 884744 | tf_op jit(solution)/shard_map/ppermute | solution.py:144
  98.8 7.6 %collective-permute-start.26 = (bf16[1,64,768]{2,1,0:T(8,128)(2,1)S(1)}, bf16[1,64,768]{2,1,0:T(8,128)(2,1)S(1)}, u32[]{:S(2)}, u32[]{:S(2)}) collective-permute-start(bf16[1,64,768]{2,1,0:T(8,128)(2,1)S(1)} %collective-permute-done.23.refs_4_), channel_id=1, source_target_pairs={{0,32},{32,64},{64,96},{96,128},{128,160},{160,192},{192,224},{224... | collective-permute-start | bytes 294920 | tf_op jit(solution)/shard_map/ppermute | solution.py:144
  98.8 7.6 %collective-permute-start.27 = (bf16[1,64,768]{2,1,0:T(8,128)(2,1)S(1)}, bf16[1,64,768]{2,1,0:T(8,128)(2,1)S(1)}, u32[]{:S(2)}, u32[]{:S(2)}) collective-permute-start(bf16[1,64,768]{2,1,0:T(8,128)(2,1)S(1)} %collective-permute-done.25.refs_5_), channel_id=1, source_target_pairs={{0,224},{32,0},{64,32},{96,64},{128,96},{160,128},{192,160},{224,1... | collective-permute-start | bytes 294920 | tf_op jit(solution)/shard_map/ppermute | solution.py:144
  106.4 11.0 %collective-permute-start.32 = (bf16[3,64,768]{2,1,0:T(8,128)(2,1)S(1)}, bf16[3,64,768]{2,1,0:T(8,128)(2,1)S(1)}, u32[]{:S(2)}, u32[]{:S(2)}) collective-permute-start(bf16[3,64,768]{2,1,0:T(8,128)(2,1)S(1)} %collective-permute-done.28.refs_8_), channel_id=1, source_target_pairs={{0,32},{32,64},{64,96},{96,128},{128,160},{160,192},{192,224},{224... | collective-permute-start | bytes 884744 | tf_op jit(solution)/shard_map/ppermute | solution.py:144
  107.9 9.5 %collective-permute-start.33 = (bf16[3,64,768]{2,1,0:T(8,128)(2,1)S(1)}, bf16[3,64,768]{2,1,0:T(8,128)(2,1)S(1)}, u32[]{:S(2)}, u32[]{:S(2)}) collective-permute-start(bf16[3,64,768]{2,1,0:T(8,128)(2,1)S(1)} %collective-permute-done.29.refs_9_), channel_id=1, source_target_pairs={{0,224},{32,0},{64,32},{96,64},{128,96},{160,128},{192,160},{224,1... | collective-permute-start | bytes 884744 | tf_op jit(solution)/shard_map/ppermute | solution.py:144
  109.7 7.7 %collective-permute-start.31 = (bf16[1,32,768]{2,1,0:T(8,128)(2,1)S(1)}, bf16[1,32,768]{2,1,0:T(8,128)(2,1)S(1)}, u32[]{:S(2)}, u32[]{:S(2)}) collective-permute-start(bf16[1,32,768]{2,1,0:T(8,128)(2,1)S(1)} %slice.29), channel_id=1, source_target_pairs={{0,224},{32,0},{64,32},{96,64},{128,96},{160,128},{192,160},{224,1... | collective-permute-start | bytes 147464 | tf_op jit(solution)/shard_map/ppermute | solution.py:144
  109.9 7.4 %collective-permute-start.30 = (bf16[1,32,768]{2,1,0:T(8,128)(2,1)S(1)}, bf16[1,32,768]{2,1,0:T(8,128)(2,1)S(1)}, u32[]{:S(2)}, u32[]{:S(2)}) collective-permute-start(bf16[1,32,768]{2,1,0:T(8,128)(2,1)S(1)} %slice.28), channel_id=1, source_target_pairs={{0,32},{32,64},{64,96},{96,128},{128,160},{160,192},{192,224},{224... | collective-permute-start | bytes 147464 | tf_op jit(solution)/shard_map/ppermute | solution.py:144
  117.4 9.1 %collective-permute-start.34 = (bf16[3,64,768]{2,1,0:T(8,128)(2,1)S(1)}, bf16[3,64,768]{2,1,0:T(8,128)(2,1)S(1)}, u32[]{:S(2)}, u32[]{:S(2)}) collective-permute-start(bf16[3,64,768]{2,1,0:T(8,128)(2,1)S(1)} %collective-permute-done.32.refs_2_), channel_id=1, source_target_pairs={{0,32},{32,64},{64,96},{96,128},{128,160},{160,192},{192,224},{224... | collective-permute-start | bytes 884744 | tf_op jit(solution)/shard_map/ppermute | solution.py:144
  117.5 9.2 %collective-permute-start.36 = (bf16[3,64,768]{2,1,0:T(8,128)(2,1)S(1)}, bf16[3,64,768]{2,1,0:T(8,128)(2,1)S(1)}, u32[]{:S(2)}, u32[]{:S(2)}) collective-permute-start(bf16[3,64,768]{2,1,0:T(8,128)(2,1)S(1)} %collective-permute-done.33.refs_3_), channel_id=1, source_target_pairs={{0,224},{32,0},{64,32},{96,64},{128,96},{160,128},{192,160},{224,1... | collective-permute-start | bytes 884744 | tf_op jit(solution)/shard_map/ppermute | solution.py:144
  126.5 6.4 %collective-permute-start.35 = (bf16[3,32,768]{2,1,0:T(8,128)(2,1)S(1)}, bf16[3,32,768]{2,1,0:T(8,128)(2,1)S(1)}, u32[]{:S(2)}, u32[]{:S(2)}) collective-permute-start(bf16[3,32,768]{2,1,0:T(8,128)(2,1)S(1)} %slice.36), channel_id=1, source_target_pairs={{0,32},{32,64},{64,96},{96,128},{128,160},{160,192},{192,224},{224... | collective-permute-start | bytes 442376 | tf_op jit(solution)/shard_map/ppermute | solution.py:144
  126.7 6.3 %collective-permute-start.37 = (bf16[3,32,768]{2,1,0:T(8,128)(2,1)S(1)}, bf16[3,32,768]{2,1,0:T(8,128)(2,1)S(1)}, u32[]{:S(2)}, u32[]{:S(2)}) collective-permute-start(bf16[3,32,768]{2,1,0:T(8,128)(2,1)S(1)} %slice.37), channel_id=1, source_target_pairs={{0,224},{32,0},{64,32},{96,64},{128,96},{160,128},{192,160},{224,1... | collective-permute-start | bytes 442376 | tf_op jit(solution)/shard_map/ppermute | solution.py:144
where the time goes:
time: 134 us
  starting transfers between devices  62.3 us (46%)
  waiting for transfers between devices  55.1 us (41%)
  Pallas kernels  11.9 us (9%)
  matrix products  2.55 us (2%)
    ppermute x38, waiting for transfers between devices, move(): return lax.ppermute(value, axis, shift(size, by))  55.1 us
    ppermute x38, starting transfers between devices, move(): return lax.ppermute(value, axis, shift(size, by))  46.9 us
    all_to_all x1, starting transfers between devices, body(): own = lax.all_to_all(mine, 'z', 0, 0, tiled=True)  8.48 us
    all_to_all x1, starting transfers between devices, body(): xz = lax.all_to_all(jnp.stack(sides, axis=1), 'z', 0, 0, tiled=True)  6.93 us
    pallas_call x1, Pallas kernels, body(): pl.pallas_call(functools.partial(newton_kernel, math.sqrt(2048)), out_sha...  5.57 us
    pallas_call x3, Pallas kernels, place(): pl.pallas_call(functools.partial(place_kernel, places, n, int(aliased)),...  3.19 us
  transfers between devices with their start and end apart: 40, of which 17 were waited for; matrix products, arithmetic and copies ran while one was open for 2% of the time, Pallas kernels for 2%

commit v1 on v0

--- a/solution.py
+++ b/solution.py
@@ -20,7 +20,6 @@
 SIDES = (0, 1, 3, 2)
 
 VMEM = pl.BlockSpec(memory_space=pltpu.VMEM)
-SMEM = pl.BlockSpec(memory_space=pltpu.SMEM)
 ANY = pl.BlockSpec(memory_space=pl.ANY)
 
 
@@ -40,11 +39,14 @@
     return lax.dot_general(rows, rows, (((0,), (0,)), ((), ())), preferred_element_type=jnp.float32)
 
 
-def pack_kernel(count_ref, x_ref, g_ref, *refs):
-    x_outs, g_out, sems = refs[:NY], refs[NY], refs[NY + 1]
+def pack_kernel(count_hbm, x_ref, g_ref, *refs):
+    x_outs, g_out, count_ref, sems = refs[:NY], *refs[NY:]
     y = lax.axis_index("y")
     block = NC * lax.axis_index("x") + lax.axis_index("c")
-    copies = [pltpu.make_async_copy(g_ref.at[y, :, block], g_out, sems.at[NY])]
+    copies = [
+        pltpu.make_async_copy(g_ref.at[y, :, block], g_out, sems.at[NY]),
+        pltpu.make_async_copy(count_hbm, count_ref, sems.at[NY + 1]),
+    ]
     for k, dy in enumerate(SIDES):
         source = x_ref.at[lax.rem(y + dy, NY)]
         copies.append(pltpu.make_async_copy(source, x_outs[k], sems.at[k]))
@@ -152,19 +154,23 @@
         pack_kernel,
         out_shape=[pltpu.VMEM((NZ, COLS, CAP), jnp.bfloat16)] * NY
         + [pltpu.VMEM((NZ, BLK, width), jnp.bfloat16)],
-        in_specs=[SMEM, ANY, ANY],
+        in_specs=[ANY] * 3,
         out_specs=[VMEM] * (NY + 1),
-        scratch_shapes=[pltpu.SemaphoreType.DMA((NY + 1,))],
+        scratch_shapes=[
+            pltpu.SMEM((1, NY * NZ), jnp.int32),
+            pltpu.SemaphoreType.DMA((NY + 2,)),
+        ],
         compiler_params=pltpu.CompilerParams(vmem_limit_bytes=2 << 20),
         name="pack",
     )(
-        counts,
+        far_hbm(counts),
         far_hbm(x.transpose(0, 2, 1).reshape(NY, NZ, COLS, CAP)),
         far_hbm(g.reshape(NY, NZ, CAP // BLK, BLK, width)),
     )
     sides = [sides[0]] + [move(sides[k], "y", NY, SIDES[k]) for k in range(1, NY)]
+    sides = jnp.stack(sides, axis=1)
     own = lax.all_to_all(mine, "z", 0, 0, tiled=True)
-    xz = lax.all_to_all(jnp.stack(sides, axis=1), "z", 0, 0, tiled=True)
+    xz = lax.all_to_all(sides, "z", 0, 0, tiled=True)
 
     right = move(own, "x", NX, 1)
     left = move(own, "x", NX, -1)
@@ -204,45 +210,20 @@
         name="newton",
     )(*near(total, other, other_far_a, other_far_b, grad))
 
-    moved = [move(pieces[k], "y", NY, -SIDES[k]) for k in range(1, NY)]
+    rows = [pieces[0]] + [move(pieces[k], "y", NY, -SIDES[k]) for k in range(1, NY)]
+    rows = jnp.stack([r[0] for r in rows])
+    right, left = rows, rows
+    items = [[(rows, (SIDES, 0, 0))]]
+    for n in range(1, 4):
+        right = move(right, "z", NZ, 1)
+        left = move(left, "z", NZ, -1)
+        items.append([(right, (SIDES, -n, 0)), (left, (SIDES, n, 0))])
     half = COLS // 2
-    a_dys, b_dys = (0,), SIDES[1:]
-
-    def step(right, left):
-        return [move(right, "z", NZ, 1), move(left, "z", NZ, -1)]
-
-    def halves(right, left):
-        return step(right[:, :half], left[:, half:])
-
-    a1 = step(pieces[0], pieces[0])
-    a2 = step(*a1)
-    *moved, a2[0], a2[1] = lax.optimization_barrier((*moved, *a2))
-    moved = jnp.stack([m[0] for m in moved])
-    a3 = step(*a2)
-    b1 = step(moved, moved)
-    *a3, b1[0], b1[1] = lax.optimization_barrier((*a3, *b1))
-    a4 = halves(*a3)
-    b2 = step(*b1)
-    *a4, b2[0], b2[1] = lax.optimization_barrier((*a4, *b2))
-    b3 = step(*b2)
-    b4 = halves(*b3)
-
-    def items(pair, dys, n):
-        if n == 4:
-            return [(pair[0], (dys, 4, 0)), (pair[1], (dys, 4, half))]
-        return [(pair[0], (dys, -n, 0)), (pair[1], (dys, n, 0))]
-
-    out = place(
-        None,
-        width,
-        [(pieces[0], (a_dys, 0, 0)), (moved, (b_dys, 0, 0))]
-        + items(a1, a_dys, 1)
-        + items(a2, a_dys, 2)
-        + items(a3, a_dys, 3)
-        + items(b1, b_dys, 1),
-    )
-    out = place(out, width, items(a4, a_dys, 4) + items(b2, b_dys, 2) + items(b3, b_dys, 3))
-    out = place(out, width, items(b4, b_dys, 4))
+    right = move(right[:, :half], "z", NZ, 1)
+    left = move(left[:, half:], "z", NZ, -1)
+    out = place(None, width, items[0] + items[1] + items[2])
+    out = place(out, width, items[3])
+    out = place(out, width, [(right, (SIDES, 4, 0)), (left, (SIDES, 4, half))])
     return out.reshape(NY * NZ, COLS, width)
 
 

time: 134 us -> 131 us (0.978)
  the two profiles are of different devices: /device:TPU:8 before, /device:TPU:1 now
where the time goes in v1:
time: 131 us; the launch traced here: 129 us
  starting transfers between devices  62.2 us (47%)
  waiting for transfers between devices  51.1 us (39%)
  Pallas kernels  11.4 us (9%)
  matrix products  2.55 us (2%)
    ppermute x30, waiting for transfers between devices, move(): return lax.ppermute(value, axis, shift(size, by))  51.1 us
    ppermute x30, starting transfers between devices, move(): return lax.ppermute(value, axis, shift(size, by))  46.6 us
    all_to_all x1, starting transfers between devices, body(): own = lax.all_to_all(mine, 'z', 0, 0, tiled=True)  9.02 us
    all_to_all x1, starting transfers between devices, body(): xz = lax.all_to_all(sides, 'z', 0, 0, tiled=True)  6.57 us
    pallas_call x1, Pallas kernels, body(): pl.pallas_call(functools.partial(newton_kernel, math.sqrt(2048)), out_sha...  5.57 us
    pallas_call x3, Pallas kernels, place(): pl.pallas_call(functools.partial(place_kernel, places, n, int(aliased)),...  3.2 us
  transfers between devices with their start and end apart: 32, of which 14 were waited for; matrix products, arithmetic and copies ran while one was open for 2% of the time, Pallas kernels for 2%

profile of v1, /device:TPU:1, one launch (start us, length us, event | category | flops | bytes accessed | tf_op | source)
XLA Modules:
  0.0 128.6 jit_solution(1723790254069521525)
XLA Ops:
  0.0 1.9 %pack.1 = (bf16[8,64,128]{2,1,0:T(8,128)(2,1)S(1)}, bf16[8,64,128]{2,1,0:T(8,128)(2,1)S(1)}, bf16[8,64,128]{2,1,0:T(8,128)(2,1)S(1)}, bf16[8,64,128]{2,1,0:T(8,128)(2,1)S(1)}, bf16[8,16,768]{2,1,0:T(8,128)(2,1)}) custom-call(s32[1,32]{1,0:T(1,128)} %count_hbm.1, bf16[4,8,64,128]{3,2,1,0:T(8,128)(2,1)} %bitcast.21, bf16[4,8,8,16,768]{4,3,2,1,0:T(8,128)(2,1)} %bitcast.20), custom_call_target="tpu_custom_call" | custom-call | tf_op jit(solution)/shard_map/pack/pallas_call | solution.py:153
  1.9 9.0 %all-to-all-start.1 = ((bf16[8,16,768]{2,1,0:T(8,128)(2,1)}), bf16[8,16,768]{2,1,0:T(8,128)(2,1)S(1)}, u32[]{:S(2)}, u32[]{:S(2)}) async-start(bf16[8,16,768]{2,1,0:T(8,128)(2,1)} %get-tuple-element.18), calls=%async_computation.1 | async-start | bytes 393216 | tf_op jit(solution)/shard_map/all_to_all | solution.py:172
  10.9 1.3 %collective-permute-start = (bf16[8,64,128]{2,1,0:T(8,128)(2,1)S(1)}, bf16[8,64,128]{2,1,0:T(8,128)(2,1)S(1)}, u32[]{:S(2)}, u32[]{:S(2)}) collective-permute-start(bf16[8,64,128]{2,1,0:T(8,128)(2,1)S(1)} %get-tuple-element.15), channel_id=1, source_target_pairs={{0,8},{8,16},{16,24},{24,0},{1,9},{9,17},{17,25},{25,1},{2,10},{10... | collective-permute-start | bytes 393224 | tf_op jit(solution)/shard_map/ppermute | solution.py:146
  12.2 1.5 %collective-permute-start.1 = (bf16[8,64,128]{2,1,0:T(8,128)(2,1)S(1)}, bf16[8,64,128]{2,1,0:T(8,128)(2,1)S(1)}, u32[]{:S(2)}, u32[]{:S(2)}) collective-permute-start(bf16[8,64,128]{2,1,0:T(8,128)(2,1)S(1)} %get-tuple-element.16), channel_id=1, source_target_pairs={{0,24},{8,0},{16,8},{24,16},{1,25},{9,1},{17,9},{25,17},{2,26},{10... | collective-permute-start | bytes 393224 | tf_op jit(solution)/shard_map/ppermute | solution.py:146
  13.8 1.6 %collective-permute-start.2 = (bf16[8,64,128]{2,1,0:T(8,128)(2,1)S(1)}, bf16[8,64,128]{2,1,0:T(8,128)(2,1)S(1)}, u32[]{:S(2)}, u32[]{:S(2)}) collective-permute-start(bf16[8,64,128]{2,1,0:T(8,128)(2,1)S(1)} %get-tuple-element.17), channel_id=1, source_target_pairs={{0,16},{8,24},{16,0},{24,8},{1,17},{9,25},{17,1},{25,9},{2,18},{10... | collective-permute-start | bytes 393224 | tf_op jit(solution)/shard_map/ppermute | solution.py:146
  15.3 1.0 collective-permute-done
  16.4 4.4 %collective-permute-done.2 = bf16[8,64,128]{2,1,0:T(8,128)(2,1)S(1)} collective-permute-done((bf16[8,64,128]{2,1,0:T(8,128)(2,1)S(1)}, bf16[8,64,128]{2,1,0:T(8,128)(2,1)S(1)}, u32[]{:S(2)}, u32[]{:S(2)}) %collective-permute-start.2) | collective-permute-done | bytes 131104 | tf_op jit(solution)/shard_map/ppermute | solution.py:146
  20.8 0.9 pad_maximum_fusion
  21.6 6.6 %all-to-all-start = ((bf16[8,4,64,128]{3,2,1,0:T(8,128)(2,1)}), bf16[8,4,64,128]{3,2,1,0:T(8,128)(2,1)S(1)}, u32[]{:S(2)}, u32[]{:S(2)}) async-start(bf16[8,4,64,128]{3,2,1,0:T(8,128)(2,1)} %pad_maximum_fusion), calls=%async_computation | async-start | bytes 1048576 | tf_op jit(solution)/shard_map/all_to_all | solution.py:173
  28.2 2.5 %collective-permute-start.4 = (bf16[8,16,768]{2,1,0:T(8,128)(2,1)S(1)}, bf16[8,16,768]{2,1,0:T(8,128)(2,1)S(1)}, u32[]{:S(2)}, u32[]{:S(2)}) collective-permute-start(bf16[8,16,768]{2,1,0:T(8,128)(2,1)S(1)} %all-to-all-done.1.refs_0_), channel_id=1, source_target_pairs={{0,6},{2,0},{4,2},{6,4},{1,7},{3,1},{5,3},{7,5},{8,14},{10,8},{12,... | collective-permute-start | bytes 589832 | tf_op jit(solution)/shard_map/ppermute | solution.py:146
  30.7 2.3 %collective-permute-start.7 = (bf16[8,16,768]{2,1,0:T(8,128)(2,1)S(1)}, bf16[8,16,768]{2,1,0:T(8,128)(2,1)S(1)}, u32[]{:S(2)}, u32[]{:S(2)}) collective-permute-start(bf16[8,16,768]{2,1,0:T(8,128)(2,1)S(1)} %all-to-all-done.1.refs_0_), channel_id=1, source_target_pairs={{0,1},{1,0},{2,3},{3,2},{4,5},{5,4},{6,7},{7,6},{8,9},{9,8},{10,11... | collective-permute-start | bytes 589832 | tf_op jit(solution)/shard_map/ppermute | solution.py:146
  33.0 0.3 collective-permute-done.4.refs_2_
  33.3 3.2 %collective-permute-start.6 = (bf16[4,16,768]{2,1,0:T(8,128)(2,1)S(1)}, bf16[4,16,768]{2,1,0:T(8,128)(2,1)S(1)}, u32[]{:S(2)}, u32[]{:S(2)}) collective-permute-start(bf16[4,16,768]{2,1,0:T(8,128)(2,1)S(1)} %slice.25), channel_id=1, source_target_pairs={{0,6},{2,0},{4,2},{6,4},{1,7},{3,1},{5,3},{7,5},{8,14},{10,8},{12,... | collective-permute-start | bytes 294920 | tf_op jit(solution)/shard_map/ppermute | solution.py:146
  36.6 3.5 %collective-permute-start.9 = (bf16[8,16,768]{2,1,0:T(8,128)(2,1)S(1)}, bf16[8,16,768]{2,1,0:T(8,128)(2,1)S(1)}, u32[]{:S(2)}, u32[]{:S(2)}) collective-permute-start(bf16[8,16,768]{2,1,0:T(8,128)(2,1)S(1)} %collective-permute-done.4.refs_2_), channel_id=1, source_target_pairs={{0,1},{1,0},{2,3},{3,2},{4,5},{5,4},{6,7},{7,6},{8,9},{9,8},{10,11... | collective-permute-start | bytes 589832 | tf_op jit(solution)/shard_map/ppermute | solution.py:146
  40.1 0.1 collective-permute-start.8
  40.3 1.9 %collective-permute-start.11 = (bf16[4,16,768]{2,1,0:T(8,128)(2,1)S(1)}, bf16[4,16,768]{2,1,0:T(8,128)(2,1)S(1)}, u32[]{:S(2)}, u32[]{:S(2)}) collective-permute-start(bf16[4,16,768]{2,1,0:T(8,128)(2,1)S(1)} %collective-permute-done.6.refs_4_), channel_id=1, source_target_pairs={{0,1},{1,0},{2,3},{3,2},{4,5},{5,4},{6,7},{7,6},{8,9},{9,8},{10,11... | collective-permute-start | bytes 294920 | tf_op jit(solution)/shard_map/ppermute | solution.py:146
  42.2 3.7 %collective-permute-start.10 = (bf16[4,16,768]{2,1,0:T(8,128)(2,1)S(1)}, bf16[4,16,768]{2,1,0:T(8,128)(2,1)S(1)}, u32[]{:S(2)}, u32[]{:S(2)}) collective-permute-start(bf16[4,16,768]{2,1,0:T(8,128)(2,1)S(1)} %collective-permute-done.5.refs_3_), channel_id=1, source_target_pairs={{0,1},{1,0},{2,3},{3,2},{4,5},{5,4},{6,7},{7,6},{8,9},{9,8},{10,11... | collective-permute-start | bytes 294920 | tf_op jit(solution)/shard_map/ppermute | solution.py:146
  45.9 0.9 collective-permute-done.10.refs_8_
  46.8 0.7 grad.1.grad_ref
  47.6 2.7 %collective-permute-start.13 = (bf16[256,768]{1,0:T(8,128)(2,1)S(1)}, bf16[256,768]{1,0:T(8,128)(2,1)S(1)}, u32[]{:S(2)}, u32[]{:S(2)}) collective-permute-start(bf16[256,768]{1,0:T(8,128)(2,1)S(1)} %grad.1.grad_ref), channel_id=1, source_target_pairs={{0,6},{2,0},{4,2},{6,4},{1,7},{3,1},{5,3},{7,5},{8,14},{10,8},{12,... | collective-permute-start | bytes 1179656 | tf_op jit(solution)/shard_map/ppermute | solution.py:146
  50.3 8.9 %collective-permute-done.12 = bf16[256,768]{1,0:T(8,128)(2,1)S(1)} collective-permute-done((bf16[256,768]{1,0:T(8,128)(2,1)S(1)}, bf16[256,768]{1,0:T(8,128)(2,1)S(1)}, u32[]{:S(2)}, u32[]{:S(2)}) %collective-permute-start.12) | collective-permute-done | bytes 393248 | tf_op jit(solution)/shard_map/ppermute | solution.py:146
  59.1 0.5 fusion
  59.7 0.5 fusion.1
  60.2 0.5 add_add_fusion.1
  60.7 1.5 %collective-permute-start.16 = (f32[768,768]{1,0:T(8,128)S(1)}, f32[768,768]{1,0:T(8,128)S(1)}, u32[]{:S(2)}, u32[]{:S(2)}) collective-permute-start(f32[768,768]{1,0:T(8,128)S(1)} %add_add_fusion.1), channel_id=1, source_target_pairs={{0,1},{1,0},{2,3},{3,2},{4,5},{5,4},{6,7},{7,6},{8,9},{9,8},{10,11... | collective-permute-start | bytes 7077896 | tf_op jit(solution)/shard_map/ppermute | solution.py:146
  62.2 2.2 %collective-permute-start.15 = (bf16[128,768]{1,0:T(8,128)(2,1)S(1)}, bf16[128,768]{1,0:T(8,128)(2,1)S(1)}, u32[]{:S(2)}, u32[]{:S(2)}) collective-permute-start(bf16[128,768]{1,0:T(8,128)(2,1)S(1)} %slice.27), channel_id=1, source_target_pairs={{0,6},{2,0},{4,2},{6,4},{1,7},{3,1},{5,3},{7,5},{8,14},{10,8},{12,... | collective-permute-start | bytes 589832 | tf_op jit(solution)/shard_map/ppermute | solution.py:146
  64.5 4.2 %collective-permute-done.15 = bf16[128,768]{1,0:T(8,128)(2,1)S(1)} collective-permute-done((bf16[128,768]{1,0:T(8,128)(2,1)S(1)}, bf16[128,768]{1,0:T(8,128)(2,1)S(1)}, u32[]{:S(2)}, u32[]{:S(2)}) %collective-permute-start.15) | collective-permute-done | bytes 196640 | tf_op jit(solution)/shard_map/ppermute | solution.py:146
  68.7 0.9 collective-permute-start.18
  69.6 2.3 %collective-permute-done.14 = bf16[128,768]{1,0:T(8,128)(2,1)S(1)} collective-permute-done((bf16[128,768]{1,0:T(8,128)(2,1)S(1)}, bf16[128,768]{1,0:T(8,128)(2,1)S(1)}, u32[]{:S(2)}, u32[]{:S(2)}) %collective-permute-start.14) | collective-permute-done | bytes 196640 | tf_op jit(solution)/shard_map/ppermute | solution.py:146
  71.9 1.2 collective-permute-start.17
  73.0 0.5 fusion.2
  73.5 0.5 add_add_fusion.mine_ref
  74.1 5.6 %newton.1 = (bf16[1,64,768]{2,1,0:T(8,128)(2,1)S(1)}, bf16[1,64,768]{2,1,0:T(8,128)(2,1)S(1)}, bf16[1,64,768]{2,1,0:T(8,128)(2,1)S(1)}, bf16[1,64,768]{2,1,0:T(8,128)(2,1)S(1)}) custom-call(f32[768,768]{1,0:T(8,128)S(1)} %add_add_fusion.mine_ref, f32[768,768]{1,0:T(8,128)S(1)} %collective-permute-done.16.other_ref, ...), custom_call_target="tpu_custom_call" | custom-call | tf_op jit(solution)/shard_map/newton/pallas_call | solution.py:204
  79.7 1.7 %collective-permute-start.19 = (bf16[1,64,768]{2,1,0:T(8,128)(2,1)S(1)}, bf16[1,64,768]{2,1,0:T(8,128)(2,1)S(1)}, u32[]{:S(2)}, u32[]{:S(2)}) collective-permute-start(bf16[1,64,768]{2,1,0:T(8,128)(2,1)S(1)} %get-tuple-element.20), channel_id=1, source_target_pairs={{0,24},{8,0},{16,8},{24,16},{1,25},{9,1},{17,9},{25,17},{2,26},{10... | collective-permute-start | bytes 294920 | tf_op jit(solution)/shard_map/ppermute | solution.py:146
  81.4 1.3 collective-permute-start.21
  82.7 1.1 collective-permute-done.19
  83.8 5.1 %collective-permute-done.20 = bf16[1,64,768]{2,1,0:T(8,128)(2,1)S(1)} collective-permute-done((bf16[1,64,768]{2,1,0:T(8,128)(2,1)S(1)}, bf16[1,64,768]{2,1,0:T(8,128)(2,1)S(1)}, u32[]{:S(2)}, u32[]{:S(2)}) %collective-permute-start.20) | collective-permute-done | bytes 98336 | tf_op jit(solution)/shard_map/ppermute | solution.py:146
  88.9 3.0 %collective-permute-start.26 = (bf16[4,64,768]{2,1,0:T(8,128)(2,1)S(1)}, bf16[4,64,768]{2,1,0:T(8,128)(2,1)S(1)}, u32[]{:S(2)}, u32[]{:S(2)}) collective-permute-start(bf16[4,64,768]{2,1,0:T(8,128)(2,1)S(1)} %constant_dynamic-update-slice_fusion.refs_0_), channel_id=1, source_target_pairs={{0,224},{32,0},{64,32},{96,64},{128,96},{160,128},{192,160},{224,1... | collective-permute-start | bytes 1179656 | tf_op jit(solution)/shard_map/ppermute | solution.py:146
  91.9 7.4 %collective-permute-done.26.refs_2_ = bf16[4,64,768]{2,1,0:T(8,128)(2,1)S(1)} collective-permute-done((bf16[4,64,768]{2,1,0:T(8,128)(2,1)S(1)}, bf16[4,64,768]{2,1,0:T(8,128)(2,1)S(1)}, u32[]{:S(2)}, u32[]{:S(2)}) %collective-permute-start.26) | collective-permute-done | bytes 393248 | tf_op jit(solution)/shard_map/ppermute | solution.py:146
  99.3 3.4 %collective-permute-start.27 = (bf16[4,64,768]{2,1,0:T(8,128)(2,1)S(1)}, bf16[4,64,768]{2,1,0:T(8,128)(2,1)S(1)}, u32[]{:S(2)}, u32[]{:S(2)}) collective-permute-start(bf16[4,64,768]{2,1,0:T(8,128)(2,1)S(1)} %collective-permute-done.26.refs_2_), channel_id=1, source_target_pairs={{0,224},{32,0},{64,32},{96,64},{128,96},{160,128},{192,160},{224,1... | collective-permute-start | bytes 1179656 | tf_op jit(solution)/shard_map/ppermute | solution.py:146
  102.7 6.5 %collective-permute-done.27.refs_4_ = bf16[4,64,768]{2,1,0:T(8,128)(2,1)S(1)} collective-permute-done((bf16[4,64,768]{2,1,0:T(8,128)(2,1)S(1)}, bf16[4,64,768]{2,1,0:T(8,128)(2,1)S(1)}, u32[]{:S(2)}, u32[]{:S(2)}) %collective-permute-start.27) | collective-permute-done | bytes 393248 | tf_op jit(solution)/shard_map/ppermute | solution.py:146
  109.2 3.4 %collective-permute-start.28 = (bf16[4,64,768]{2,1,0:T(8,128)(2,1)S(1)}, bf16[4,64,768]{2,1,0:T(8,128)(2,1)S(1)}, u32[]{:S(2)}, u32[]{:S(2)}) collective-permute-start(bf16[4,64,768]{2,1,0:T(8,128)(2,1)S(1)} %collective-permute-done.27.refs_4_), channel_id=1, source_target_pairs={{0,224},{32,0},{64,32},{96,64},{128,96},{160,128},{192,160},{224,1... | collective-permute-start | bytes 1179656 | tf_op jit(solution)/shard_map/ppermute | solution.py:146
  112.6 5.6 %collective-permute-done.28.refs_1_ = bf16[4,64,768]{2,1,0:T(8,128)(2,1)S(1)} collective-permute-done((bf16[4,64,768]{2,1,0:T(8,128)(2,1)S(1)}, bf16[4,64,768]{2,1,0:T(8,128)(2,1)S(1)}, u32[]{:S(2)}, u32[]{:S(2)}) %collective-permute-start.28) | collective-permute-done | bytes 393248 | tf_op jit(solution)/shard_map/ppermute | solution.py:146
  118.3 3.5 %collective-permute-start.29 = (bf16[4,32,768]{2,1,0:T(8,128)(2,1)S(1)}, bf16[4,32,768]{2,1,0:T(8,128)(2,1)S(1)}, u32[]{:S(2)}, u32[]{:S(2)}) collective-permute-start(bf16[4,32,768]{2,1,0:T(8,128)(2,1)S(1)} %slice.29), channel_id=1, source_target_pairs={{0,224},{32,0},{64,32},{96,64},{128,96},{160,128},{192,160},{224,1... | collective-permute-start | bytes 589832 | tf_op jit(solution)/shard_map/ppermute | solution.py:146
  121.9 1.4 %shard_map.37.refs_2_ = bf16[4,8,64,768]{3,2,1,0:T(8,128)(2,1)} custom-call(bf16[4,64,768]{2,1,0:T(8,128)(2,1)S(1)} %constant_dynamic-update-slice_fusion.refs_0_, bf16[4,64,768]{2,1,0:T(8,128)(2,1)S(1)} %collective-permute-done.22.refs_1_, bf16[4,64,768]{2,1,0:T(8,128)(2,1)S(1)} %collective-permute-done.26.refs_2_, ...), custom_call_target="tpu_custom_call" | custom-call | tf_op jit(solution)/shard_map/pallas_call | solution.py:134
  123.3 1.0 shard_map.38.refs_2_
  124.4 3.2 %collective-permute-done.25.refs_0_ = bf16[4,32,768]{2,1,0:T(8,128)(2,1)S(1)} collective-permute-done((bf16[4,32,768]{2,1,0:T(8,128)(2,1)S(1)}, bf16[4,32,768]{2,1,0:T(8,128)(2,1)S(1)}, u32[]{:S(2)}, u32[]{:S(2)}) %collective-permute-start.25) | collective-permute-done | bytes 196640 | tf_op jit(solution)/shard_map/ppermute | solution.py:146
  127.6 0.8 shard_map.39
  (38 shorter events, 0.6 us)
Async XLA Ops:
  1.9 19.7 %all-to-all-start.1 = ((bf16[8,16,768]{2,1,0:T(8,128)(2,1)}), bf16[8,16,768]{2,1,0:T(8,128)(2,1)S(1)}, u32[]{:S(2)}, u32[]{:S(2)}) async-start(bf16[8,16,768]{2,1,0:T(8,128)(2,1)} %get-tuple-element.18), calls=%async_computation.1 | async-start | bytes 393216 | tf_op jit(solution)/shard_map/all_to_all | solution.py:172
  10.9 5.4 %collective-permute-start = (bf16[8,64,128]{2,1,0:T(8,128)(2,1)S(1)}, bf16[8,64,128]{2,1,0:T(8,128)(2,1)S(1)}, u32[]{:S(2)}, u32[]{:S(2)}) collective-permute-start(bf16[8,64,128]{2,1,0:T(8,128)(2,1)S(1)} %get-tuple-element.15), channel_id=1, source_target_pairs={{0,8},{8,16},{16,24},{24,0},{1,9},{9,17},{17,25},{25,1},{2,10},{10... | collective-permute-start | bytes 393224 | tf_op jit(solution)/shard_map/ppermute | solution.py:146
  12.2 4.1 %collective-permute-start.1 = (bf16[8,64,128]{2,1,0:T(8,128)(2,1)S(1)}, bf16[8,64,128]{2,1,0:T(8,128)(2,1)S(1)}, u32[]{:S(2)}, u32[]{:S(2)}) collective-permute-start(bf16[8,64,128]{2,1,0:T(8,128)(2,1)S(1)} %get-tuple-element.16), channel_id=1, source_target_pairs={{0,24},{8,0},{16,8},{24,16},{1,25},{9,1},{17,9},{25,17},{2,26},{10... | collective-permute-start | bytes 393224 | tf_op jit(solution)/shard_map/ppermute | solution.py:146
  13.8 7.0 %collective-permute-start.2 = (bf16[8,64,128]{2,1,0:T(8,128)(2,1)S(1)}, bf16[8,64,128]{2,1,0:T(8,128)(2,1)S(1)}, u32[]{:S(2)}, u32[]{:S(2)}) collective-permute-start(bf16[8,64,128]{2,1,0:T(8,128)(2,1)S(1)} %get-tuple-element.17), channel_id=1, source_target_pairs={{0,16},{8,24},{16,0},{24,8},{1,17},{9,25},{17,1},{25,9},{2,18},{10... | collective-permute-start | bytes 393224 | tf_op jit(solution)/shard_map/ppermute | solution.py:146
  21.6 25.2 %all-to-all-start = ((bf16[8,4,64,128]{3,2,1,0:T(8,128)(2,1)}), bf16[8,4,64,128]{3,2,1,0:T(8,128)(2,1)S(1)}, u32[]{:S(2)}, u32[]{:S(2)}) async-start(bf16[8,4,64,128]{3,2,1,0:T(8,128)(2,1)} %pad_maximum_fusion), calls=%async_computation | async-start | bytes 1048576 | tf_op jit(solution)/shard_map/all_to_all | solution.py:173
  28.2 5.1 %collective-permute-start.4 = (bf16[8,16,768]{2,1,0:T(8,128)(2,1)S(1)}, bf16[8,16,768]{2,1,0:T(8,128)(2,1)S(1)}, u32[]{:S(2)}, u32[]{:S(2)}) collective-permute-start(bf16[8,16,768]{2,1,0:T(8,128)(2,1)S(1)} %all-to-all-done.1.refs_0_), channel_id=1, source_target_pairs={{0,6},{2,0},{4,2},{6,4},{1,7},{3,1},{5,3},{7,5},{8,14},{10,8},{12,... | collective-permute-start | bytes 589832 | tf_op jit(solution)/shard_map/ppermute | solution.py:146
  30.7 5.8 %collective-permute-start.3 = (bf16[8,16,768]{2,1,0:T(8,128)(2,1)S(1)}, bf16[8,16,768]{2,1,0:T(8,128)(2,1)S(1)}, u32[]{:S(2)}, u32[]{:S(2)}) collective-permute-start(bf16[8,16,768]{2,1,0:T(8,128)(2,1)S(1)} %all-to-all-done.1.refs_0_), channel_id=1, source_target_pairs={{0,2},{2,4},{4,6},{6,0},{1,3},{3,5},{5,7},{7,1},{8,10},{10,12},{12... | collective-permute-start | bytes 589832 | tf_op jit(solution)/shard_map/ppermute | solution.py:146
  30.7 15.2 %collective-permute-start.7 = (bf16[8,16,768]{2,1,0:T(8,128)(2,1)S(1)}, bf16[8,16,768]{2,1,0:T(8,128)(2,1)S(1)}, u32[]{:S(2)}, u32[]{:S(2)}) collective-permute-start(bf16[8,16,768]{2,1,0:T(8,128)(2,1)S(1)} %all-to-all-done.1.refs_0_), channel_id=1, source_target_pairs={{0,1},{1,0},{2,3},{3,2},{4,5},{5,4},{6,7},{7,6},{8,9},{9,8},{10,11... | collective-permute-start | bytes 589832 | tf_op jit(solution)/shard_map/ppermute | solution.py:146
  33.3 6.9 %collective-permute-start.6 = (bf16[4,16,768]{2,1,0:T(8,128)(2,1)S(1)}, bf16[4,16,768]{2,1,0:T(8,128)(2,1)S(1)}, u32[]{:S(2)}, u32[]{:S(2)}) collective-permute-start(bf16[4,16,768]{2,1,0:T(8,128)(2,1)S(1)} %slice.25), channel_id=1, source_target_pairs={{0,6},{2,0},{4,2},{6,4},{1,7},{3,1},{5,3},{7,5},{8,14},{10,8},{12,... | collective-permute-start | bytes 294920 | tf_op jit(solution)/shard_map/ppermute | solution.py:146
  36.6 5.6 %collective-permute-start.5 = (bf16[4,16,768]{2,1,0:T(8,128)(2,1)S(1)}, bf16[4,16,768]{2,1,0:T(8,128)(2,1)S(1)}, u32[]{:S(2)}, u32[]{:S(2)}) collective-permute-start(bf16[4,16,768]{2,1,0:T(8,128)(2,1)S(1)} %slice.24), channel_id=1, source_target_pairs={{0,2},{2,4},{4,6},{6,0},{1,3},{3,5},{5,7},{7,1},{8,10},{10,12},{12... | collective-permute-start | bytes 294920 | tf_op jit(solution)/shard_map/ppermute | solution.py:146
  36.6 9.2 %collective-permute-start.9 = (bf16[8,16,768]{2,1,0:T(8,128)(2,1)S(1)}, bf16[8,16,768]{2,1,0:T(8,128)(2,1)S(1)}, u32[]{:S(2)}, u32[]{:S(2)}) collective-permute-start(bf16[8,16,768]{2,1,0:T(8,128)(2,1)S(1)} %collective-permute-done.4.refs_2_), channel_id=1, source_target_pairs={{0,1},{1,0},{2,3},{3,2},{4,5},{5,4},{6,7},{7,6},{8,9},{9,8},{10,11... | collective-permute-start | bytes 589832 | tf_op jit(solution)/shard_map/ppermute | solution.py:146
  40.1 6.7 %collective-permute-start.8 = (bf16[8,16,768]{2,1,0:T(8,128)(2,1)S(1)}, bf16[8,16,768]{2,1,0:T(8,128)(2,1)S(1)}, u32[]{:S(2)}, u32[]{:S(2)}) collective-permute-start(bf16[8,16,768]{2,1,0:T(8,128)(2,1)S(1)} %collective-permute-done.3.refs_1_), channel_id=1, source_target_pairs={{0,1},{1,0},{2,3},{3,2},{4,5},{5,4},{6,7},{7,6},{8,9},{9,8},{10,11... | collective-permute-start | bytes 589832 | tf_op jit(solution)/shard_map/ppermute | solution.py:146
  40.3 5.6 %collective-permute-start.11 = (bf16[4,16,768]{2,1,0:T(8,128)(2,1)S(1)}, bf16[4,16,768]{2,1,0:T(8,128)(2,1)S(1)}, u32[]{:S(2)}, u32[]{:S(2)}) collective-permute-start(bf16[4,16,768]{2,1,0:T(8,128)(2,1)S(1)} %collective-permute-done.6.refs_4_), channel_id=1, source_target_pairs={{0,1},{1,0},{2,3},{3,2},{4,5},{5,4},{6,7},{7,6},{8,9},{9,8},{10,11... | collective-permute-start | bytes 294920 | tf_op jit(solution)/shard_map/ppermute | solution.py:146
  42.2 4.6 %collective-permute-start.10 = (bf16[4,16,768]{2,1,0:T(8,128)(2,1)S(1)}, bf16[4,16,768]{2,1,0:T(8,128)(2,1)S(1)}, u32[]{:S(2)}, u32[]{:S(2)}) collective-permute-start(bf16[4,16,768]{2,1,0:T(8,128)(2,1)S(1)} %collective-permute-done.5.refs_3_), channel_id=1, source_target_pairs={{0,1},{1,0},{2,3},{3,2},{4,5},{5,4},{6,7},{7,6},{8,9},{9,8},{10,11... | collective-permute-start | bytes 294920 | tf_op jit(solution)/shard_map/ppermute | solution.py:146
  47.5 11.6 %collective-permute-start.12 = (bf16[256,768]{1,0:T(8,128)(2,1)S(1)}, bf16[256,768]{1,0:T(8,128)(2,1)S(1)}, u32[]{:S(2)}, u32[]{:S(2)}) collective-permute-start(bf16[256,768]{1,0:T(8,128)(2,1)S(1)} %grad.1.grad_ref), channel_id=1, source_target_pairs={{0,2},{2,4},{4,6},{6,0},{1,3},{3,5},{5,7},{7,1},{8,10},{10,12},{12... | collective-permute-start | bytes 1179656 | tf_op jit(solution)/shard_map/ppermute | solution.py:146
  47.6 12.0 %collective-permute-start.13 = (bf16[256,768]{1,0:T(8,128)(2,1)S(1)}, bf16[256,768]{1,0:T(8,128)(2,1)S(1)}, u32[]{:S(2)}, u32[]{:S(2)}) collective-permute-start(bf16[256,768]{1,0:T(8,128)(2,1)S(1)} %grad.1.grad_ref), channel_id=1, source_target_pairs={{0,6},{2,0},{4,2},{6,4},{1,7},{3,1},{5,3},{7,5},{8,14},{10,8},{12,... | collective-permute-start | bytes 1179656 | tf_op jit(solution)/shard_map/ppermute | solution.py:146
  60.7 13.4 %collective-permute-start.16 = (f32[768,768]{1,0:T(8,128)S(1)}, f32[768,768]{1,0:T(8,128)S(1)}, u32[]{:S(2)}, u32[]{:S(2)}) collective-permute-start(f32[768,768]{1,0:T(8,128)S(1)} %add_add_fusion.1), channel_id=1, source_target_pairs={{0,1},{1,0},{2,3},{3,2},{4,5},{5,4},{6,7},{7,6},{8,9},{9,8},{10,11... | collective-permute-start | bytes 7077896 | tf_op jit(solution)/shard_map/ppermute | solution.py:146
  62.2 6.5 %collective-permute-start.15 = (bf16[128,768]{1,0:T(8,128)(2,1)S(1)}, bf16[128,768]{1,0:T(8,128)(2,1)S(1)}, u32[]{:S(2)}, u32[]{:S(2)}) collective-permute-start(bf16[128,768]{1,0:T(8,128)(2,1)S(1)} %slice.27), channel_id=1, source_target_pairs={{0,6},{2,0},{4,2},{6,4},{1,7},{3,1},{5,3},{7,5},{8,14},{10,8},{12,... | collective-permute-start | bytes 589832 | tf_op jit(solution)/shard_map/ppermute | solution.py:146
  64.4 7.4 %collective-permute-start.14 = (bf16[128,768]{1,0:T(8,128)(2,1)S(1)}, bf16[128,768]{1,0:T(8,128)(2,1)S(1)}, u32[]{:S(2)}, u32[]{:S(2)}) collective-permute-start(bf16[128,768]{1,0:T(8,128)(2,1)S(1)} %slice.26), channel_id=1, source_target_pairs={{0,2},{2,4},{4,6},{6,0},{1,3},{3,5},{5,7},{7,1},{8,10},{10,12},{12... | collective-permute-start | bytes 589832 | tf_op jit(solution)/shard_map/ppermute | solution.py:146
  68.7 5.3 %collective-permute-start.18 = (bf16[128,768]{1,0:T(8,128)(2,1)S(1)}, bf16[128,768]{1,0:T(8,128)(2,1)S(1)}, u32[]{:S(2)}, u32[]{:S(2)}) collective-permute-start(bf16[128,768]{1,0:T(8,128)(2,1)S(1)} %collective-permute-done.15), channel_id=1, source_target_pairs={{0,1},{1,0},{2,3},{3,2},{4,5},{5,4},{6,7},{7,6},{8,9},{9,8},{10,11... | collective-permute-start | bytes 589832 | tf_op jit(solution)/shard_map/ppermute | solution.py:146
  71.9 2.2 %collective-permute-start.17 = (bf16[128,768]{1,0:T(8,128)(2,1)S(1)}, bf16[128,768]{1,0:T(8,128)(2,1)S(1)}, u32[]{:S(2)}, u32[]{:S(2)}) collective-permute-start(bf16[128,768]{1,0:T(8,128)(2,1)S(1)} %collective-permute-done.14), channel_id=1, source_target_pairs={{0,1},{1,0},{2,3},{3,2},{4,5},{5,4},{6,7},{7,6},{8,9},{9,8},{10,11... | collective-permute-start | bytes 589832 | tf_op jit(solution)/shard_map/ppermute | solution.py:146
  79.7 4.1 %collective-permute-start.19 = (bf16[1,64,768]{2,1,0:T(8,128)(2,1)S(1)}, bf16[1,64,768]{2,1,0:T(8,128)(2,1)S(1)}, u32[]{:S(2)}, u32[]{:S(2)}) collective-permute-start(bf16[1,64,768]{2,1,0:T(8,128)(2,1)S(1)} %get-tuple-element.20), channel_id=1, source_target_pairs={{0,24},{8,0},{16,8},{24,16},{1,25},{9,1},{17,9},{25,17},{2,26},{10... | collective-permute-start | bytes 294920 | tf_op jit(solution)/shard_map/ppermute | solution.py:146
  81.4 7.4 %collective-permute-start.20 = (bf16[1,64,768]{2,1,0:T(8,128)(2,1)S(1)}, bf16[1,64,768]{2,1,0:T(8,128)(2,1)S(1)}, u32[]{:S(2)}, u32[]{:S(2)}) collective-permute-start(bf16[1,64,768]{2,1,0:T(8,128)(2,1)S(1)} %get-tuple-element.21), channel_id=1, source_target_pairs={{0,8},{8,16},{16,24},{24,0},{1,9},{9,17},{17,25},{25,1},{2,10},{10... | collective-permute-start | bytes 294920 | tf_op jit(solution)/shard_map/ppermute | solution.py:146
  81.4 7.4 %collective-permute-start.21 = (bf16[1,64,768]{2,1,0:T(8,128)(2,1)S(1)}, bf16[1,64,768]{2,1,0:T(8,128)(2,1)S(1)}, u32[]{:S(2)}, u32[]{:S(2)}) collective-permute-start(bf16[1,64,768]{2,1,0:T(8,128)(2,1)S(1)} %get-tuple-element.22), channel_id=1, source_target_pairs={{0,16},{8,24},{16,0},{24,8},{1,17},{9,25},{17,1},{25,9},{2,18},{10... | collective-permute-start | bytes 294920 | tf_op jit(solution)/shard_map/ppermute | solution.py:146
  88.9 10.4 %collective-permute-start.26 = (bf16[4,64,768]{2,1,0:T(8,128)(2,1)S(1)}, bf16[4,64,768]{2,1,0:T(8,128)(2,1)S(1)}, u32[]{:S(2)}, u32[]{:S(2)}) collective-permute-start(bf16[4,64,768]{2,1,0:T(8,128)(2,1)S(1)} %constant_dynamic-update-slice_fusion.refs_0_), channel_id=1, source_target_pairs={{0,224},{32,0},{64,32},{96,64},{128,96},{160,128},{192,160},{224,1... | collective-permute-start | bytes 1179656 | tf_op jit(solution)/shard_map/ppermute | solution.py:146
  91.9 10.8 %collective-permute-start.22 = (bf16[4,64,768]{2,1,0:T(8,128)(2,1)S(1)}, bf16[4,64,768]{2,1,0:T(8,128)(2,1)S(1)}, u32[]{:S(2)}, u32[]{:S(2)}) collective-permute-start(bf16[4,64,768]{2,1,0:T(8,128)(2,1)S(1)} %constant_dynamic-update-slice_fusion.refs_0_), channel_id=1, source_target_pairs={{0,32},{32,64},{64,96},{96,128},{128,160},{160,192},{192,224},{224... | collective-permute-start | bytes 1179656 | tf_op jit(solution)/shard_map/ppermute | solution.py:146
  99.3 9.9 %collective-permute-start.27 = (bf16[4,64,768]{2,1,0:T(8,128)(2,1)S(1)}, bf16[4,64,768]{2,1,0:T(8,128)(2,1)S(1)}, u32[]{:S(2)}, u32[]{:S(2)}) collective-permute-start(bf16[4,64,768]{2,1,0:T(8,128)(2,1)S(1)} %collective-permute-done.26.refs_2_), channel_id=1, source_target_pairs={{0,224},{32,0},{64,32},{96,64},{128,96},{160,128},{192,160},{224,1... | collective-permute-start | bytes 1179656 | tf_op jit(solution)/shard_map/ppermute | solution.py:146
  102.7 9.9 %collective-permute-start.23 = (bf16[4,64,768]{2,1,0:T(8,128)(2,1)S(1)}, bf16[4,64,768]{2,1,0:T(8,128)(2,1)S(1)}, u32[]{:S(2)}, u32[]{:S(2)}) collective-permute-start(bf16[4,64,768]{2,1,0:T(8,128)(2,1)S(1)} %collective-permute-done.22.refs_1_), channel_id=1, source_target_pairs={{0,32},{32,64},{64,96},{96,128},{128,160},{160,192},{192,224},{224... | collective-permute-start | bytes 1179656 | tf_op jit(solution)/shard_map/ppermute | solution.py:146
  109.2 9.1 %collective-permute-start.28 = (bf16[4,64,768]{2,1,0:T(8,128)(2,1)S(1)}, bf16[4,64,768]{2,1,0:T(8,128)(2,1)S(1)}, u32[]{:S(2)}, u32[]{:S(2)}) collective-permute-start(bf16[4,64,768]{2,1,0:T(8,128)(2,1)S(1)} %collective-permute-done.27.refs_4_), channel_id=1, source_target_pairs={{0,224},{32,0},{64,32},{96,64},{128,96},{160,128},{192,160},{224,1... | collective-permute-start | bytes 1179656 | tf_op jit(solution)/shard_map/ppermute | solution.py:146
  112.6 9.2 %collective-permute-start.24 = (bf16[4,64,768]{2,1,0:T(8,128)(2,1)S(1)}, bf16[4,64,768]{2,1,0:T(8,128)(2,1)S(1)}, u32[]{:S(2)}, u32[]{:S(2)}) collective-permute-start(bf16[4,64,768]{2,1,0:T(8,128)(2,1)S(1)} %collective-permute-done.23.refs_3_), channel_id=1, source_target_pairs={{0,32},{32,64},{64,96},{96,128},{128,160},{160,192},{192,224},{224... | collective-permute-start | bytes 1179656 | tf_op jit(solution)/shard_map/ppermute | solution.py:146
  118.3 6.1 %collective-permute-start.29 = (bf16[4,32,768]{2,1,0:T(8,128)(2,1)S(1)}, bf16[4,32,768]{2,1,0:T(8,128)(2,1)S(1)}, u32[]{:S(2)}, u32[]{:S(2)}) collective-permute-start(bf16[4,32,768]{2,1,0:T(8,128)(2,1)S(1)} %slice.29), channel_id=1, source_target_pairs={{0,224},{32,0},{64,32},{96,64},{128,96},{160,128},{192,160},{224,1... | collective-permute-start | bytes 589832 | tf_op jit(solution)/shard_map/ppermute | solution.py:146
  121.8 5.8 %collective-permute-start.25 = (bf16[4,32,768]{2,1,0:T(8,128)(2,1)S(1)}, bf16[4,32,768]{2,1,0:T(8,128)(2,1)S(1)}, u32[]{:S(2)}, u32[]{:S(2)}) collective-permute-start(bf16[4,32,768]{2,1,0:T(8,128)(2,1)S(1)} %slice.28), channel_id=1, source_target_pairs={{0,32},{32,64},{64,96},{96,128},{128,160},{160,192},{192,224},{224... | collective-permute-start | bytes 589832 | tf_op jit(solution)/shard_map/ppermute | solution.py:146

commit v2 on v1

--- a/solution.py
+++ b/solution.py
@@ -18,6 +18,7 @@
 NZ, NY, NX, NC = 8, 4, 4, 2
 COLS, CAP = 64, 128
 SIDES = (0, 1, 3, 2)
+CHUNKS = ((0, 1), (2, 3))
 
 VMEM = pl.BlockSpec(memory_space=pltpu.VMEM)
 ANY = pl.BlockSpec(memory_space=pl.ANY)
@@ -211,19 +212,25 @@
     )(*near(total, other, other_far_a, other_far_b, grad))
 
     rows = [pieces[0]] + [move(pieces[k], "y", NY, -SIDES[k]) for k in range(1, NY)]
-    rows = jnp.stack([r[0] for r in rows])
-    right, left = rows, rows
-    items = [[(rows, (SIDES, 0, 0))]]
-    for n in range(1, 4):
-        right = move(right, "z", NZ, 1)
-        left = move(left, "z", NZ, -1)
-        items.append([(right, (SIDES, -n, 0)), (left, (SIDES, n, 0))])
     half = COLS // 2
-    right = move(right[:, :half], "z", NZ, 1)
-    left = move(left[:, half:], "z", NZ, -1)
-    out = place(None, width, items[0] + items[1] + items[2])
-    out = place(out, width, items[3])
-    out = place(out, width, [(right, (SIDES, 4, 0)), (left, (SIDES, 4, half))])
+    items = []
+    for ks in CHUNKS:
+        piece = jnp.stack([rows[k][0] for k in ks])
+        dys = tuple(SIDES[k] for k in ks)
+        items.append([(piece, (dys, 0, 0))])
+        right, left = piece, piece
+        for n in range(1, 4):
+            right = move(right, "z", NZ, 1)
+            left = move(left, "z", NZ, -1)
+            items[-1] += [(right, (dys, -n, 0)), (left, (dys, n, 0))]
+        right = move(right[:, :half], "z", NZ, 1)
+        left = move(left[:, half:], "z", NZ, -1)
+        items[-1] += [(right, (dys, 4, 0)), (left, (dys, 4, half))]
+    a, b = items
+    out = place(None, width, a[:5] + b[:3])
+    out = place(out, width, a[5:7] + b[3:5])
+    out = place(out, width, a[7:] + b[5:7])
+    out = place(out, width, b[7:])
     return out.reshape(NY * NZ, COLS, width)
 
 

time: 131 us -> 128 us (0.977)
  the two profiles are of different devices: /device:TPU:1 before, /device:TPU:24 now
where the time goes in v2:
time: 128 us; the launch traced here: 127 us
  starting transfers between devices  63.8 us (50%)
  waiting for transfers between devices  47.6 us (37%)
  Pallas kernels  12 us (9%)
  matrix products  2.55 us (2%)
    ppermute x38, starting transfers between devices, move(): return lax.ppermute(value, axis, shift(size, by))  48.6 us
    ppermute x38, waiting for transfers between devices, move(): return lax.ppermute(value, axis, shift(size, by))  47.2 us
    all_to_all x1, starting transfers between devices, body(): own = lax.all_to_all(mine, 'z', 0, 0, tiled=True)  8.48 us
    all_to_all x1, starting transfers between devices, body(): xz = lax.all_to_all(sides, 'z', 0, 0, tiled=True)  6.74 us
    pallas_call x1, Pallas kernels, body(): pl.pallas_call(functools.partial(newton_kernel, math.sqrt(2048)), out_sha...  5.57 us
    pallas_call x4, Pallas kernels, place(): pl.pallas_call(functools.partial(place_kernel, places, n, int(aliased)),...  3.81 us
  transfers between devices with their start and end apart: 40, of which 19 were waited for; matrix products, arithmetic and copies ran while one was open for 2% of the time, Pallas kernels for 2%

profile of v2, /device:TPU:24, one launch (start us, length us, event | category | flops | bytes accessed | tf_op | source)
XLA Modules:
  0.0 127.4 jit_solution(5768132169677283514)
XLA Ops:
  0.0 1.9 %pack.1 = (bf16[8,64,128]{2,1,0:T(8,128)(2,1)S(1)}, bf16[8,64,128]{2,1,0:T(8,128)(2,1)S(1)}, bf16[8,64,128]{2,1,0:T(8,128)(2,1)S(1)}, bf16[8,64,128]{2,1,0:T(8,128)(2,1)S(1)}, bf16[8,16,768]{2,1,0:T(8,128)(2,1)}) custom-call(s32[1,32]{1,0:T(1,128)} %count_hbm.1, bf16[4,8,64,128]{3,2,1,0:T(8,128)(2,1)} %bitcast.21, bf16[4,8,8,16,768]{4,3,2,1,0:T(8,128)(2,1)} %bitcast.20), custom_call_target="tpu_custom_call" | custom-call | tf_op jit(solution)/shard_map/pack/pallas_call | solution.py:154
  1.9 8.5 %all-to-all-start.1 = ((bf16[8,16,768]{2,1,0:T(8,128)(2,1)}), bf16[8,16,768]{2,1,0:T(8,128)(2,1)S(1)}, u32[]{:S(2)}, u32[]{:S(2)}) async-start(bf16[8,16,768]{2,1,0:T(8,128)(2,1)} %get-tuple-element.18), calls=%async_computation.1 | async-start | bytes 393216 | tf_op jit(solution)/shard_map/all_to_all | solution.py:173
  10.6 1.8 %collective-permute-start.1 = (bf16[8,64,128]{2,1,0:T(8,128)(2,1)S(1)}, bf16[8,64,128]{2,1,0:T(8,128)(2,1)S(1)}, u32[]{:S(2)}, u32[]{:S(2)}) collective-permute-start(bf16[8,64,128]{2,1,0:T(8,128)(2,1)S(1)} %get-tuple-element.16), channel_id=1, source_target_pairs={{0,24},{8,0},{16,8},{24,16},{1,25},{9,1},{17,9},{25,17},{2,26},{10... | collective-permute-start | bytes 393224 | tf_op jit(solution)/shard_map/ppermute | solution.py:147
  12.4 1.2 collective-permute-start.2
  13.7 2.6 %collective-permute-done = bf16[8,64,128]{2,1,0:T(8,128)(2,1)S(1)} collective-permute-done((bf16[8,64,128]{2,1,0:T(8,128)(2,1)S(1)}, bf16[8,64,128]{2,1,0:T(8,128)(2,1)S(1)}, u32[]{:S(2)}, u32[]{:S(2)}) %collective-permute-start) | collective-permute-done | bytes 131104 | tf_op jit(solution)/shard_map/ppermute | solution.py:147
  16.3 3.3 %collective-permute-done.1 = bf16[8,64,128]{2,1,0:T(8,128)(2,1)S(1)} collective-permute-done((bf16[8,64,128]{2,1,0:T(8,128)(2,1)S(1)}, bf16[8,64,128]{2,1,0:T(8,128)(2,1)S(1)}, u32[]{:S(2)}, u32[]{:S(2)}) %collective-permute-start.1) | collective-permute-done | bytes 131104 | tf_op jit(solution)/shard_map/ppermute | solution.py:147
  19.6 0.9 pad_maximum_fusion
  20.9 6.7 %all-to-all-start = ((bf16[8,4,64,128]{3,2,1,0:T(8,128)(2,1)}), bf16[8,4,64,128]{3,2,1,0:T(8,128)(2,1)S(1)}, u32[]{:S(2)}, u32[]{:S(2)}) async-start(bf16[8,4,64,128]{3,2,1,0:T(8,128)(2,1)} %pad_maximum_fusion), calls=%async_computation | async-start | bytes 1048576 | tf_op jit(solution)/shard_map/all_to_all | solution.py:174
  27.6 2.8 %collective-permute-start.4 = (bf16[8,16,768]{2,1,0:T(8,128)(2,1)S(1)}, bf16[8,16,768]{2,1,0:T(8,128)(2,1)S(1)}, u32[]{:S(2)}, u32[]{:S(2)}) collective-permute-start(bf16[8,16,768]{2,1,0:T(8,128)(2,1)S(1)} %all-to-all-done.1.refs_0_), channel_id=1, source_target_pairs={{0,6},{2,0},{4,2},{6,4},{1,7},{3,1},{5,3},{7,5},{8,14},{10,8},{12,... | collective-permute-start | bytes 589832 | tf_op jit(solution)/shard_map/ppermute | solution.py:147
  30.4 3.2 %collective-permute-done.4.refs_2_ = bf16[8,16,768]{2,1,0:T(8,128)(2,1)S(1)} collective-permute-done((bf16[8,16,768]{2,1,0:T(8,128)(2,1)S(1)}, bf16[8,16,768]{2,1,0:T(8,128)(2,1)S(1)}, u32[]{:S(2)}, u32[]{:S(2)}) %collective-permute-start.4) | collective-permute-done | bytes 196640 | tf_op jit(solution)/shard_map/ppermute | solution.py:147
  33.6 3.8 %collective-permute-start.6 = (bf16[4,16,768]{2,1,0:T(8,128)(2,1)S(1)}, bf16[4,16,768]{2,1,0:T(8,128)(2,1)S(1)}, u32[]{:S(2)}, u32[]{:S(2)}) collective-permute-start(bf16[4,16,768]{2,1,0:T(8,128)(2,1)S(1)} %slice.33), channel_id=1, source_target_pairs={{0,6},{2,0},{4,2},{6,4},{1,7},{3,1},{5,3},{7,5},{8,14},{10,8},{12,... | collective-permute-start | bytes 294920 | tf_op jit(solution)/shard_map/ppermute | solution.py:147
  38.1 1.5 %collective-permute-done.6.refs_4_ = bf16[4,16,768]{2,1,0:T(8,128)(2,1)S(1)} collective-permute-done((bf16[4,16,768]{2,1,0:T(8,128)(2,1)S(1)}, bf16[4,16,768]{2,1,0:T(8,128)(2,1)S(1)}, u32[]{:S(2)}, u32[]{:S(2)}) %collective-permute-start.6) | collective-permute-done | bytes 98336 | tf_op jit(solution)/shard_map/ppermute | solution.py:147
  39.6 3.7 %collective-permute-done.5.refs_3_ = bf16[4,16,768]{2,1,0:T(8,128)(2,1)S(1)} collective-permute-done((bf16[4,16,768]{2,1,0:T(8,128)(2,1)S(1)}, bf16[4,16,768]{2,1,0:T(8,128)(2,1)S(1)}, u32[]{:S(2)}, u32[]{:S(2)}) %collective-permute-start.5) | collective-permute-done | bytes 98336 | tf_op jit(solution)/shard_map/ppermute | solution.py:147
  43.3 1.3 %collective-permute-done.10.refs_8_ = bf16[4,16,768]{2,1,0:T(8,128)(2,1)S(1)} collective-permute-done((bf16[4,16,768]{2,1,0:T(8,128)(2,1)S(1)}, bf16[4,16,768]{2,1,0:T(8,128)(2,1)S(1)}, u32[]{:S(2)}, u32[]{:S(2)}) %collective-permute-start.10) | collective-permute-done | bytes 98336 | tf_op jit(solution)/shard_map/ppermute | solution.py:147
  44.6 0.7 grad.1.grad_ref
  45.3 0.9 collective-permute-start.12
  46.2 2.4 %collective-permute-start.13 = (bf16[256,768]{1,0:T(8,128)(2,1)S(1)}, bf16[256,768]{1,0:T(8,128)(2,1)S(1)}, u32[]{:S(2)}, u32[]{:S(2)}) collective-permute-start(bf16[256,768]{1,0:T(8,128)(2,1)S(1)} %grad.1.grad_ref), channel_id=1, source_target_pairs={{0,6},{2,0},{4,2},{6,4},{1,7},{3,1},{5,3},{7,5},{8,14},{10,8},{12,... | collective-permute-start | bytes 1179656 | tf_op jit(solution)/shard_map/ppermute | solution.py:147
  48.6 9.1 %collective-permute-done.12 = bf16[256,768]{1,0:T(8,128)(2,1)S(1)} collective-permute-done((bf16[256,768]{1,0:T(8,128)(2,1)S(1)}, bf16[256,768]{1,0:T(8,128)(2,1)S(1)}, u32[]{:S(2)}, u32[]{:S(2)}) %collective-permute-start.12) | collective-permute-done | bytes 393248 | tf_op jit(solution)/shard_map/ppermute | solution.py:147
  57.7 0.5 fusion
  58.3 0.5 fusion.1
  58.8 0.5 add_add_fusion.1
  59.6 2.5 %collective-permute-start.15 = (bf16[128,768]{1,0:T(8,128)(2,1)S(1)}, bf16[128,768]{1,0:T(8,128)(2,1)S(1)}, u32[]{:S(2)}, u32[]{:S(2)}) collective-permute-start(bf16[128,768]{1,0:T(8,128)(2,1)S(1)} %slice.35), channel_id=1, source_target_pairs={{0,6},{2,0},{4,2},{6,4},{1,7},{3,1},{5,3},{7,5},{8,14},{10,8},{12,... | collective-permute-start | bytes 589832 | tf_op jit(solution)/shard_map/ppermute | solution.py:147
  62.2 4.8 %collective-permute-done.15 = bf16[128,768]{1,0:T(8,128)(2,1)S(1)} collective-permute-done((bf16[128,768]{1,0:T(8,128)(2,1)S(1)}, bf16[128,768]{1,0:T(8,128)(2,1)S(1)}, u32[]{:S(2)}, u32[]{:S(2)}) %collective-permute-start.15) | collective-permute-done | bytes 196640 | tf_op jit(solution)/shard_map/ppermute | solution.py:147
  67.0 3.5 %collective-permute-done.14 = bf16[128,768]{1,0:T(8,128)(2,1)S(1)} collective-permute-done((bf16[128,768]{1,0:T(8,128)(2,1)S(1)}, bf16[128,768]{1,0:T(8,128)(2,1)S(1)}, u32[]{:S(2)}, u32[]{:S(2)}) %collective-permute-start.14) | collective-permute-done | bytes 196640 | tf_op jit(solution)/shard_map/ppermute | solution.py:147
  71.0 0.5 add_add_fusion.mine_ref
  71.9 5.6 %newton.1 = (bf16[1,64,768]{2,1,0:T(8,128)(2,1)S(1)}, bf16[1,64,768]{2,1,0:T(8,128)(2,1)S(1)}, bf16[1,64,768]{2,1,0:T(8,128)(2,1)S(1)}, bf16[1,64,768]{2,1,0:T(8,128)(2,1)S(1)}) custom-call(f32[768,768]{1,0:T(8,128)S(1)} %add_add_fusion.mine_ref, f32[768,768]{1,0:T(8,128)S(1)} %collective-permute-done.16.other_ref, ...), custom_call_target="tpu_custom_call" | custom-call | tf_op jit(solution)/shard_map/newton/pallas_call | solution.py:205
  77.5 1.4 %collective-permute-start.19 = (bf16[1,64,768]{2,1,0:T(8,128)(2,1)S(1)}, bf16[1,64,768]{2,1,0:T(8,128)(2,1)S(1)}, u32[]{:S(2)}, u32[]{:S(2)}) collective-permute-start(bf16[1,64,768]{2,1,0:T(8,128)(2,1)S(1)} %get-tuple-element.19), channel_id=1, source_target_pairs={{0,8},{8,16},{16,24},{24,0},{1,9},{9,17},{17,25},{25,1},{2,10},{10... | collective-permute-start | bytes 294920 | tf_op jit(solution)/shard_map/ppermute | solution.py:147
  78.9 0.9 collective-permute-start.20
  79.7 0.9 collective-permute-start.29
  80.6 6.4 %collective-permute-done.29 = bf16[1,64,768]{2,1,0:T(8,128)(2,1)S(1)} collective-permute-done((bf16[1,64,768]{2,1,0:T(8,128)(2,1)S(1)}, bf16[1,64,768]{2,1,0:T(8,128)(2,1)S(1)}, u32[]{:S(2)}, u32[]{:S(2)}) %collective-permute-start.29) | collective-permute-done | bytes 98336 | tf_op jit(solution)/shard_map/ppermute | solution.py:147
  87.1 3.3 %collective-permute-start.34 = (bf16[2,64,768]{2,1,0:T(8,128)(2,1)S(1)}, bf16[2,64,768]{2,1,0:T(8,128)(2,1)S(1)}, u32[]{:S(2)}, u32[]{:S(2)}) collective-permute-start(bf16[2,64,768]{2,1,0:T(8,128)(2,1)S(1)} %constant_dynamic-update-slice_fusion.2.refs_0_), channel_id=1, source_target_pairs={{0,224},{32,0},{64,32},{96,64},{128,96},{160,128},{192,160},{224,1... | collective-permute-start | bytes 589832 | tf_op jit(solution)/shard_map/ppermute | solution.py:147
  90.4 3.5 %collective-permute-start.25 = (bf16[2,64,768]{2,1,0:T(8,128)(2,1)S(1)}, bf16[2,64,768]{2,1,0:T(8,128)(2,1)S(1)}, u32[]{:S(2)}, u32[]{:S(2)}) collective-permute-start(bf16[2,64,768]{2,1,0:T(8,128)(2,1)S(1)} %constant_dynamic-update-slice_fusion.refs_5_), channel_id=1, source_target_pairs={{0,224},{32,0},{64,32},{96,64},{128,96},{160,128},{192,160},{224,1... | collective-permute-start | bytes 589832 | tf_op jit(solution)/shard_map/ppermute | solution.py:147
  93.9 1.7 %collective-permute-done.34.refs_2_ = bf16[2,64,768]{2,1,0:T(8,128)(2,1)S(1)} collective-permute-done((bf16[2,64,768]{2,1,0:T(8,128)(2,1)S(1)}, bf16[2,64,768]{2,1,0:T(8,128)(2,1)S(1)}, u32[]{:S(2)}, u32[]{:S(2)}) %collective-permute-start.34) | collective-permute-done | bytes 196640 | tf_op jit(solution)/shard_map/ppermute | solution.py:147
  95.7 3.7 %collective-permute-start.35 = (bf16[2,64,768]{2,1,0:T(8,128)(2,1)S(1)}, bf16[2,64,768]{2,1,0:T(8,128)(2,1)S(1)}, u32[]{:S(2)}, u32[]{:S(2)}) collective-permute-start(bf16[2,64,768]{2,1,0:T(8,128)(2,1)S(1)} %collective-permute-done.34.refs_2_), channel_id=1, source_target_pairs={{0,224},{32,0},{64,32},{96,64},{128,96},{160,128},{192,160},{224,1... | collective-permute-start | bytes 589832 | tf_op jit(solution)/shard_map/ppermute | solution.py:147
  99.3 0.5 collective-permute-done.25.refs_7_
  99.9 3.7 %collective-permute-start.26 = (bf16[2,64,768]{2,1,0:T(8,128)(2,1)S(1)}, bf16[2,64,768]{2,1,0:T(8,128)(2,1)S(1)}, u32[]{:S(2)}, u32[]{:S(2)}) collective-permute-start(bf16[2,64,768]{2,1,0:T(8,128)(2,1)S(1)} %collective-permute-done.25.refs_7_), channel_id=1, source_target_pairs={{0,224},{32,0},{64,32},{96,64},{128,96},{160,128},{192,160},{224,1... | collective-permute-start | bytes 589832 | tf_op jit(solution)/shard_map/ppermute | solution.py:147
  103.6 0.8 collective-permute-done.35.refs_4_
  104.4 3.7 %collective-permute-start.36 = (bf16[2,64,768]{2,1,0:T(8,128)(2,1)S(1)}, bf16[2,64,768]{2,1,0:T(8,128)(2,1)S(1)}, u32[]{:S(2)}, u32[]{:S(2)}) collective-permute-start(bf16[2,64,768]{2,1,0:T(8,128)(2,1)S(1)} %collective-permute-done.35.refs_4_), channel_id=1, source_target_pairs={{0,224},{32,0},{64,32},{96,64},{128,96},{160,128},{192,160},{224,1... | collective-permute-start | bytes 589832 | tf_op jit(solution)/shard_map/ppermute | solution.py:147
  108.1 0.8 collective-permute-done.26.refs_3_
  108.8 3.7 %collective-permute-start.27 = (bf16[2,64,768]{2,1,0:T(8,128)(2,1)S(1)}, bf16[2,64,768]{2,1,0:T(8,128)(2,1)S(1)}, u32[]{:S(2)}, u32[]{:S(2)}) collective-permute-start(bf16[2,64,768]{2,1,0:T(8,128)(2,1)S(1)} %collective-permute-done.26.refs_3_), channel_id=1, source_target_pairs={{0,224},{32,0},{64,32},{96,64},{128,96},{160,128},{192,160},{224,1... | collective-permute-start | bytes 589832 | tf_op jit(solution)/shard_map/ppermute | solution.py:147
  112.5 0.8 collective-permute-done.36.refs_1_
  113.4 3.8 %collective-permute-start.37 = (bf16[2,32,768]{2,1,0:T(8,128)(2,1)S(1)}, bf16[2,32,768]{2,1,0:T(8,128)(2,1)S(1)}, u32[]{:S(2)}, u32[]{:S(2)}) collective-permute-start(bf16[2,32,768]{2,1,0:T(8,128)(2,1)S(1)} %slice.39), channel_id=1, source_target_pairs={{0,224},{32,0},{64,32},{96,64},{128,96},{160,128},{192,160},{224,1... | collective-permute-start | bytes 294920 | tf_op jit(solution)/shard_map/ppermute | solution.py:147
  117.3 3.3 %collective-permute-start.28 = (bf16[2,32,768]{2,1,0:T(8,128)(2,1)S(1)}, bf16[2,32,768]{2,1,0:T(8,128)(2,1)S(1)}, u32[]{:S(2)}, u32[]{:S(2)}) collective-permute-start(bf16[2,32,768]{2,1,0:T(8,128)(2,1)S(1)} %slice.37), channel_id=1, source_target_pairs={{0,224},{32,0},{64,32},{96,64},{128,96},{160,128},{192,160},{224,1... | collective-permute-start | bytes 294920 | tf_op jit(solution)/shard_map/ppermute | solution.py:147
  120.7 1.3 %shard_map.37.refs_4_ = bf16[4,8,64,768]{3,2,1,0:T(8,128)(2,1)} custom-call(bf16[2,64,768]{2,1,0:T(8,128)(2,1)S(1)} %constant_dynamic-update-slice_fusion.2.refs_0_, bf16[2,64,768]{2,1,0:T(8,128)(2,1)S(1)} %collective-permute-done.30.refs_1_, bf16[2,64,768]{2,1,0:T(8,128)(2,1)S(1)} %collective-permute-done.34.refs_2_, ...), custom_call_target="tpu_custom_call" | custom-call | tf_op jit(solution)/shard_map/pallas_call | solution.py:135
  122.0 1.0 shard_map.38.refs_4_
  123.1 0.9 shard_map.39.refs_2_
  123.9 2.5 %collective-permute-done.24.refs_0_ = bf16[2,32,768]{2,1,0:T(8,128)(2,1)S(1)} collective-permute-done((bf16[2,32,768]{2,1,0:T(8,128)(2,1)S(1)}, bf16[2,32,768]{2,1,0:T(8,128)(2,1)S(1)}, u32[]{:S(2)}, u32[]{:S(2)}) %collective-permute-start.24) | collective-permute-done | bytes 98336 | tf_op jit(solution)/shard_map/ppermute | solution.py:147
  126.5 0.7 shard_map.40
  (57 shorter events, 3.0 us)
Async XLA Ops:
  1.9 18.9 %all-to-all-start.1 = ((bf16[8,16,768]{2,1,0:T(8,128)(2,1)}), bf16[8,16,768]{2,1,0:T(8,128)(2,1)S(1)}, u32[]{:S(2)}, u32[]{:S(2)}) async-start(bf16[8,16,768]{2,1,0:T(8,128)(2,1)} %get-tuple-element.18), calls=%async_computation.1 | async-start | bytes 393216 | tf_op jit(solution)/shard_map/all_to_all | solution.py:173
  10.4 5.9 %collective-permute-start = (bf16[8,64,128]{2,1,0:T(8,128)(2,1)S(1)}, bf16[8,64,128]{2,1,0:T(8,128)(2,1)S(1)}, u32[]{:S(2)}, u32[]{:S(2)}) collective-permute-start(bf16[8,64,128]{2,1,0:T(8,128)(2,1)S(1)} %get-tuple-element.15), channel_id=1, source_target_pairs={{0,8},{8,16},{16,24},{24,0},{1,9},{9,17},{17,25},{25,1},{2,10},{10... | collective-permute-start | bytes 393224 | tf_op jit(solution)/shard_map/ppermute | solution.py:147
  10.6 9.0 %collective-permute-start.1 = (bf16[8,64,128]{2,1,0:T(8,128)(2,1)S(1)}, bf16[8,64,128]{2,1,0:T(8,128)(2,1)S(1)}, u32[]{:S(2)}, u32[]{:S(2)}) collective-permute-start(bf16[8,64,128]{2,1,0:T(8,128)(2,1)S(1)} %get-tuple-element.16), channel_id=1, source_target_pairs={{0,24},{8,0},{16,8},{24,16},{1,25},{9,1},{17,9},{25,17},{2,26},{10... | collective-permute-start | bytes 393224 | tf_op jit(solution)/shard_map/ppermute | solution.py:147
  12.4 7.2 %collective-permute-start.2 = (bf16[8,64,128]{2,1,0:T(8,128)(2,1)S(1)}, bf16[8,64,128]{2,1,0:T(8,128)(2,1)S(1)}, u32[]{:S(2)}, u32[]{:S(2)}) collective-permute-start(bf16[8,64,128]{2,1,0:T(8,128)(2,1)S(1)} %get-tuple-element.17), channel_id=1, source_target_pairs={{0,16},{8,24},{16,0},{24,8},{1,17},{9,25},{17,1},{25,9},{2,18},{10... | collective-permute-start | bytes 393224 | tf_op jit(solution)/shard_map/ppermute | solution.py:147
  20.9 23.7 %all-to-all-start = ((bf16[8,4,64,128]{3,2,1,0:T(8,128)(2,1)}), bf16[8,4,64,128]{3,2,1,0:T(8,128)(2,1)S(1)}, u32[]{:S(2)}, u32[]{:S(2)}) async-start(bf16[8,4,64,128]{3,2,1,0:T(8,128)(2,1)} %pad_maximum_fusion), calls=%async_computation | async-start | bytes 1048576 | tf_op jit(solution)/shard_map/all_to_all | solution.py:174
  27.6 6.0 %collective-permute-start.4 = (bf16[8,16,768]{2,1,0:T(8,128)(2,1)S(1)}, bf16[8,16,768]{2,1,0:T(8,128)(2,1)S(1)}, u32[]{:S(2)}, u32[]{:S(2)}) collective-permute-start(bf16[8,16,768]{2,1,0:T(8,128)(2,1)S(1)} %all-to-all-done.1.refs_0_), channel_id=1, source_target_pairs={{0,6},{2,0},{4,2},{6,4},{1,7},{3,1},{5,3},{7,5},{8,14},{10,8},{12,... | collective-permute-start | bytes 589832 | tf_op jit(solution)/shard_map/ppermute | solution.py:147
  30.4 7.0 %collective-permute-start.3 = (bf16[8,16,768]{2,1,0:T(8,128)(2,1)S(1)}, bf16[8,16,768]{2,1,0:T(8,128)(2,1)S(1)}, u32[]{:S(2)}, u32[]{:S(2)}) collective-permute-start(bf16[8,16,768]{2,1,0:T(8,128)(2,1)S(1)} %all-to-all-done.1.refs_0_), channel_id=1, source_target_pairs={{0,2},{2,4},{4,6},{6,0},{1,3},{3,5},{5,7},{7,1},{8,10},{10,12},{12... | collective-permute-start | bytes 589832 | tf_op jit(solution)/shard_map/ppermute | solution.py:147
  30.4 12.9 %collective-permute-start.7 = (bf16[8,16,768]{2,1,0:T(8,128)(2,1)S(1)}, bf16[8,16,768]{2,1,0:T(8,128)(2,1)S(1)}, u32[]{:S(2)}, u32[]{:S(2)}) collective-permute-start(bf16[8,16,768]{2,1,0:T(8,128)(2,1)S(1)} %all-to-all-done.1.refs_0_), channel_id=1, source_target_pairs={{0,1},{1,0},{2,3},{3,2},{4,5},{5,4},{6,7},{7,6},{8,9},{9,8},{10,11... | collective-permute-start | bytes 589832 | tf_op jit(solution)/shard_map/ppermute | solution.py:147
  33.6 6.0 %collective-permute-start.6 = (bf16[4,16,768]{2,1,0:T(8,128)(2,1)S(1)}, bf16[4,16,768]{2,1,0:T(8,128)(2,1)S(1)}, u32[]{:S(2)}, u32[]{:S(2)}) collective-permute-start(bf16[4,16,768]{2,1,0:T(8,128)(2,1)S(1)} %slice.33), channel_id=1, source_target_pairs={{0,6},{2,0},{4,2},{6,4},{1,7},{3,1},{5,3},{7,5},{8,14},{10,8},{12,... | collective-permute-start | bytes 294920 | tf_op jit(solution)/shard_map/ppermute | solution.py:147
  37.4 5.9 %collective-permute-start.5 = (bf16[4,16,768]{2,1,0:T(8,128)(2,1)S(1)}, bf16[4,16,768]{2,1,0:T(8,128)(2,1)S(1)}, u32[]{:S(2)}, u32[]{:S(2)}) collective-permute-start(bf16[4,16,768]{2,1,0:T(8,128)(2,1)S(1)} %slice.32), channel_id=1, source_target_pairs={{0,2},{2,4},{4,6},{6,0},{1,3},{3,5},{5,7},{7,1},{8,10},{10,12},{12... | collective-permute-start | bytes 294920 | tf_op jit(solution)/shard_map/ppermute | solution.py:147
  37.5 5.8 %collective-permute-start.9 = (bf16[8,16,768]{2,1,0:T(8,128)(2,1)S(1)}, bf16[8,16,768]{2,1,0:T(8,128)(2,1)S(1)}, u32[]{:S(2)}, u32[]{:S(2)}) collective-permute-start(bf16[8,16,768]{2,1,0:T(8,128)(2,1)S(1)} %collective-permute-done.4.refs_2_), channel_id=1, source_target_pairs={{0,1},{1,0},{2,3},{3,2},{4,5},{5,4},{6,7},{7,6},{8,9},{9,8},{10,11... | collective-permute-start | bytes 589832 | tf_op jit(solution)/shard_map/ppermute | solution.py:147
  37.6 7.0 %collective-permute-start.8 = (bf16[8,16,768]{2,1,0:T(8,128)(2,1)S(1)}, bf16[8,16,768]{2,1,0:T(8,128)(2,1)S(1)}, u32[]{:S(2)}, u32[]{:S(2)}) collective-permute-start(bf16[8,16,768]{2,1,0:T(8,128)(2,1)S(1)} %collective-permute-done.3.refs_1_), channel_id=1, source_target_pairs={{0,1},{1,0},{2,3},{3,2},{4,5},{5,4},{6,7},{7,6},{8,9},{9,8},{10,11... | collective-permute-start | bytes 589832 | tf_op jit(solution)/shard_map/ppermute | solution.py:147
  39.6 3.7 %collective-permute-start.11 = (bf16[4,16,768]{2,1,0:T(8,128)(2,1)S(1)}, bf16[4,16,768]{2,1,0:T(8,128)(2,1)S(1)}, u32[]{:S(2)}, u32[]{:S(2)}) collective-permute-start(bf16[4,16,768]{2,1,0:T(8,128)(2,1)S(1)} %collective-permute-done.6.refs_4_), channel_id=1, source_target_pairs={{0,1},{1,0},{2,3},{3,2},{4,5},{5,4},{6,7},{7,6},{8,9},{9,8},{10,11... | collective-permute-start | bytes 294920 | tf_op jit(solution)/shard_map/ppermute | solution.py:147
  43.3 1.3 %collective-permute-start.10 = (bf16[4,16,768]{2,1,0:T(8,128)(2,1)S(1)}, bf16[4,16,768]{2,1,0:T(8,128)(2,1)S(1)}, u32[]{:S(2)}, u32[]{:S(2)}) collective-permute-start(bf16[4,16,768]{2,1,0:T(8,128)(2,1)S(1)} %collective-permute-done.5.refs_3_), channel_id=1, source_target_pairs={{0,1},{1,0},{2,3},{3,2},{4,5},{5,4},{6,7},{7,6},{8,9},{9,8},{10,11... | collective-permute-start | bytes 294920 | tf_op jit(solution)/shard_map/ppermute | solution.py:147
  45.3 12.5 %collective-permute-start.12 = (bf16[256,768]{1,0:T(8,128)(2,1)S(1)}, bf16[256,768]{1,0:T(8,128)(2,1)S(1)}, u32[]{:S(2)}, u32[]{:S(2)}) collective-permute-start(bf16[256,768]{1,0:T(8,128)(2,1)S(1)} %grad.1.grad_ref), channel_id=1, source_target_pairs={{0,2},{2,4},{4,6},{6,0},{1,3},{3,5},{5,7},{7,1},{8,10},{10,12},{12... | collective-permute-start | bytes 1179656 | tf_op jit(solution)/shard_map/ppermute | solution.py:147
  46.2 12.1 %collective-permute-start.13 = (bf16[256,768]{1,0:T(8,128)(2,1)S(1)}, bf16[256,768]{1,0:T(8,128)(2,1)S(1)}, u32[]{:S(2)}, u32[]{:S(2)}) collective-permute-start(bf16[256,768]{1,0:T(8,128)(2,1)S(1)} %grad.1.grad_ref), channel_id=1, source_target_pairs={{0,6},{2,0},{4,2},{6,4},{1,7},{3,1},{5,3},{7,5},{8,14},{10,8},{12,... | collective-permute-start | bytes 1179656 | tf_op jit(solution)/shard_map/ppermute | solution.py:147
  59.3 12.6 %collective-permute-start.16 = (f32[768,768]{1,0:T(8,128)S(1)}, f32[768,768]{1,0:T(8,128)S(1)}, u32[]{:S(2)}, u32[]{:S(2)}) collective-permute-start(f32[768,768]{1,0:T(8,128)S(1)} %add_add_fusion.1), channel_id=1, source_target_pairs={{0,1},{1,0},{2,3},{3,2},{4,5},{5,4},{6,7},{7,6},{8,9},{9,8},{10,11... | collective-permute-start | bytes 7077896 | tf_op jit(solution)/shard_map/ppermute | solution.py:147
  59.6 7.4 %collective-permute-start.15 = (bf16[128,768]{1,0:T(8,128)(2,1)S(1)}, bf16[128,768]{1,0:T(8,128)(2,1)S(1)}, u32[]{:S(2)}, u32[]{:S(2)}) collective-permute-start(bf16[128,768]{1,0:T(8,128)(2,1)S(1)} %slice.35), channel_id=1, source_target_pairs={{0,6},{2,0},{4,2},{6,4},{1,7},{3,1},{5,3},{7,5},{8,14},{10,8},{12,... | collective-permute-start | bytes 589832 | tf_op jit(solution)/shard_map/ppermute | solution.py:147
  62.1 8.3 %collective-permute-start.14 = (bf16[128,768]{1,0:T(8,128)(2,1)S(1)}, bf16[128,768]{1,0:T(8,128)(2,1)S(1)}, u32[]{:S(2)}, u32[]{:S(2)}) collective-permute-start(bf16[128,768]{1,0:T(8,128)(2,1)S(1)} %slice.34), channel_id=1, source_target_pairs={{0,2},{2,4},{4,6},{6,0},{1,3},{3,5},{5,7},{7,1},{8,10},{10,12},{12... | collective-permute-start | bytes 589832 | tf_op jit(solution)/shard_map/ppermute | solution.py:147
  67.0 4.5 %collective-permute-start.18 = (bf16[128,768]{1,0:T(8,128)(2,1)S(1)}, bf16[128,768]{1,0:T(8,128)(2,1)S(1)}, u32[]{:S(2)}, u32[]{:S(2)}) collective-permute-start(bf16[128,768]{1,0:T(8,128)(2,1)S(1)} %collective-permute-done.15), channel_id=1, source_target_pairs={{0,1},{1,0},{2,3},{3,2},{4,5},{5,4},{6,7},{7,6},{8,9},{9,8},{10,11... | collective-permute-start | bytes 589832 | tf_op jit(solution)/shard_map/ppermute | solution.py:147
  70.5 1.4 %collective-permute-start.17 = (bf16[128,768]{1,0:T(8,128)(2,1)S(1)}, bf16[128,768]{1,0:T(8,128)(2,1)S(1)}, u32[]{:S(2)}, u32[]{:S(2)}) collective-permute-start(bf16[128,768]{1,0:T(8,128)(2,1)S(1)} %collective-permute-done.14), channel_id=1, source_target_pairs={{0,1},{1,0},{2,3},{3,2},{4,5},{5,4},{6,7},{7,6},{8,9},{9,8},{10,11... | collective-permute-start | bytes 589832 | tf_op jit(solution)/shard_map/ppermute | solution.py:147
  77.5 12.9 %collective-permute-start.19 = (bf16[1,64,768]{2,1,0:T(8,128)(2,1)S(1)}, bf16[1,64,768]{2,1,0:T(8,128)(2,1)S(1)}, u32[]{:S(2)}, u32[]{:S(2)}) collective-permute-start(bf16[1,64,768]{2,1,0:T(8,128)(2,1)S(1)} %get-tuple-element.19), channel_id=1, source_target_pairs={{0,8},{8,16},{16,24},{24,0},{1,9},{9,17},{17,25},{25,1},{2,10},{10... | collective-permute-start | bytes 294920 | tf_op jit(solution)/shard_map/ppermute | solution.py:147
  78.9 11.5 %collective-permute-start.20 = (bf16[1,64,768]{2,1,0:T(8,128)(2,1)S(1)}, bf16[1,64,768]{2,1,0:T(8,128)(2,1)S(1)}, u32[]{:S(2)}, u32[]{:S(2)}) collective-permute-start(bf16[1,64,768]{2,1,0:T(8,128)(2,1)S(1)} %get-tuple-element.20), channel_id=1, source_target_pairs={{0,16},{8,24},{16,0},{24,8},{1,17},{9,25},{17,1},{25,9},{2,18},{10... | collective-permute-start | bytes 294920 | tf_op jit(solution)/shard_map/ppermute | solution.py:147
  79.7 7.3 %collective-permute-start.29 = (bf16[1,64,768]{2,1,0:T(8,128)(2,1)S(1)}, bf16[1,64,768]{2,1,0:T(8,128)(2,1)S(1)}, u32[]{:S(2)}, u32[]{:S(2)}) collective-permute-start(bf16[1,64,768]{2,1,0:T(8,128)(2,1)S(1)} %get-tuple-element.22), channel_id=1, source_target_pairs={{0,24},{8,0},{16,8},{24,16},{1,25},{9,1},{17,9},{25,17},{2,26},{10... | collective-permute-start | bytes 294920 | tf_op jit(solution)/shard_map/ppermute | solution.py:147
  87.1 8.6 %collective-permute-start.34 = (bf16[2,64,768]{2,1,0:T(8,128)(2,1)S(1)}, bf16[2,64,768]{2,1,0:T(8,128)(2,1)S(1)}, u32[]{:S(2)}, u32[]{:S(2)}) collective-permute-start(bf16[2,64,768]{2,1,0:T(8,128)(2,1)S(1)} %constant_dynamic-update-slice_fusion.2.refs_0_), channel_id=1, source_target_pairs={{0,224},{32,0},{64,32},{96,64},{128,96},{160,128},{192,160},{224,1... | collective-permute-start | bytes 589832 | tf_op jit(solution)/shard_map/ppermute | solution.py:147
  90.4 9.0 %collective-permute-start.30 = (bf16[2,64,768]{2,1,0:T(8,128)(2,1)S(1)}, bf16[2,64,768]{2,1,0:T(8,128)(2,1)S(1)}, u32[]{:S(2)}, u32[]{:S(2)}) collective-permute-start(bf16[2,64,768]{2,1,0:T(8,128)(2,1)S(1)} %constant_dynamic-update-slice_fusion.2.refs_0_), channel_id=1, source_target_pairs={{0,32},{32,64},{64,96},{96,128},{128,160},{160,192},{192,224},{224... | collective-permute-start | bytes 589832 | tf_op jit(solution)/shard_map/ppermute | solution.py:147
  90.4 9.5 %collective-permute-start.25 = (bf16[2,64,768]{2,1,0:T(8,128)(2,1)S(1)}, bf16[2,64,768]{2,1,0:T(8,128)(2,1)S(1)}, u32[]{:S(2)}, u32[]{:S(2)}) collective-permute-start(bf16[2,64,768]{2,1,0:T(8,128)(2,1)S(1)} %constant_dynamic-update-slice_fusion.refs_5_), channel_id=1, source_target_pairs={{0,224},{32,0},{64,32},{96,64},{128,96},{160,128},{192,160},{224,1... | collective-permute-start | bytes 589832 | tf_op jit(solution)/shard_map/ppermute | solution.py:147
  93.9 9.6 %collective-permute-start.21 = (bf16[2,64,768]{2,1,0:T(8,128)(2,1)S(1)}, bf16[2,64,768]{2,1,0:T(8,128)(2,1)S(1)}, u32[]{:S(2)}, u32[]{:S(2)}) collective-permute-start(bf16[2,64,768]{2,1,0:T(8,128)(2,1)S(1)} %constant_dynamic-update-slice_fusion.refs_5_), channel_id=1, source_target_pairs={{0,32},{32,64},{64,96},{96,128},{128,160},{160,192},{192,224},{224... | collective-permute-start | bytes 589832 | tf_op jit(solution)/shard_map/ppermute | solution.py:147
  95.7 8.7 %collective-permute-start.35 = (bf16[2,64,768]{2,1,0:T(8,128)(2,1)S(1)}, bf16[2,64,768]{2,1,0:T(8,128)(2,1)S(1)}, u32[]{:S(2)}, u32[]{:S(2)}) collective-permute-start(bf16[2,64,768]{2,1,0:T(8,128)(2,1)S(1)} %collective-permute-done.34.refs_2_), channel_id=1, source_target_pairs={{0,224},{32,0},{64,32},{96,64},{128,96},{160,128},{192,160},{224,1... | collective-permute-start | bytes 589832 | tf_op jit(solution)/shard_map/ppermute | solution.py:147
  99.3 8.7 %collective-permute-start.31 = (bf16[2,64,768]{2,1,0:T(8,128)(2,1)S(1)}, bf16[2,64,768]{2,1,0:T(8,128)(2,1)S(1)}, u32[]{:S(2)}, u32[]{:S(2)}) collective-permute-start(bf16[2,64,768]{2,1,0:T(8,128)(2,1)S(1)} %collective-permute-done.30.refs_1_), channel_id=1, source_target_pairs={{0,32},{32,64},{64,96},{96,128},{128,160},{160,192},{192,224},{224... | collective-permute-start | bytes 589832 | tf_op jit(solution)/shard_map/ppermute | solution.py:147
  99.9 9.0 %collective-permute-start.26 = (bf16[2,64,768]{2,1,0:T(8,128)(2,1)S(1)}, bf16[2,64,768]{2,1,0:T(8,128)(2,1)S(1)}, u32[]{:S(2)}, u32[]{:S(2)}) collective-permute-start(bf16[2,64,768]{2,1,0:T(8,128)(2,1)S(1)} %collective-permute-done.25.refs_7_), channel_id=1, source_target_pairs={{0,224},{32,0},{64,32},{96,64},{128,96},{160,128},{192,160},{224,1... | collective-permute-start | bytes 589832 | tf_op jit(solution)/shard_map/ppermute | solution.py:147
  103.6 9.0 %collective-permute-start.22 = (bf16[2,64,768]{2,1,0:T(8,128)(2,1)S(1)}, bf16[2,64,768]{2,1,0:T(8,128)(2,1)S(1)}, u32[]{:S(2)}, u32[]{:S(2)}) collective-permute-start(bf16[2,64,768]{2,1,0:T(8,128)(2,1)S(1)} %collective-permute-done.21.refs_6_), channel_id=1, source_target_pairs={{0,32},{32,64},{64,96},{96,128},{128,160},{160,192},{192,224},{224... | collective-permute-start | bytes 589832 | tf_op jit(solution)/shard_map/ppermute | solution.py:147
  104.4 9.0 %collective-permute-start.36 = (bf16[2,64,768]{2,1,0:T(8,128)(2,1)S(1)}, bf16[2,64,768]{2,1,0:T(8,128)(2,1)S(1)}, u32[]{:S(2)}, u32[]{:S(2)}) collective-permute-start(bf16[2,64,768]{2,1,0:T(8,128)(2,1)S(1)} %collective-permute-done.35.refs_4_), channel_id=1, source_target_pairs={{0,224},{32,0},{64,32},{96,64},{128,96},{160,128},{192,160},{224,1... | collective-permute-start | bytes 589832 | tf_op jit(solution)/shard_map/ppermute | solution.py:147
  108.1 9.1 %collective-permute-start.32 = (bf16[2,64,768]{2,1,0:T(8,128)(2,1)S(1)}, bf16[2,64,768]{2,1,0:T(8,128)(2,1)S(1)}, u32[]{:S(2)}, u32[]{:S(2)}) collective-permute-start(bf16[2,64,768]{2,1,0:T(8,128)(2,1)S(1)} %collective-permute-done.31.refs_3_), channel_id=1, source_target_pairs={{0,32},{32,64},{64,96},{96,128},{128,160},{160,192},{192,224},{224... | collective-permute-start | bytes 589832 | tf_op jit(solution)/shard_map/ppermute | solution.py:147
  108.8 8.4 %collective-permute-start.27 = (bf16[2,64,768]{2,1,0:T(8,128)(2,1)S(1)}, bf16[2,64,768]{2,1,0:T(8,128)(2,1)S(1)}, u32[]{:S(2)}, u32[]{:S(2)}) collective-permute-start(bf16[2,64,768]{2,1,0:T(8,128)(2,1)S(1)} %collective-permute-done.26.refs_3_), channel_id=1, source_target_pairs={{0,224},{32,0},{64,32},{96,64},{128,96},{160,128},{192,160},{224,1... | collective-permute-start | bytes 589832 | tf_op jit(solution)/shard_map/ppermute | solution.py:147
  112.5 8.0 %collective-permute-start.23 = (bf16[2,64,768]{2,1,0:T(8,128)(2,1)S(1)}, bf16[2,64,768]{2,1,0:T(8,128)(2,1)S(1)}, u32[]{:S(2)}, u32[]{:S(2)}) collective-permute-start(bf16[2,64,768]{2,1,0:T(8,128)(2,1)S(1)} %collective-permute-done.22.refs_2_), channel_id=1, source_target_pairs={{0,32},{32,64},{64,96},{96,128},{128,160},{160,192},{192,224},{224... | collective-permute-start | bytes 589832 | tf_op jit(solution)/shard_map/ppermute | solution.py:147
  113.4 9.6 %collective-permute-start.37 = (bf16[2,32,768]{2,1,0:T(8,128)(2,1)S(1)}, bf16[2,32,768]{2,1,0:T(8,128)(2,1)S(1)}, u32[]{:S(2)}, u32[]{:S(2)}) collective-permute-start(bf16[2,32,768]{2,1,0:T(8,128)(2,1)S(1)} %slice.39), channel_id=1, source_target_pairs={{0,224},{32,0},{64,32},{96,64},{128,96},{160,128},{192,160},{224,1... | collective-permute-start | bytes 294920 | tf_op jit(solution)/shard_map/ppermute | solution.py:147
  117.2 5.9 %collective-permute-start.33 = (bf16[2,32,768]{2,1,0:T(8,128)(2,1)S(1)}, bf16[2,32,768]{2,1,0:T(8,128)(2,1)S(1)}, u32[]{:S(2)}, u32[]{:S(2)}) collective-permute-start(bf16[2,32,768]{2,1,0:T(8,128)(2,1)S(1)} %slice.38), channel_id=1, source_target_pairs={{0,32},{32,64},{64,96},{96,128},{128,160},{160,192},{192,224},{224... | collective-permute-start | bytes 294920 | tf_op jit(solution)/shard_map/ppermute | solution.py:147
  117.3 6.7 %collective-permute-start.28 = (bf16[2,32,768]{2,1,0:T(8,128)(2,1)S(1)}, bf16[2,32,768]{2,1,0:T(8,128)(2,1)S(1)}, u32[]{:S(2)}, u32[]{:S(2)}) collective-permute-start(bf16[2,32,768]{2,1,0:T(8,128)(2,1)S(1)} %slice.37), channel_id=1, source_target_pairs={{0,224},{32,0},{64,32},{96,64},{128,96},{160,128},{192,160},{224,1... | collective-permute-start | bytes 294920 | tf_op jit(solution)/shard_map/ppermute | solution.py:147
  120.6 5.9 %collective-permute-start.24 = (bf16[2,32,768]{2,1,0:T(8,128)(2,1)S(1)}, bf16[2,32,768]{2,1,0:T(8,128)(2,1)S(1)}, u32[]{:S(2)}, u32[]{:S(2)}) collective-permute-start(bf16[2,32,768]{2,1,0:T(8,128)(2,1)S(1)} %slice.36), channel_id=1, source_target_pairs={{0,32},{32,64},{64,96},{96,128},{128,160},{160,192},{192,224},{224... | collective-permute-start | bytes 294920 | tf_op jit(solution)/shard_map/ppermute | solution.py:147

commit v3 on v2

--- a/solution.py
+++ b/solution.py
@@ -26,6 +26,10 @@
 
 def shift(n, k):
     return [(i, (i + k) % n) for i in range(n)]
+
+
+def pair(n, mask):
+    return [(i, i ^ mask) for i in range(n)]
 
 
 def near(*arrays):
@@ -48,8 +52,8 @@
         pltpu.make_async_copy(g_ref.at[y, :, block], g_out, sems.at[NY]),
         pltpu.make_async_copy(count_hbm, count_ref, sems.at[NY + 1]),
     ]
-    for k, dy in enumerate(SIDES):
-        source = x_ref.at[lax.rem(y + dy, NY)]
+    for k, mask in enumerate(SIDES):
+        source = x_ref.at[y ^ mask]
         copies.append(pltpu.make_async_copy(source, x_outs[k], sems.at[k]))
     for copy in copies:
         copy.start()
@@ -67,15 +71,15 @@
     x, c = lax.axis_index("x"), lax.axis_index("c")
     half = NZ // 2
     for core in range(NC):
-        own, right, left, far_a, far_b = pieces[5 * core : 5 * core + 5]
-        for offset, ref, first in (
+        own, near_1, near_3, far_a, far_b = pieces[5 * core : 5 * core + 5]
+        for mask, ref, first in (
             (0, own, 0),
-            (3, right, 0),
-            (1, left, 0),
+            (1, near_1, 0),
+            (3, near_3, 0),
             (2, far_a, 0),
             (2, far_b, half),
         ):
-            block = NC * lax.rem(x + offset, NX) + (c if core == 0 else 1 - c)
+            block = NC * (x ^ mask) + (c if core == 0 else 1 - c)
             for r in range(ref.shape[0]):
                 rows[first + r, block] = ref[r]
     total = None
@@ -116,10 +120,10 @@
     pieces, (out_ref, sems) = refs[:n], refs[n + aliased :]
     y, z = lax.axis_index("y"), lax.axis_index("z")
     copies = []
-    for piece, (dys, dz, row) in zip(pieces, places):
-        for index, dy in enumerate(dys):
+    for piece, (masks, dz, row) in zip(pieces, places):
+        for index, mask in enumerate(masks):
             target = out_ref.at[
-                lax.rem(y + dy, NY), lax.rem(z + dz + NZ, NZ), pl.ds(row, piece.shape[1])
+                y ^ mask, lax.rem(z + dz + NZ, NZ), pl.ds(row, piece.shape[1])
             ]
             copies.append(pltpu.make_async_copy(piece.at[index], target, sems.at[len(copies)]))
             copies[-1].start()
@@ -143,8 +147,8 @@
     )(*pieces, *([out] if aliased else []))
 
 
-def move(value, axis, size, by):
-    return lax.ppermute(value, axis, shift(size, by))
+def move(value, axis, to):
+    return lax.ppermute(value, axis, to)
 
 
 def body(x, g, counts):
@@ -168,17 +172,17 @@
         far_hbm(x.transpose(0, 2, 1).reshape(NY, NZ, COLS, CAP)),
         far_hbm(g.reshape(NY, NZ, CAP // BLK, BLK, width)),
     )
-    sides = [sides[0]] + [move(sides[k], "y", NY, SIDES[k]) for k in range(1, NY)]
+    sides = [sides[0]] + [move(sides[k], "y", pair(NY, SIDES[k])) for k in range(1, NY)]
     sides = jnp.stack(sides, axis=1)
     own = lax.all_to_all(mine, "z", 0, 0, tiled=True)
     xz = lax.all_to_all(sides, "z", 0, 0, tiled=True)
 
-    right = move(own, "x", NX, 1)
-    left = move(own, "x", NX, -1)
-    far_a = move(right[: NZ // 2], "x", NX, 1)
-    far_b = move(left[NZ // 2 :], "x", NX, -1)
-    pieces = [own, right, left, far_a, far_b]
-    pieces = pieces + [move(p, "c", NC, 1) for p in pieces]
+    near_1 = move(own, "x", pair(NX, 1))
+    near_3 = move(own, "x", pair(NX, 3))
+    far_a = move(near_3[: NZ // 2], "x", pair(NX, 1))
+    far_b = move(near_1[NZ // 2 :], "x", pair(NX, 3))
+    pieces = [own, near_1, near_3, far_a, far_b]
+    pieces = pieces + [move(p, "c", pair(NC, 1)) for p in pieces]
 
     grad = pl.pallas_call(
         grad_kernel,
@@ -191,15 +195,15 @@
     )(*near(xz, *pieces))
 
     mid = NY * COLS // 2
-    right = move(grad, "x", NX, 1)
-    left = move(grad, "x", NX, -1)
+    near_1 = move(grad, "x", pair(NX, 1))
+    near_3 = move(grad, "x", pair(NX, 3))
     total = gram_of(grad)
-    far_a = move(right[:mid], "x", NX, 1)
-    far_b = move(left[mid:], "x", NX, -1)
-    total = total + (gram_of(right) + gram_of(left))
-    other = move(total, "c", NC, 1)
-    other_far_a = move(far_a, "c", NC, 1)
-    other_far_b = move(far_b, "c", NC, 1)
+    far_a = move(near_3[:mid], "x", pair(NX, 1))
+    far_b = move(near_1[mid:], "x", pair(NX, 3))
+    total = total + (gram_of(near_1) + gram_of(near_3))
+    other = move(total, "c", pair(NC, 1))
+    other_far_a = move(far_a, "c", pair(NC, 1))
+    other_far_b = move(far_b, "c", pair(NC, 1))
     total = total + (gram_of(far_a) + gram_of(far_b))
 
     pieces = pl.pallas_call(
@@ -211,21 +215,21 @@
         name="newton",
     )(*near(total, other, other_far_a, other_far_b, grad))
 
-    rows = [pieces[0]] + [move(pieces[k], "y", NY, -SIDES[k]) for k in range(1, NY)]
+    rows = [pieces[0]] + [move(pieces[k], "y", pair(NY, SIDES[k])) for k in range(1, NY)]
     half = COLS // 2
     items = []
     for ks in CHUNKS:
         piece = jnp.stack([rows[k][0] for k in ks])
-        dys = tuple(SIDES[k] for k in ks)
-        items.append([(piece, (dys, 0, 0))])
+        masks = tuple(SIDES[k] for k in ks)
+        items.append([(piece, (masks, 0, 0))])
         right, left = piece, piece
         for n in range(1, 4):
-            right = move(right, "z", NZ, 1)
-            left = move(left, "z", NZ, -1)
-            items[-1] += [(right, (dys, -n, 0)), (left, (dys, n, 0))]
-        right = move(right[:, :half], "z", NZ, 1)
-        left = move(left[:, half:], "z", NZ, -1)
-        items[-1] += [(right, (dys, 4, 0)), (left, (dys, 4, half))]
+            right = move(right, "z", shift(NZ, 1))
+            left = move(left, "z", shift(NZ, -1))
+            items[-1] += [(right, (masks, -n, 0)), (left, (masks, n, 0))]
+        right = move(right[:, :half], "z", shift(NZ, 1))
+        left = move(left[:, half:], "z", shift(NZ, -1))
+        items[-1] += [(right, (masks, 4, 0)), (left, (masks, 4, half))]
     a, b = items
     out = place(None, width, a[:5] + b[:3])
     out = place(out, width, a[5:7] + b[3:5])

time: 128 us -> 124 us (0.969)
  the two profiles are of different devices: /device:TPU:24 before, /device:TPU:8 now
where the time goes in v3:
time: 124 us
  starting transfers between devices  60.8 us (49%)
  waiting for transfers between devices  47.2 us (38%)
  Pallas kernels  12 us (10%)
  matrix products  2.55 us (2%)
    ppermute x38, waiting for transfers between devices, move(): return lax.ppermute(value, axis, to)  46.9 us
    ppermute x38, starting transfers between devices, move(): return lax.ppermute(value, axis, to)  45.4 us
    all_to_all x1, starting transfers between devices, body(): own = lax.all_to_all(mine, 'z', 0, 0, tiled=True)  8.48 us
    all_to_all x1, starting transfers between devices, body(): xz = lax.all_to_all(sides, 'z', 0, 0, tiled=True)  6.93 us
    pallas_call x1, Pallas kernels, body(): pl.pallas_call(functools.partial(newton_kernel, math.sqrt(2048)), out_sha...  5.57 us
    pallas_call x4, Pallas kernels, place(): pl.pallas_call(functools.partial(place_kernel, places, n, int(aliased)),...  3.81 us
    dot_general x5, matrix products, gram_of(): lax.dot_general(rows, rows, (((0,), (0,)), ((), ())), preferred_element_t...  2.55 us
  transfers between devices with their start and end apart: 40, of which 22 were waited for; matrix products, arithmetic and copies ran while one was open for 2% of the time, Pallas kernels for 3%

profile of v3, /device:TPU:8, one launch (start us, length us, event | category | flops | bytes accessed | tf_op | source)
XLA Modules:
  0.0 123.9 jit_solution(13891591364475790326)
XLA Ops:
  0.0 1.9 %pack.1 = (bf16[8,64,128]{2,1,0:T(8,128)(2,1)S(1)}, bf16[8,64,128]{2,1,0:T(8,128)(2,1)S(1)}, bf16[8,64,128]{2,1,0:T(8,128)(2,1)S(1)}, bf16[8,64,128]{2,1,0:T(8,128)(2,1)S(1)}, bf16[8,16,768]{2,1,0:T(8,128)(2,1)}) custom-call(s32[1,32]{1,0:T(1,128)} %count_hbm.1, bf16[4,8,64,128]{3,2,1,0:T(8,128)(2,1)} %bitcast.21, bf16[4,8,8,16,768]{4,3,2,1,0:T(8,128)(2,1)} %bitcast.20), custom_call_target="tpu_custom_call" | custom-call | tf_op jit(solution)/shard_map/pack/pallas_call | solution.py:158
  1.9 8.5 %all-to-all-start.1 = ((bf16[8,16,768]{2,1,0:T(8,128)(2,1)}), bf16[8,16,768]{2,1,0:T(8,128)(2,1)S(1)}, u32[]{:S(2)}, u32[]{:S(2)}) async-start(bf16[8,16,768]{2,1,0:T(8,128)(2,1)} %get-tuple-element.18), calls=%async_computation.1 | async-start | bytes 393216 | tf_op jit(solution)/shard_map/all_to_all | solution.py:177
  10.9 2.4 %collective-permute-start.1 = (bf16[8,64,128]{2,1,0:T(8,128)(2,1)S(1)}, bf16[8,64,128]{2,1,0:T(8,128)(2,1)S(1)}, u32[]{:S(2)}, u32[]{:S(2)}) collective-permute-start(bf16[8,64,128]{2,1,0:T(8,128)(2,1)S(1)} %get-tuple-element.16), channel_id=1, source_target_pairs={{0,24},{8,16},{16,8},{24,0},{1,25},{9,17},{17,9},{25,1},{2,26},{10... | collective-permute-start | bytes 393224 | tf_op jit(solution)/shard_map/ppermute | solution.py:151
  13.3 1.2 collective-permute-start.2
  14.5 1.1 collective-permute-done
  15.6 2.9 %collective-permute-done.1 = bf16[8,64,128]{2,1,0:T(8,128)(2,1)S(1)} collective-permute-done((bf16[8,64,128]{2,1,0:T(8,128)(2,1)S(1)}, bf16[8,64,128]{2,1,0:T(8,128)(2,1)S(1)}, u32[]{:S(2)}, u32[]{:S(2)}) %collective-permute-start.1) | collective-permute-done | bytes 131104 | tf_op jit(solution)/shard_map/ppermute | solution.py:151
  18.5 1.3 %collective-permute-done.2 = bf16[8,64,128]{2,1,0:T(8,128)(2,1)S(1)} collective-permute-done((bf16[8,64,128]{2,1,0:T(8,128)(2,1)S(1)}, bf16[8,64,128]{2,1,0:T(8,128)(2,1)S(1)}, u32[]{:S(2)}, u32[]{:S(2)}) %collective-permute-start.2) | collective-permute-done | bytes 131104 | tf_op jit(solution)/shard_map/ppermute | solution.py:151
  19.7 0.9 pad_maximum_fusion
  20.9 6.9 %all-to-all-start = ((bf16[8,4,64,128]{3,2,1,0:T(8,128)(2,1)}), bf16[8,4,64,128]{3,2,1,0:T(8,128)(2,1)S(1)}, u32[]{:S(2)}, u32[]{:S(2)}) async-start(bf16[8,4,64,128]{3,2,1,0:T(8,128)(2,1)} %pad_maximum_fusion), calls=%async_computation | async-start | bytes 1048576 | tf_op jit(solution)/shard_map/all_to_all | solution.py:178
  27.8 2.8 %collective-permute-start.4 = (bf16[8,16,768]{2,1,0:T(8,128)(2,1)S(1)}, bf16[8,16,768]{2,1,0:T(8,128)(2,1)S(1)}, u32[]{:S(2)}, u32[]{:S(2)}) collective-permute-start(bf16[8,16,768]{2,1,0:T(8,128)(2,1)S(1)} %all-to-all-done.1.refs_0_), channel_id=1, source_target_pairs={{0,6},{2,4},{4,2},{6,0},{1,7},{3,5},{5,3},{7,1},{8,14},{10,12},{12... | collective-permute-start | bytes 589832 | tf_op jit(solution)/shard_map/ppermute | solution.py:151
  30.8 3.9 %collective-permute-done.4.refs_2_ = bf16[8,16,768]{2,1,0:T(8,128)(2,1)S(1)} collective-permute-done((bf16[8,16,768]{2,1,0:T(8,128)(2,1)S(1)}, bf16[8,16,768]{2,1,0:T(8,128)(2,1)S(1)}, u32[]{:S(2)}, u32[]{:S(2)}) %collective-permute-start.4) | collective-permute-done | bytes 196640 | tf_op jit(solution)/shard_map/ppermute | solution.py:151
  35.1 2.2 %collective-permute-done.3.refs_1_ = bf16[8,16,768]{2,1,0:T(8,128)(2,1)S(1)} collective-permute-done((bf16[8,16,768]{2,1,0:T(8,128)(2,1)S(1)}, bf16[8,16,768]{2,1,0:T(8,128)(2,1)S(1)}, u32[]{:S(2)}, u32[]{:S(2)}) %collective-permute-start.3) | collective-permute-done | bytes 196640 | tf_op jit(solution)/shard_map/ppermute | solution.py:151
  38.2 1.2 collective-permute-done.5.refs_3_
  39.4 3.8 %collective-permute-done.6.refs_4_ = bf16[4,16,768]{2,1,0:T(8,128)(2,1)S(1)} collective-permute-done((bf16[4,16,768]{2,1,0:T(8,128)(2,1)S(1)}, bf16[4,16,768]{2,1,0:T(8,128)(2,1)S(1)}, u32[]{:S(2)}, u32[]{:S(2)}) %collective-permute-start.6) | collective-permute-done | bytes 98336 | tf_op jit(solution)/shard_map/ppermute | solution.py:151
  43.2 1.3 %collective-permute-done.11.refs_9_ = bf16[4,16,768]{2,1,0:T(8,128)(2,1)S(1)} collective-permute-done((bf16[4,16,768]{2,1,0:T(8,128)(2,1)S(1)}, bf16[4,16,768]{2,1,0:T(8,128)(2,1)S(1)}, u32[]{:S(2)}, u32[]{:S(2)}) %collective-permute-start.11) | collective-permute-done | bytes 98336 | tf_op jit(solution)/shard_map/ppermute | solution.py:151
  44.5 0.7 grad.1.grad_ref
  45.6 2.1 %collective-permute-start.13 = (bf16[256,768]{1,0:T(8,128)(2,1)S(1)}, bf16[256,768]{1,0:T(8,128)(2,1)S(1)}, u32[]{:S(2)}, u32[]{:S(2)}) collective-permute-start(bf16[256,768]{1,0:T(8,128)(2,1)S(1)} %grad.1.grad_ref), channel_id=1, source_target_pairs={{0,6},{2,4},{4,2},{6,0},{1,7},{3,5},{5,3},{7,1},{8,14},{10,12},{12... | collective-permute-start | bytes 1179656 | tf_op jit(solution)/shard_map/ppermute | solution.py:151
  47.7 8.7 %collective-permute-done.12 = bf16[256,768]{1,0:T(8,128)(2,1)S(1)} collective-permute-done((bf16[256,768]{1,0:T(8,128)(2,1)S(1)}, bf16[256,768]{1,0:T(8,128)(2,1)S(1)}, u32[]{:S(2)}, u32[]{:S(2)}) %collective-permute-start.12) | collective-permute-done | bytes 393248 | tf_op jit(solution)/shard_map/ppermute | solution.py:151
  56.4 0.5 fusion
  57.0 0.8 collective-permute-done.13
  58.3 0.5 add_add_fusion.1
  58.9 0.5 collective-permute-start.14
  59.5 1.0 collective-permute-start.15
  60.4 5.9 %collective-permute-done.14 = bf16[128,768]{1,0:T(8,128)(2,1)S(1)} collective-permute-done((bf16[128,768]{1,0:T(8,128)(2,1)S(1)}, bf16[128,768]{1,0:T(8,128)(2,1)S(1)}, u32[]{:S(2)}, u32[]{:S(2)}) %collective-permute-start.14) | collective-permute-done | bytes 196640 | tf_op jit(solution)/shard_map/ppermute | solution.py:151
  66.3 1.5 %collective-permute-done.15 = bf16[128,768]{1,0:T(8,128)(2,1)S(1)} collective-permute-done((bf16[128,768]{1,0:T(8,128)(2,1)S(1)}, bf16[128,768]{1,0:T(8,128)(2,1)S(1)}, u32[]{:S(2)}, u32[]{:S(2)}) %collective-permute-start.15) | collective-permute-done | bytes 196640 | tf_op jit(solution)/shard_map/ppermute | solution.py:151
  68.3 0.5 add_add_fusion.mine_ref
  69.2 5.6 %newton.1 = (bf16[1,64,768]{2,1,0:T(8,128)(2,1)S(1)}, bf16[1,64,768]{2,1,0:T(8,128)(2,1)S(1)}, bf16[1,64,768]{2,1,0:T(8,128)(2,1)S(1)}, bf16[1,64,768]{2,1,0:T(8,128)(2,1)S(1)}) custom-call(f32[768,768]{1,0:T(8,128)S(1)} %add_add_fusion.mine_ref, f32[768,768]{1,0:T(8,128)S(1)} %collective-permute-done.16.other_ref, ...), custom_call_target="tpu_custom_call" | custom-call | tf_op jit(solution)/shard_map/newton/pallas_call | solution.py:209
  74.8 1.2 collective-permute-start.19
  76.0 2.7 %collective-permute-start.20 = (bf16[1,64,768]{2,1,0:T(8,128)(2,1)S(1)}, bf16[1,64,768]{2,1,0:T(8,128)(2,1)S(1)}, u32[]{:S(2)}, u32[]{:S(2)}) collective-permute-start(bf16[1,64,768]{2,1,0:T(8,128)(2,1)S(1)} %get-tuple-element.20), channel_id=1, source_target_pairs={{0,16},{8,24},{16,0},{24,8},{1,17},{9,25},{17,1},{25,9},{2,18},{10... | collective-permute-start | bytes 294920 | tf_op jit(solution)/shard_map/ppermute | solution.py:151
  79.0 4.7 %collective-permute-done.29 = bf16[1,64,768]{2,1,0:T(8,128)(2,1)S(1)} collective-permute-done((bf16[1,64,768]{2,1,0:T(8,128)(2,1)S(1)}, bf16[1,64,768]{2,1,0:T(8,128)(2,1)S(1)}, u32[]{:S(2)}, u32[]{:S(2)}) %collective-permute-start.29) | collective-permute-done | bytes 98336 | tf_op jit(solution)/shard_map/ppermute | solution.py:151
  83.7 3.3 %collective-permute-start.34 = (bf16[2,64,768]{2,1,0:T(8,128)(2,1)S(1)}, bf16[2,64,768]{2,1,0:T(8,128)(2,1)S(1)}, u32[]{:S(2)}, u32[]{:S(2)}) collective-permute-start(bf16[2,64,768]{2,1,0:T(8,128)(2,1)S(1)} %constant_dynamic-update-slice_fusion.2.refs_0_), channel_id=1, source_target_pairs={{0,224},{32,0},{64,32},{96,64},{128,96},{160,128},{192,160},{224,1... | collective-permute-start | bytes 589832 | tf_op jit(solution)/shard_map/ppermute | solution.py:151
  87.0 3.3 %collective-permute-start.25 = (bf16[2,64,768]{2,1,0:T(8,128)(2,1)S(1)}, bf16[2,64,768]{2,1,0:T(8,128)(2,1)S(1)}, u32[]{:S(2)}, u32[]{:S(2)}) collective-permute-start(bf16[2,64,768]{2,1,0:T(8,128)(2,1)S(1)} %constant_dynamic-update-slice_fusion.refs_5_), channel_id=1, source_target_pairs={{0,224},{32,0},{64,32},{96,64},{128,96},{160,128},{192,160},{224,1... | collective-permute-start | bytes 589832 | tf_op jit(solution)/shard_map/ppermute | solution.py:151
  90.3 1.8 %collective-permute-done.34.refs_2_ = bf16[2,64,768]{2,1,0:T(8,128)(2,1)S(1)} collective-permute-done((bf16[2,64,768]{2,1,0:T(8,128)(2,1)S(1)}, bf16[2,64,768]{2,1,0:T(8,128)(2,1)S(1)}, u32[]{:S(2)}, u32[]{:S(2)}) %collective-permute-start.34) | collective-permute-done | bytes 196640 | tf_op jit(solution)/shard_map/ppermute | solution.py:151
  92.1 3.7 %collective-permute-start.35 = (bf16[2,64,768]{2,1,0:T(8,128)(2,1)S(1)}, bf16[2,64,768]{2,1,0:T(8,128)(2,1)S(1)}, u32[]{:S(2)}, u32[]{:S(2)}) collective-permute-start(bf16[2,64,768]{2,1,0:T(8,128)(2,1)S(1)} %collective-permute-done.34.refs_2_), channel_id=1, source_target_pairs={{0,224},{32,0},{64,32},{96,64},{128,96},{160,128},{192,160},{224,1... | collective-permute-start | bytes 589832 | tf_op jit(solution)/shard_map/ppermute | solution.py:151
  95.8 0.5 collective-permute-done.25.refs_7_
  96.4 3.7 %collective-permute-start.26 = (bf16[2,64,768]{2,1,0:T(8,128)(2,1)S(1)}, bf16[2,64,768]{2,1,0:T(8,128)(2,1)S(1)}, u32[]{:S(2)}, u32[]{:S(2)}) collective-permute-start(bf16[2,64,768]{2,1,0:T(8,128)(2,1)S(1)} %collective-permute-done.25.refs_7_), channel_id=1, source_target_pairs={{0,224},{32,0},{64,32},{96,64},{128,96},{160,128},{192,160},{224,1... | collective-permute-start | bytes 589832 | tf_op jit(solution)/shard_map/ppermute | solution.py:151
  100.1 0.8 collective-permute-done.35.refs_4_
  100.9 3.7 %collective-permute-start.36 = (bf16[2,64,768]{2,1,0:T(8,128)(2,1)S(1)}, bf16[2,64,768]{2,1,0:T(8,128)(2,1)S(1)}, u32[]{:S(2)}, u32[]{:S(2)}) collective-permute-start(bf16[2,64,768]{2,1,0:T(8,128)(2,1)S(1)} %collective-permute-done.35.refs_4_), channel_id=1, source_target_pairs={{0,224},{32,0},{64,32},{96,64},{128,96},{160,128},{192,160},{224,1... | collective-permute-start | bytes 589832 | tf_op jit(solution)/shard_map/ppermute | solution.py:151
  104.6 0.8 collective-permute-done.26.refs_3_
  105.3 3.7 %collective-permute-start.27 = (bf16[2,64,768]{2,1,0:T(8,128)(2,1)S(1)}, bf16[2,64,768]{2,1,0:T(8,128)(2,1)S(1)}, u32[]{:S(2)}, u32[]{:S(2)}) collective-permute-start(bf16[2,64,768]{2,1,0:T(8,128)(2,1)S(1)} %collective-permute-done.26.refs_3_), channel_id=1, source_target_pairs={{0,224},{32,0},{64,32},{96,64},{128,96},{160,128},{192,160},{224,1... | collective-permute-start | bytes 589832 | tf_op jit(solution)/shard_map/ppermute | solution.py:151
  109.0 0.8 collective-permute-done.36.refs_1_
  109.9 3.8 %collective-permute-start.37 = (bf16[2,32,768]{2,1,0:T(8,128)(2,1)S(1)}, bf16[2,32,768]{2,1,0:T(8,128)(2,1)S(1)}, u32[]{:S(2)}, u32[]{:S(2)}) collective-permute-start(bf16[2,32,768]{2,1,0:T(8,128)(2,1)S(1)} %slice.39), channel_id=1, source_target_pairs={{0,224},{32,0},{64,32},{96,64},{128,96},{160,128},{192,160},{224,1... | collective-permute-start | bytes 294920 | tf_op jit(solution)/shard_map/ppermute | solution.py:151
  113.8 3.3 %collective-permute-start.28 = (bf16[2,32,768]{2,1,0:T(8,128)(2,1)S(1)}, bf16[2,32,768]{2,1,0:T(8,128)(2,1)S(1)}, u32[]{:S(2)}, u32[]{:S(2)}) collective-permute-start(bf16[2,32,768]{2,1,0:T(8,128)(2,1)S(1)} %slice.37), channel_id=1, source_target_pairs={{0,224},{32,0},{64,32},{96,64},{128,96},{160,128},{192,160},{224,1... | collective-permute-start | bytes 294920 | tf_op jit(solution)/shard_map/ppermute | solution.py:151
  117.2 1.3 %shard_map.37.refs_4_ = bf16[4,8,64,768]{3,2,1,0:T(8,128)(2,1)} custom-call(bf16[2,64,768]{2,1,0:T(8,128)(2,1)S(1)} %constant_dynamic-update-slice_fusion.2.refs_0_, bf16[2,64,768]{2,1,0:T(8,128)(2,1)S(1)} %collective-permute-done.30.refs_1_, bf16[2,64,768]{2,1,0:T(8,128)(2,1)S(1)} %collective-permute-done.34.refs_2_, ...), custom_call_target="tpu_custom_call" | custom-call | tf_op jit(solution)/shard_map/pallas_call | solution.py:139
  118.4 1.0 shard_map.38.refs_4_
  119.6 0.9 shard_map.39.refs_2_
  120.4 2.5 %collective-permute-done.24.refs_0_ = bf16[2,32,768]{2,1,0:T(8,128)(2,1)S(1)} collective-permute-done((bf16[2,32,768]{2,1,0:T(8,128)(2,1)S(1)}, bf16[2,32,768]{2,1,0:T(8,128)(2,1)S(1)}, u32[]{:S(2)}, u32[]{:S(2)}) %collective-permute-start.24) | collective-permute-done | bytes 98336 | tf_op jit(solution)/shard_map/ppermute | solution.py:151
  123.0 0.7 shard_map.40
  (57 shorter events, 5.0 us)
Async XLA Ops:
  1.9 18.9 %all-to-all-start.1 = ((bf16[8,16,768]{2,1,0:T(8,128)(2,1)}), bf16[8,16,768]{2,1,0:T(8,128)(2,1)S(1)}, u32[]{:S(2)}, u32[]{:S(2)}) async-start(bf16[8,16,768]{2,1,0:T(8,128)(2,1)} %get-tuple-element.18), calls=%async_computation.1 | async-start | bytes 393216 | tf_op jit(solution)/shard_map/all_to_all | solution.py:177
  10.4 5.2 %collective-permute-start = (bf16[8,64,128]{2,1,0:T(8,128)(2,1)S(1)}, bf16[8,64,128]{2,1,0:T(8,128)(2,1)S(1)}, u32[]{:S(2)}, u32[]{:S(2)}) collective-permute-start(bf16[8,64,128]{2,1,0:T(8,128)(2,1)S(1)} %get-tuple-element.15), channel_id=1, source_target_pairs={{0,8},{8,0},{16,24},{24,16},{1,9},{9,1},{17,25},{25,17},{2,10},{10... | collective-permute-start | bytes 393224 | tf_op jit(solution)/shard_map/ppermute | solution.py:151
  10.9 7.6 %collective-permute-start.1 = (bf16[8,64,128]{2,1,0:T(8,128)(2,1)S(1)}, bf16[8,64,128]{2,1,0:T(8,128)(2,1)S(1)}, u32[]{:S(2)}, u32[]{:S(2)}) collective-permute-start(bf16[8,64,128]{2,1,0:T(8,128)(2,1)S(1)} %get-tuple-element.16), channel_id=1, source_target_pairs={{0,24},{8,16},{16,8},{24,0},{1,25},{9,17},{17,9},{25,1},{2,26},{10... | collective-permute-start | bytes 393224 | tf_op jit(solution)/shard_map/ppermute | solution.py:151
  13.3 6.5 %collective-permute-start.2 = (bf16[8,64,128]{2,1,0:T(8,128)(2,1)S(1)}, bf16[8,64,128]{2,1,0:T(8,128)(2,1)S(1)}, u32[]{:S(2)}, u32[]{:S(2)}) collective-permute-start(bf16[8,64,128]{2,1,0:T(8,128)(2,1)S(1)} %get-tuple-element.17), channel_id=1, source_target_pairs={{0,16},{8,24},{16,0},{24,8},{1,17},{9,25},{17,1},{25,9},{2,18},{10... | collective-permute-start | bytes 393224 | tf_op jit(solution)/shard_map/ppermute | solution.py:151
  20.9 23.6 %all-to-all-start = ((bf16[8,4,64,128]{3,2,1,0:T(8,128)(2,1)}), bf16[8,4,64,128]{3,2,1,0:T(8,128)(2,1)S(1)}, u32[]{:S(2)}, u32[]{:S(2)}) async-start(bf16[8,4,64,128]{3,2,1,0:T(8,128)(2,1)} %pad_maximum_fusion), calls=%async_computation | async-start | bytes 1048576 | tf_op jit(solution)/shard_map/all_to_all | solution.py:178
  27.8 6.9 %collective-permute-start.4 = (bf16[8,16,768]{2,1,0:T(8,128)(2,1)S(1)}, bf16[8,16,768]{2,1,0:T(8,128)(2,1)S(1)}, u32[]{:S(2)}, u32[]{:S(2)}) collective-permute-start(bf16[8,16,768]{2,1,0:T(8,128)(2,1)S(1)} %all-to-all-done.1.refs_0_), channel_id=1, source_target_pairs={{0,6},{2,4},{4,2},{6,0},{1,7},{3,5},{5,3},{7,1},{8,14},{10,12},{12... | collective-permute-start | bytes 589832 | tf_op jit(solution)/shard_map/ppermute | solution.py:151
  30.6 6.7 %collective-permute-start.3 = (bf16[8,16,768]{2,1,0:T(8,128)(2,1)S(1)}, bf16[8,16,768]{2,1,0:T(8,128)(2,1)S(1)}, u32[]{:S(2)}, u32[]{:S(2)}) collective-permute-start(bf16[8,16,768]{2,1,0:T(8,128)(2,1)S(1)} %all-to-all-done.1.refs_0_), channel_id=1, source_target_pairs={{0,2},{2,0},{4,6},{6,4},{1,3},{3,1},{5,7},{7,5},{8,10},{10,8},{12,... | collective-permute-start | bytes 589832 | tf_op jit(solution)/shard_map/ppermute | solution.py:151
  30.8 12.4 %collective-permute-start.7 = (bf16[8,16,768]{2,1,0:T(8,128)(2,1)S(1)}, bf16[8,16,768]{2,1,0:T(8,128)(2,1)S(1)}, u32[]{:S(2)}, u32[]{:S(2)}) collective-permute-start(bf16[8,16,768]{2,1,0:T(8,128)(2,1)S(1)} %all-to-all-done.1.refs_0_), channel_id=1, source_target_pairs={{0,1},{1,0},{2,3},{3,2},{4,5},{5,4},{6,7},{7,6},{8,9},{9,8},{10,11... | collective-permute-start | bytes 589832 | tf_op jit(solution)/shard_map/ppermute | solution.py:151
  34.7 4.7 %collective-permute-start.5 = (bf16[4,16,768]{2,1,0:T(8,128)(2,1)S(1)}, bf16[4,16,768]{2,1,0:T(8,128)(2,1)S(1)}, u32[]{:S(2)}, u32[]{:S(2)}) collective-permute-start(bf16[4,16,768]{2,1,0:T(8,128)(2,1)S(1)} %slice.32), channel_id=1, source_target_pairs={{0,2},{2,0},{4,6},{6,4},{1,3},{3,1},{5,7},{7,5},{8,10},{10,8},{12,... | collective-permute-start | bytes 294920 | tf_op jit(solution)/shard_map/ppermute | solution.py:151
  37.3 5.9 %collective-permute-start.6 = (bf16[4,16,768]{2,1,0:T(8,128)(2,1)S(1)}, bf16[4,16,768]{2,1,0:T(8,128)(2,1)S(1)}, u32[]{:S(2)}, u32[]{:S(2)}) collective-permute-start(bf16[4,16,768]{2,1,0:T(8,128)(2,1)S(1)} %slice.33), channel_id=1, source_target_pairs={{0,6},{2,4},{4,2},{6,0},{1,7},{3,5},{5,3},{7,1},{8,14},{10,12},{12... | collective-permute-start | bytes 294920 | tf_op jit(solution)/shard_map/ppermute | solution.py:151
  37.7 5.5 %collective-permute-start.9 = (bf16[8,16,768]{2,1,0:T(8,128)(2,1)S(1)}, bf16[8,16,768]{2,1,0:T(8,128)(2,1)S(1)}, u32[]{:S(2)}, u32[]{:S(2)}) collective-permute-start(bf16[8,16,768]{2,1,0:T(8,128)(2,1)S(1)} %collective-permute-done.4.refs_2_), channel_id=1, source_target_pairs={{0,1},{1,0},{2,3},{3,2},{4,5},{5,4},{6,7},{7,6},{8,9},{9,8},{10,11... | collective-permute-start | bytes 589832 | tf_op jit(solution)/shard_map/ppermute | solution.py:151
  37.7 6.8 %collective-permute-start.8 = (bf16[8,16,768]{2,1,0:T(8,128)(2,1)S(1)}, bf16[8,16,768]{2,1,0:T(8,128)(2,1)S(1)}, u32[]{:S(2)}, u32[]{:S(2)}) collective-permute-start(bf16[8,16,768]{2,1,0:T(8,128)(2,1)S(1)} %collective-permute-done.3.refs_1_), channel_id=1, source_target_pairs={{0,1},{1,0},{2,3},{3,2},{4,5},{5,4},{6,7},{7,6},{8,9},{9,8},{10,11... | collective-permute-start | bytes 589832 | tf_op jit(solution)/shard_map/ppermute | solution.py:151
  39.4 3.8 %collective-permute-start.10 = (bf16[4,16,768]{2,1,0:T(8,128)(2,1)S(1)}, bf16[4,16,768]{2,1,0:T(8,128)(2,1)S(1)}, u32[]{:S(2)}, u32[]{:S(2)}) collective-permute-start(bf16[4,16,768]{2,1,0:T(8,128)(2,1)S(1)} %collective-permute-done.5.refs_3_), channel_id=1, source_target_pairs={{0,1},{1,0},{2,3},{3,2},{4,5},{5,4},{6,7},{7,6},{8,9},{9,8},{10,11... | collective-permute-start | bytes 294920 | tf_op jit(solution)/shard_map/ppermute | solution.py:151
  43.2 1.3 %collective-permute-start.11 = (bf16[4,16,768]{2,1,0:T(8,128)(2,1)S(1)}, bf16[4,16,768]{2,1,0:T(8,128)(2,1)S(1)}, u32[]{:S(2)}, u32[]{:S(2)}) collective-permute-start(bf16[4,16,768]{2,1,0:T(8,128)(2,1)S(1)} %collective-permute-done.6.refs_4_), channel_id=1, source_target_pairs={{0,1},{1,0},{2,3},{3,2},{4,5},{5,4},{6,7},{7,6},{8,9},{9,8},{10,11... | collective-permute-start | bytes 294920 | tf_op jit(solution)/shard_map/ppermute | solution.py:151
  45.2 11.3 %collective-permute-start.12 = (bf16[256,768]{1,0:T(8,128)(2,1)S(1)}, bf16[256,768]{1,0:T(8,128)(2,1)S(1)}, u32[]{:S(2)}, u32[]{:S(2)}) collective-permute-start(bf16[256,768]{1,0:T(8,128)(2,1)S(1)} %grad.1.grad_ref), channel_id=1, source_target_pairs={{0,2},{2,0},{4,6},{6,4},{1,3},{3,1},{5,7},{7,5},{8,10},{10,8},{12,... | collective-permute-start | bytes 1179656 | tf_op jit(solution)/shard_map/ppermute | solution.py:151
  45.6 12.1 %collective-permute-start.13 = (bf16[256,768]{1,0:T(8,128)(2,1)S(1)}, bf16[256,768]{1,0:T(8,128)(2,1)S(1)}, u32[]{:S(2)}, u32[]{:S(2)}) collective-permute-start(bf16[256,768]{1,0:T(8,128)(2,1)S(1)} %grad.1.grad_ref), channel_id=1, source_target_pairs={{0,6},{2,4},{4,2},{6,0},{1,7},{3,5},{5,3},{7,1},{8,14},{10,12},{12... | collective-permute-start | bytes 1179656 | tf_op jit(solution)/shard_map/ppermute | solution.py:151
  58.8 10.4 %collective-permute-start.16 = (f32[768,768]{1,0:T(8,128)S(1)}, f32[768,768]{1,0:T(8,128)S(1)}, u32[]{:S(2)}, u32[]{:S(2)}) collective-permute-start(f32[768,768]{1,0:T(8,128)S(1)} %add_add_fusion.1), channel_id=1, source_target_pairs={{0,1},{1,0},{2,3},{3,2},{4,5},{5,4},{6,7},{7,6},{8,9},{9,8},{10,11... | collective-permute-start | bytes 7077896 | tf_op jit(solution)/shard_map/ppermute | solution.py:151
  58.9 7.4 %collective-permute-start.14 = (bf16[128,768]{1,0:T(8,128)(2,1)S(1)}, bf16[128,768]{1,0:T(8,128)(2,1)S(1)}, u32[]{:S(2)}, u32[]{:S(2)}) collective-permute-start(bf16[128,768]{1,0:T(8,128)(2,1)S(1)} %slice.34), channel_id=1, source_target_pairs={{0,2},{2,0},{4,6},{6,4},{1,3},{3,1},{5,7},{7,5},{8,10},{10,8},{12,... | collective-permute-start | bytes 589832 | tf_op jit(solution)/shard_map/ppermute | solution.py:151
  59.5 8.3 %collective-permute-start.15 = (bf16[128,768]{1,0:T(8,128)(2,1)S(1)}, bf16[128,768]{1,0:T(8,128)(2,1)S(1)}, u32[]{:S(2)}, u32[]{:S(2)}) collective-permute-start(bf16[128,768]{1,0:T(8,128)(2,1)S(1)} %slice.35), channel_id=1, source_target_pairs={{0,6},{2,4},{4,2},{6,0},{1,7},{3,5},{5,3},{7,1},{8,14},{10,12},{12... | collective-permute-start | bytes 589832 | tf_op jit(solution)/shard_map/ppermute | solution.py:151
  66.3 2.5 %collective-permute-start.17 = (bf16[128,768]{1,0:T(8,128)(2,1)S(1)}, bf16[128,768]{1,0:T(8,128)(2,1)S(1)}, u32[]{:S(2)}, u32[]{:S(2)}) collective-permute-start(bf16[128,768]{1,0:T(8,128)(2,1)S(1)} %collective-permute-done.14), channel_id=1, source_target_pairs={{0,1},{1,0},{2,3},{3,2},{4,5},{5,4},{6,7},{7,6},{8,9},{9,8},{10,11... | collective-permute-start | bytes 589832 | tf_op jit(solution)/shard_map/ppermute | solution.py:151
  67.8 1.4 %collective-permute-start.18 = (bf16[128,768]{1,0:T(8,128)(2,1)S(1)}, bf16[128,768]{1,0:T(8,128)(2,1)S(1)}, u32[]{:S(2)}, u32[]{:S(2)}) collective-permute-start(bf16[128,768]{1,0:T(8,128)(2,1)S(1)} %collective-permute-done.15), channel_id=1, source_target_pairs={{0,1},{1,0},{2,3},{3,2},{4,5},{5,4},{6,7},{7,6},{8,9},{9,8},{10,11... | collective-permute-start | bytes 589832 | tf_op jit(solution)/shard_map/ppermute | solution.py:151
  74.8 12.2 %collective-permute-start.19 = (bf16[1,64,768]{2,1,0:T(8,128)(2,1)S(1)}, bf16[1,64,768]{2,1,0:T(8,128)(2,1)S(1)}, u32[]{:S(2)}, u32[]{:S(2)}) collective-permute-start(bf16[1,64,768]{2,1,0:T(8,128)(2,1)S(1)} %get-tuple-element.19), channel_id=1, source_target_pairs={{0,24},{8,16},{16,8},{24,0},{1,25},{9,17},{17,9},{25,1},{2,26},{10... | collective-permute-start | bytes 294920 | tf_op jit(solution)/shard_map/ppermute | solution.py:151
  76.0 11.1 %collective-permute-start.20 = (bf16[1,64,768]{2,1,0:T(8,128)(2,1)S(1)}, bf16[1,64,768]{2,1,0:T(8,128)(2,1)S(1)}, u32[]{:S(2)}, u32[]{:S(2)}) collective-permute-start(bf16[1,64,768]{2,1,0:T(8,128)(2,1)S(1)} %get-tuple-element.20), channel_id=1, source_target_pairs={{0,16},{8,24},{16,0},{24,8},{1,17},{9,25},{17,1},{25,9},{2,18},{10... | collective-permute-start | bytes 294920 | tf_op jit(solution)/shard_map/ppermute | solution.py:151
  78.7 5.0 %collective-permute-start.29 = (bf16[1,64,768]{2,1,0:T(8,128)(2,1)S(1)}, bf16[1,64,768]{2,1,0:T(8,128)(2,1)S(1)}, u32[]{:S(2)}, u32[]{:S(2)}) collective-permute-start(bf16[1,64,768]{2,1,0:T(8,128)(2,1)S(1)} %get-tuple-element.22), channel_id=1, source_target_pairs={{0,8},{8,0},{16,24},{24,16},{1,9},{9,1},{17,25},{25,17},{2,10},{10... | collective-permute-start | bytes 294920 | tf_op jit(solution)/shard_map/ppermute | solution.py:151
  83.7 8.5 %collective-permute-start.34 = (bf16[2,64,768]{2,1,0:T(8,128)(2,1)S(1)}, bf16[2,64,768]{2,1,0:T(8,128)(2,1)S(1)}, u32[]{:S(2)}, u32[]{:S(2)}) collective-permute-start(bf16[2,64,768]{2,1,0:T(8,128)(2,1)S(1)} %constant_dynamic-update-slice_fusion.2.refs_0_), channel_id=1, source_target_pairs={{0,224},{32,0},{64,32},{96,64},{128,96},{160,128},{192,160},{224,1... | collective-permute-start | bytes 589832 | tf_op jit(solution)/shard_map/ppermute | solution.py:151
  87.0 8.8 %collective-permute-start.30 = (bf16[2,64,768]{2,1,0:T(8,128)(2,1)S(1)}, bf16[2,64,768]{2,1,0:T(8,128)(2,1)S(1)}, u32[]{:S(2)}, u32[]{:S(2)}) collective-permute-start(bf16[2,64,768]{2,1,0:T(8,128)(2,1)S(1)} %constant_dynamic-update-slice_fusion.2.refs_0_), channel_id=1, source_target_pairs={{0,32},{32,64},{64,96},{96,128},{128,160},{160,192},{192,224},{224... | collective-permute-start | bytes 589832 | tf_op jit(solution)/shard_map/ppermute | solution.py:151
  87.0 9.3 %collective-permute-start.25 = (bf16[2,64,768]{2,1,0:T(8,128)(2,1)S(1)}, bf16[2,64,768]{2,1,0:T(8,128)(2,1)S(1)}, u32[]{:S(2)}, u32[]{:S(2)}) collective-permute-start(bf16[2,64,768]{2,1,0:T(8,128)(2,1)S(1)} %constant_dynamic-update-slice_fusion.refs_5_), channel_id=1, source_target_pairs={{0,224},{32,0},{64,32},{96,64},{128,96},{160,128},{192,160},{224,1... | collective-permute-start | bytes 589832 | tf_op jit(solution)/shard_map/ppermute | solution.py:151
  90.3 9.7 %collective-permute-start.21 = (bf16[2,64,768]{2,1,0:T(8,128)(2,1)S(1)}, bf16[2,64,768]{2,1,0:T(8,128)(2,1)S(1)}, u32[]{:S(2)}, u32[]{:S(2)}) collective-permute-start(bf16[2,64,768]{2,1,0:T(8,128)(2,1)S(1)} %constant_dynamic-update-slice_fusion.refs_5_), channel_id=1, source_target_pairs={{0,32},{32,64},{64,96},{96,128},{128,160},{160,192},{192,224},{224... | collective-permute-start | bytes 589832 | tf_op jit(solution)/shard_map/ppermute | solution.py:151
  92.1 8.7 %collective-permute-start.35 = (bf16[2,64,768]{2,1,0:T(8,128)(2,1)S(1)}, bf16[2,64,768]{2,1,0:T(8,128)(2,1)S(1)}, u32[]{:S(2)}, u32[]{:S(2)}) collective-permute-start(bf16[2,64,768]{2,1,0:T(8,128)(2,1)S(1)} %collective-permute-done.34.refs_2_), channel_id=1, source_target_pairs={{0,224},{32,0},{64,32},{96,64},{128,96},{160,128},{192,160},{224,1... | collective-permute-start | bytes 589832 | tf_op jit(solution)/shard_map/ppermute | solution.py:151
  95.8 8.7 %collective-permute-start.31 = (bf16[2,64,768]{2,1,0:T(8,128)(2,1)S(1)}, bf16[2,64,768]{2,1,0:T(8,128)(2,1)S(1)}, u32[]{:S(2)}, u32[]{:S(2)}) collective-permute-start(bf16[2,64,768]{2,1,0:T(8,128)(2,1)S(1)} %collective-permute-done.30.refs_1_), channel_id=1, source_target_pairs={{0,32},{32,64},{64,96},{96,128},{128,160},{160,192},{192,224},{224... | collective-permute-start | bytes 589832 | tf_op jit(solution)/shard_map/ppermute | solution.py:151
  96.4 9.0 %collective-permute-start.26 = (bf16[2,64,768]{2,1,0:T(8,128)(2,1)S(1)}, bf16[2,64,768]{2,1,0:T(8,128)(2,1)S(1)}, u32[]{:S(2)}, u32[]{:S(2)}) collective-permute-start(bf16[2,64,768]{2,1,0:T(8,128)(2,1)S(1)} %collective-permute-done.25.refs_7_), channel_id=1, source_target_pairs={{0,224},{32,0},{64,32},{96,64},{128,96},{160,128},{192,160},{224,1... | collective-permute-start | bytes 589832 | tf_op jit(solution)/shard_map/ppermute | solution.py:151
  100.1 9.0 %collective-permute-start.22 = (bf16[2,64,768]{2,1,0:T(8,128)(2,1)S(1)}, bf16[2,64,768]{2,1,0:T(8,128)(2,1)S(1)}, u32[]{:S(2)}, u32[]{:S(2)}) collective-permute-start(bf16[2,64,768]{2,1,0:T(8,128)(2,1)S(1)} %collective-permute-done.21.refs_6_), channel_id=1, source_target_pairs={{0,32},{32,64},{64,96},{96,128},{128,160},{160,192},{192,224},{224... | collective-permute-start | bytes 589832 | tf_op jit(solution)/shard_map/ppermute | solution.py:151
  100.9 9.0 %collective-permute-start.36 = (bf16[2,64,768]{2,1,0:T(8,128)(2,1)S(1)}, bf16[2,64,768]{2,1,0:T(8,128)(2,1)S(1)}, u32[]{:S(2)}, u32[]{:S(2)}) collective-permute-start(bf16[2,64,768]{2,1,0:T(8,128)(2,1)S(1)} %collective-permute-done.35.refs_4_), channel_id=1, source_target_pairs={{0,224},{32,0},{64,32},{96,64},{128,96},{160,128},{192,160},{224,1... | collective-permute-start | bytes 589832 | tf_op jit(solution)/shard_map/ppermute | solution.py:151
  104.6 9.1 %collective-permute-start.32 = (bf16[2,64,768]{2,1,0:T(8,128)(2,1)S(1)}, bf16[2,64,768]{2,1,0:T(8,128)(2,1)S(1)}, u32[]{:S(2)}, u32[]{:S(2)}) collective-permute-start(bf16[2,64,768]{2,1,0:T(8,128)(2,1)S(1)} %collective-permute-done.31.refs_3_), channel_id=1, source_target_pairs={{0,32},{32,64},{64,96},{96,128},{128,160},{160,192},{192,224},{224... | collective-permute-start | bytes 589832 | tf_op jit(solution)/shard_map/ppermute | solution.py:151
  105.3 8.4 %collective-permute-start.27 = (bf16[2,64,768]{2,1,0:T(8,128)(2,1)S(1)}, bf16[2,64,768]{2,1,0:T(8,128)(2,1)S(1)}, u32[]{:S(2)}, u32[]{:S(2)}) collective-permute-start(bf16[2,64,768]{2,1,0:T(8,128)(2,1)S(1)} %collective-permute-done.26.refs_3_), channel_id=1, source_target_pairs={{0,224},{32,0},{64,32},{96,64},{128,96},{160,128},{192,160},{224,1... | collective-permute-start | bytes 589832 | tf_op jit(solution)/shard_map/ppermute | solution.py:151
  109.0 8.0 %collective-permute-start.23 = (bf16[2,64,768]{2,1,0:T(8,128)(2,1)S(1)}, bf16[2,64,768]{2,1,0:T(8,128)(2,1)S(1)}, u32[]{:S(2)}, u32[]{:S(2)}) collective-permute-start(bf16[2,64,768]{2,1,0:T(8,128)(2,1)S(1)} %collective-permute-done.22.refs_2_), channel_id=1, source_target_pairs={{0,32},{32,64},{64,96},{96,128},{128,160},{160,192},{192,224},{224... | collective-permute-start | bytes 589832 | tf_op jit(solution)/shard_map/ppermute | solution.py:151
  109.9 9.6 %collective-permute-start.37 = (bf16[2,32,768]{2,1,0:T(8,128)(2,1)S(1)}, bf16[2,32,768]{2,1,0:T(8,128)(2,1)S(1)}, u32[]{:S(2)}, u32[]{:S(2)}) collective-permute-start(bf16[2,32,768]{2,1,0:T(8,128)(2,1)S(1)} %slice.39), channel_id=1, source_target_pairs={{0,224},{32,0},{64,32},{96,64},{128,96},{160,128},{192,160},{224,1... | collective-permute-start | bytes 294920 | tf_op jit(solution)/shard_map/ppermute | solution.py:151
  113.6 5.9 %collective-permute-start.33 = (bf16[2,32,768]{2,1,0:T(8,128)(2,1)S(1)}, bf16[2,32,768]{2,1,0:T(8,128)(2,1)S(1)}, u32[]{:S(2)}, u32[]{:S(2)}) collective-permute-start(bf16[2,32,768]{2,1,0:T(8,128)(2,1)S(1)} %slice.38), channel_id=1, source_target_pairs={{0,32},{32,64},{64,96},{96,128},{128,160},{160,192},{192,224},{224... | collective-permute-start | bytes 294920 | tf_op jit(solution)/shard_map/ppermute | solution.py:151
  113.8 6.7 %collective-permute-start.28 = (bf16[2,32,768]{2,1,0:T(8,128)(2,1)S(1)}, bf16[2,32,768]{2,1,0:T(8,128)(2,1)S(1)}, u32[]{:S(2)}, u32[]{:S(2)}) collective-permute-start(bf16[2,32,768]{2,1,0:T(8,128)(2,1)S(1)} %slice.37), channel_id=1, source_target_pairs={{0,224},{32,0},{64,32},{96,64},{128,96},{160,128},{192,160},{224,1... | collective-permute-start | bytes 294920 | tf_op jit(solution)/shard_map/ppermute | solution.py:151
  117.1 5.9 %collective-permute-start.24 = (bf16[2,32,768]{2,1,0:T(8,128)(2,1)S(1)}, bf16[2,32,768]{2,1,0:T(8,128)(2,1)S(1)}, u32[]{:S(2)}, u32[]{:S(2)}) collective-permute-start(bf16[2,32,768]{2,1,0:T(8,128)(2,1)S(1)} %slice.36), channel_id=1, source_target_pairs={{0,32},{32,64},{64,96},{96,128},{128,160},{160,192},{192,224},{224... | collective-permute-start | bytes 294920 | tf_op jit(solution)/shard_map/ppermute | solution.py:151

commit v4 on v3

--- a/solution.py
+++ b/solution.py
@@ -24,12 +24,12 @@
 ANY = pl.BlockSpec(memory_space=pl.ANY)
 
 
-def shift(n, k):
-    return [(i, (i + k) % n) for i in range(n)]
-
-
 def pair(n, mask):
     return [(i, i ^ mask) for i in range(n)]
+
+
+def link(n, odd):
+    return [(i, (i + (1 if i % 2 == odd else n - 1)) % n) for i in range(n)]
 
 
 def near(*arrays):
@@ -119,11 +119,12 @@
 def place_kernel(places, n, aliased, *refs):
     pieces, (out_ref, sems) = refs[:n], refs[n + aliased :]
     y, z = lax.axis_index("y"), lax.axis_index("z")
+    side = 1 - 2 * (z & 1)
     copies = []
     for piece, (masks, dz, row) in zip(pieces, places):
         for index, mask in enumerate(masks):
             target = out_ref.at[
-                y ^ mask, lax.rem(z + dz + NZ, NZ), pl.ds(row, piece.shape[1])
+                y ^ mask, lax.rem(z + side * dz + NZ, NZ), pl.ds(row, piece.shape[1])
             ]
             copies.append(pltpu.make_async_copy(piece.at[index], target, sems.at[len(copies)]))
             copies[-1].start()
@@ -222,14 +223,12 @@
         piece = jnp.stack([rows[k][0] for k in ks])
         masks = tuple(SIDES[k] for k in ks)
         items.append([(piece, (masks, 0, 0))])
-        right, left = piece, piece
+        even, odd = piece, piece
         for n in range(1, 4):
-            right = move(right, "z", shift(NZ, 1))
-            left = move(left, "z", shift(NZ, -1))
-            items[-1] += [(right, (masks, -n, 0)), (left, (masks, n, 0))]
-        right = move(right[:, :half], "z", shift(NZ, 1))
-        left = move(left[:, half:], "z", shift(NZ, -1))
-        items[-1] += [(right, (masks, 4, 0)), (left, (masks, 4, half))]
+            even, odd = (move(odd, "z", link(NZ, 0)), move(even, "z", link(NZ, 1)))
+            items[-1] += [(even, (masks, n, 0)), (odd, (masks, -n, 0))]
+        even, odd = (move(odd[:, :half], "z", link(NZ, 0)), move(even[:, half:], "z", link(NZ, 1)))
+        items[-1] += [(even, (masks, 4, 0)), (odd, (masks, -4, half))]
     a, b = items
     out = place(None, width, a[:5] + b[:3])
     out = place(out, width, a[5:7] + b[3:5])

time: 124 us -> 123 us (level)
  starting transfers between devices: 60.8 us -> 58.4 us
    ppermute x38, starting transfers between devices: 45.4 us -> 43 us  [move(): return lax.ppermute(value, axis, to)]
where the time goes in v4:
time: 123 us; the launch traced here: 122 us
  starting transfers between devices  58.4 us (47%)
  waiting for transfers between devices  48 us (39%)
  Pallas kernels  12 us (10%)
  matrix products  2.55 us (2%)
    ppermute x38, waiting for transfers between devices, move(): return lax.ppermute(value, axis, to)  47.7 us
    ppermute x38, starting transfers between devices, move(): return lax.ppermute(value, axis, to)  43 us
    all_to_all x1, starting transfers between devices, body(): own = lax.all_to_all(mine, 'z', 0, 0, tiled=True)  8.48 us
    all_to_all x1, starting transfers between devices, body(): xz = lax.all_to_all(sides, 'z', 0, 0, tiled=True)  6.93 us
    pallas_call x1, Pallas kernels, body(): pl.pallas_call(functools.partial(newton_kernel, math.sqrt(2048)), out_sha...  5.57 us
    pallas_call x4, Pallas kernels, place(): pl.pallas_call(functools.partial(place_kernel, places, n, int(aliased)),...  3.82 us
    dot_general x5, matrix products, gram_of(): lax.dot_general(rows, rows, (((0,), (0,)), ((), ())), preferred_element_t...  2.55 us
  transfers between devices with their start and end apart: 40, of which 22 were waited for; matrix products, arithmetic and copies ran while one was open for 2% of the time, Pallas kernels for 3%

profile of v4, /device:TPU:8, one launch (start us, length us, event | category | flops | bytes accessed | tf_op | source)
XLA Modules:
  0.0 122.3 jit_solution(13484541318099283839)
XLA Ops:
  0.0 1.9 %pack.1 = (bf16[8,64,128]{2,1,0:T(8,128)(2,1)S(1)}, bf16[8,64,128]{2,1,0:T(8,128)(2,1)S(1)}, bf16[8,64,128]{2,1,0:T(8,128)(2,1)S(1)}, bf16[8,64,128]{2,1,0:T(8,128)(2,1)S(1)}, bf16[8,16,768]{2,1,0:T(8,128)(2,1)}) custom-call(s32[1,32]{1,0:T(1,128)} %count_hbm.1, bf16[4,8,64,128]{3,2,1,0:T(8,128)(2,1)} %bitcast.21, bf16[4,8,8,16,768]{4,3,2,1,0:T(8,128)(2,1)} %bitcast.20), custom_call_target="tpu_custom_call" | custom-call | tf_op jit(solution)/shard_map/pack/pallas_call | solution.py:159
  1.9 8.5 %all-to-all-start.1 = ((bf16[8,16,768]{2,1,0:T(8,128)(2,1)}), bf16[8,16,768]{2,1,0:T(8,128)(2,1)S(1)}, u32[]{:S(2)}, u32[]{:S(2)}) async-start(bf16[8,16,768]{2,1,0:T(8,128)(2,1)} %get-tuple-element.18), calls=%async_computation.1 | async-start | bytes 393216 | tf_op jit(solution)/shard_map/all_to_all | solution.py:178
  10.9 2.4 %collective-permute-start.1 = (bf16[8,64,128]{2,1,0:T(8,128)(2,1)S(1)}, bf16[8,64,128]{2,1,0:T(8,128)(2,1)S(1)}, u32[]{:S(2)}, u32[]{:S(2)}) collective-permute-start(bf16[8,64,128]{2,1,0:T(8,128)(2,1)S(1)} %get-tuple-element.16), channel_id=1, source_target_pairs={{0,24},{8,16},{16,8},{24,0},{1,25},{9,17},{17,9},{25,1},{2,26},{10... | collective-permute-start | bytes 393224 | tf_op jit(solution)/shard_map/ppermute | solution.py:152
  13.3 1.2 %collective-permute-start.2 = (bf16[8,64,128]{2,1,0:T(8,128)(2,1)S(1)}, bf16[8,64,128]{2,1,0:T(8,128)(2,1)S(1)}, u32[]{:S(2)}, u32[]{:S(2)}) collective-permute-start(bf16[8,64,128]{2,1,0:T(8,128)(2,1)S(1)} %get-tuple-element.17), channel_id=1, source_target_pairs={{0,16},{8,24},{16,0},{24,8},{1,17},{9,25},{17,1},{25,9},{2,18},{10... | collective-permute-start | bytes 393224 | tf_op jit(solution)/shard_map/ppermute | solution.py:152
  14.5 1.1 collective-permute-done
  15.6 2.9 %collective-permute-done.1 = bf16[8,64,128]{2,1,0:T(8,128)(2,1)S(1)} collective-permute-done((bf16[8,64,128]{2,1,0:T(8,128)(2,1)S(1)}, bf16[8,64,128]{2,1,0:T(8,128)(2,1)S(1)}, u32[]{:S(2)}, u32[]{:S(2)}) %collective-permute-start.1) | collective-permute-done | bytes 131104 | tf_op jit(solution)/shard_map/ppermute | solution.py:152
  18.5 1.3 %collective-permute-done.2 = bf16[8,64,128]{2,1,0:T(8,128)(2,1)S(1)} collective-permute-done((bf16[8,64,128]{2,1,0:T(8,128)(2,1)S(1)}, bf16[8,64,128]{2,1,0:T(8,128)(2,1)S(1)}, u32[]{:S(2)}, u32[]{:S(2)}) %collective-permute-start.2) | collective-permute-done | bytes 131104 | tf_op jit(solution)/shard_map/ppermute | solution.py:152
  19.7 0.9 pad_maximum_fusion
  20.9 6.9 %all-to-all-start = ((bf16[8,4,64,128]{3,2,1,0:T(8,128)(2,1)}), bf16[8,4,64,128]{3,2,1,0:T(8,128)(2,1)S(1)}, u32[]{:S(2)}, u32[]{:S(2)}) async-start(bf16[8,4,64,128]{3,2,1,0:T(8,128)(2,1)} %pad_maximum_fusion), calls=%async_computation | async-start | bytes 1048576 | tf_op jit(solution)/shard_map/all_to_all | solution.py:179
  27.8 2.8 %collective-permute-start.4 = (bf16[8,16,768]{2,1,0:T(8,128)(2,1)S(1)}, bf16[8,16,768]{2,1,0:T(8,128)(2,1)S(1)}, u32[]{:S(2)}, u32[]{:S(2)}) collective-permute-start(bf16[8,16,768]{2,1,0:T(8,128)(2,1)S(1)} %all-to-all-done.1.refs_0_), channel_id=1, source_target_pairs={{0,6},{2,4},{4,2},{6,0},{1,7},{3,5},{5,3},{7,1},{8,14},{10,12},{12... | collective-permute-start | bytes 589832 | tf_op jit(solution)/shard_map/ppermute | solution.py:152
  30.8 3.9 %collective-permute-done.4.refs_2_ = bf16[8,16,768]{2,1,0:T(8,128)(2,1)S(1)} collective-permute-done((bf16[8,16,768]{2,1,0:T(8,128)(2,1)S(1)}, bf16[8,16,768]{2,1,0:T(8,128)(2,1)S(1)}, u32[]{:S(2)}, u32[]{:S(2)}) %collective-permute-start.4) | collective-permute-done | bytes 196640 | tf_op jit(solution)/shard_map/ppermute | solution.py:152
  35.1 2.2 %collective-permute-done.3.refs_1_ = bf16[8,16,768]{2,1,0:T(8,128)(2,1)S(1)} collective-permute-done((bf16[8,16,768]{2,1,0:T(8,128)(2,1)S(1)}, bf16[8,16,768]{2,1,0:T(8,128)(2,1)S(1)}, u32[]{:S(2)}, u32[]{:S(2)}) %collective-permute-start.3) | collective-permute-done | bytes 196640 | tf_op jit(solution)/shard_map/ppermute | solution.py:152
  38.2 1.2 collective-permute-done.5.refs_3_
  39.4 3.8 %collective-permute-done.6.refs_4_ = bf16[4,16,768]{2,1,0:T(8,128)(2,1)S(1)} collective-permute-done((bf16[4,16,768]{2,1,0:T(8,128)(2,1)S(1)}, bf16[4,16,768]{2,1,0:T(8,128)(2,1)S(1)}, u32[]{:S(2)}, u32[]{:S(2)}) %collective-permute-start.6) | collective-permute-done | bytes 98336 | tf_op jit(solution)/shard_map/ppermute | solution.py:152
  43.2 1.3 %collective-permute-done.11.refs_9_ = bf16[4,16,768]{2,1,0:T(8,128)(2,1)S(1)} collective-permute-done((bf16[4,16,768]{2,1,0:T(8,128)(2,1)S(1)}, bf16[4,16,768]{2,1,0:T(8,128)(2,1)S(1)}, u32[]{:S(2)}, u32[]{:S(2)}) %collective-permute-start.11) | collective-permute-done | bytes 98336 | tf_op jit(solution)/shard_map/ppermute | solution.py:152
  44.5 0.7 grad.1.grad_ref
  45.6 2.1 %collective-permute-start.13 = (bf16[256,768]{1,0:T(8,128)(2,1)S(1)}, bf16[256,768]{1,0:T(8,128)(2,1)S(1)}, u32[]{:S(2)}, u32[]{:S(2)}) collective-permute-start(bf16[256,768]{1,0:T(8,128)(2,1)S(1)} %grad.1.grad_ref), channel_id=1, source_target_pairs={{0,6},{2,4},{4,2},{6,0},{1,7},{3,5},{5,3},{7,1},{8,14},{10,12},{12... | collective-permute-start | bytes 1179656 | tf_op jit(solution)/shard_map/ppermute | solution.py:152
  47.7 8.7 %collective-permute-done.12 = bf16[256,768]{1,0:T(8,128)(2,1)S(1)} collective-permute-done((bf16[256,768]{1,0:T(8,128)(2,1)S(1)}, bf16[256,768]{1,0:T(8,128)(2,1)S(1)}, u32[]{:S(2)}, u32[]{:S(2)}) %collective-permute-start.12) | collective-permute-done | bytes 393248 | tf_op jit(solution)/shard_map/ppermute | solution.py:152
  56.4 0.5 fusion
  57.0 0.8 collective-permute-done.13
  57.8 0.5 fusion.1
  58.3 0.5 add_add_fusion.1
  58.9 0.5 collective-permute-start.14
  59.5 1.0 collective-permute-start.15
  60.4 5.9 %collective-permute-done.14 = bf16[128,768]{1,0:T(8,128)(2,1)S(1)} collective-permute-done((bf16[128,768]{1,0:T(8,128)(2,1)S(1)}, bf16[128,768]{1,0:T(8,128)(2,1)S(1)}, u32[]{:S(2)}, u32[]{:S(2)}) %collective-permute-start.14) | collective-permute-done | bytes 196640 | tf_op jit(solution)/shard_map/ppermute | solution.py:152
  66.3 1.5 %collective-permute-done.15 = bf16[128,768]{1,0:T(8,128)(2,1)S(1)} collective-permute-done((bf16[128,768]{1,0:T(8,128)(2,1)S(1)}, bf16[128,768]{1,0:T(8,128)(2,1)S(1)}, u32[]{:S(2)}, u32[]{:S(2)}) %collective-permute-start.15) | collective-permute-done | bytes 196640 | tf_op jit(solution)/shard_map/ppermute | solution.py:152
  68.3 0.5 add_add_fusion.mine_ref
  69.2 5.6 %newton.1 = (bf16[1,64,768]{2,1,0:T(8,128)(2,1)S(1)}, bf16[1,64,768]{2,1,0:T(8,128)(2,1)S(1)}, bf16[1,64,768]{2,1,0:T(8,128)(2,1)S(1)}, bf16[1,64,768]{2,1,0:T(8,128)(2,1)S(1)}) custom-call(f32[768,768]{1,0:T(8,128)S(1)} %add_add_fusion.mine_ref, f32[768,768]{1,0:T(8,128)S(1)} %collective-permute-done.16.other_ref, ...), custom_call_target="tpu_custom_call" | custom-call | tf_op jit(solution)/shard_map/newton/pallas_call | solution.py:210
  74.8 1.2 collective-permute-start.19
  76.0 2.7 %collective-permute-start.20 = (bf16[1,64,768]{2,1,0:T(8,128)(2,1)S(1)}, bf16[1,64,768]{2,1,0:T(8,128)(2,1)S(1)}, u32[]{:S(2)}, u32[]{:S(2)}) collective-permute-start(bf16[1,64,768]{2,1,0:T(8,128)(2,1)S(1)} %get-tuple-element.20), channel_id=1, source_target_pairs={{0,16},{8,24},{16,0},{24,8},{1,17},{9,25},{17,1},{25,9},{2,18},{10... | collective-permute-start | bytes 294920 | tf_op jit(solution)/shard_map/ppermute | solution.py:152
  79.0 4.7 %collective-permute-done.29 = bf16[1,64,768]{2,1,0:T(8,128)(2,1)S(1)} collective-permute-done((bf16[1,64,768]{2,1,0:T(8,128)(2,1)S(1)}, bf16[1,64,768]{2,1,0:T(8,128)(2,1)S(1)}, u32[]{:S(2)}, u32[]{:S(2)}) %collective-permute-start.29) | collective-permute-done | bytes 98336 | tf_op jit(solution)/shard_map/ppermute | solution.py:152
  83.7 2.1 %collective-permute-start.34 = (bf16[2,64,768]{2,1,0:T(8,128)(2,1)S(1)}, bf16[2,64,768]{2,1,0:T(8,128)(2,1)S(1)}, u32[]{:S(2)}, u32[]{:S(2)}) collective-permute-start(bf16[2,64,768]{2,1,0:T(8,128)(2,1)S(1)} %constant_dynamic-update-slice_fusion.2.refs_0_), channel_id=1, source_target_pairs={{0,32},{32,0},{64,96},{96,64},{128,160},{160,128},{192,224},{224,1... | collective-permute-start | bytes 589832 | tf_op jit(solution)/shard_map/ppermute | solution.py:152
  85.8 2.7 %collective-permute-start.30 = (bf16[2,64,768]{2,1,0:T(8,128)(2,1)S(1)}, bf16[2,64,768]{2,1,0:T(8,128)(2,1)S(1)}, u32[]{:S(2)}, u32[]{:S(2)}) collective-permute-start(bf16[2,64,768]{2,1,0:T(8,128)(2,1)S(1)} %constant_dynamic-update-slice_fusion.2.refs_0_), channel_id=1, source_target_pairs={{0,224},{32,64},{64,32},{96,128},{128,96},{160,192},{192,160},{224... | collective-permute-start | bytes 589832 | tf_op jit(solution)/shard_map/ppermute | solution.py:152
  88.9 2.7 %collective-permute-start.21 = (bf16[2,64,768]{2,1,0:T(8,128)(2,1)S(1)}, bf16[2,64,768]{2,1,0:T(8,128)(2,1)S(1)}, u32[]{:S(2)}, u32[]{:S(2)}) collective-permute-start(bf16[2,64,768]{2,1,0:T(8,128)(2,1)S(1)} %constant_dynamic-update-slice_fusion.refs_5_), channel_id=1, source_target_pairs={{0,224},{32,64},{64,32},{96,128},{128,96},{160,192},{192,160},{224... | collective-permute-start | bytes 589832 | tf_op jit(solution)/shard_map/ppermute | solution.py:152
  91.5 3.2 %collective-permute-start.35 = (bf16[2,64,768]{2,1,0:T(8,128)(2,1)S(1)}, bf16[2,64,768]{2,1,0:T(8,128)(2,1)S(1)}, u32[]{:S(2)}, u32[]{:S(2)}) collective-permute-start(bf16[2,64,768]{2,1,0:T(8,128)(2,1)S(1)} %collective-permute-done.34.refs_1_), channel_id=1, source_target_pairs={{0,224},{32,64},{64,32},{96,128},{128,96},{160,192},{192,160},{224... | collective-permute-start | bytes 589832 | tf_op jit(solution)/shard_map/ppermute | solution.py:152
  95.3 3.2 %collective-permute-start.26 = (bf16[2,64,768]{2,1,0:T(8,128)(2,1)S(1)}, bf16[2,64,768]{2,1,0:T(8,128)(2,1)S(1)}, u32[]{:S(2)}, u32[]{:S(2)}) collective-permute-start(bf16[2,64,768]{2,1,0:T(8,128)(2,1)S(1)} %collective-permute-done.25.refs_6_), channel_id=1, source_target_pairs={{0,224},{32,64},{64,32},{96,128},{128,96},{160,192},{192,160},{224... | collective-permute-start | bytes 589832 | tf_op jit(solution)/shard_map/ppermute | solution.py:152
  99.2 3.7 %collective-permute-done.35.refs_4_ = bf16[2,64,768]{2,1,0:T(8,128)(2,1)S(1)} collective-permute-done((bf16[2,64,768]{2,1,0:T(8,128)(2,1)S(1)}, bf16[2,64,768]{2,1,0:T(8,128)(2,1)S(1)}, u32[]{:S(2)}, u32[]{:S(2)}) %collective-permute-start.35) | collective-permute-done | bytes 196640 | tf_op jit(solution)/shard_map/ppermute | solution.py:152
  102.9 2.8 %collective-permute-start.32 = (bf16[2,64,768]{2,1,0:T(8,128)(2,1)S(1)}, bf16[2,64,768]{2,1,0:T(8,128)(2,1)S(1)}, u32[]{:S(2)}, u32[]{:S(2)}) collective-permute-start(bf16[2,64,768]{2,1,0:T(8,128)(2,1)S(1)} %collective-permute-done.31.refs_3_), channel_id=1, source_target_pairs={{0,224},{32,64},{64,32},{96,128},{128,96},{160,192},{192,160},{224... | collective-permute-start | bytes 589832 | tf_op jit(solution)/shard_map/ppermute | solution.py:152
  105.7 1.4 %collective-permute-done.26.refs_3_ = bf16[2,64,768]{2,1,0:T(8,128)(2,1)S(1)} collective-permute-done((bf16[2,64,768]{2,1,0:T(8,128)(2,1)S(1)}, bf16[2,64,768]{2,1,0:T(8,128)(2,1)S(1)}, u32[]{:S(2)}, u32[]{:S(2)}) %collective-permute-start.26) | collective-permute-done | bytes 196640 | tf_op jit(solution)/shard_map/ppermute | solution.py:152
  107.1 2.8 %collective-permute-start.23 = (bf16[2,64,768]{2,1,0:T(8,128)(2,1)S(1)}, bf16[2,64,768]{2,1,0:T(8,128)(2,1)S(1)}, u32[]{:S(2)}, u32[]{:S(2)}) collective-permute-start(bf16[2,64,768]{2,1,0:T(8,128)(2,1)S(1)} %collective-permute-done.22.refs_2_), channel_id=1, source_target_pairs={{0,224},{32,64},{64,32},{96,128},{128,96},{160,192},{192,160},{224... | collective-permute-start | bytes 589832 | tf_op jit(solution)/shard_map/ppermute | solution.py:152
  109.9 1.1 collective-permute-done.36.refs_0_
  111.0 2.6 %collective-permute-start.37 = (bf16[2,32,768]{2,1,0:T(8,128)(2,1)S(1)}, bf16[2,32,768]{2,1,0:T(8,128)(2,1)S(1)}, u32[]{:S(2)}, u32[]{:S(2)}) collective-permute-start(bf16[2,32,768]{2,1,0:T(8,128)(2,1)S(1)} %slice.39), channel_id=1, source_target_pairs={{0,224},{32,64},{64,32},{96,128},{128,96},{160,192},{192,160},{224... | collective-permute-start | bytes 294920 | tf_op jit(solution)/shard_map/ppermute | solution.py:152
  114.1 2.6 %collective-permute-start.28 = (bf16[2,32,768]{2,1,0:T(8,128)(2,1)S(1)}, bf16[2,32,768]{2,1,0:T(8,128)(2,1)S(1)}, u32[]{:S(2)}, u32[]{:S(2)}) collective-permute-start(bf16[2,32,768]{2,1,0:T(8,128)(2,1)S(1)} %slice.37), channel_id=1, source_target_pairs={{0,224},{32,64},{64,32},{96,128},{128,96},{160,192},{192,160},{224... | collective-permute-start | bytes 294920 | tf_op jit(solution)/shard_map/ppermute | solution.py:152
  117.2 1.3 %shard_map.37.refs_4_ = bf16[4,8,64,768]{3,2,1,0:T(8,128)(2,1)} custom-call(bf16[2,64,768]{2,1,0:T(8,128)(2,1)S(1)} %constant_dynamic-update-slice_fusion.2.refs_0_, bf16[2,64,768]{2,1,0:T(8,128)(2,1)S(1)} %collective-permute-done.34.refs_1_, bf16[2,64,768]{2,1,0:T(8,128)(2,1)S(1)} %collective-permute-done.30.refs_2_, ...), custom_call_target="tpu_custom_call" | custom-call | tf_op jit(solution)/shard_map/pallas_call | solution.py:140
  118.5 1.0 shard_map.38.refs_4_
  119.5 0.9 shard_map.39.refs_2_
  120.4 1.0 collective-permute-done.24.refs_0_
  121.4 0.7 shard_map.40
  (57 shorter events, 6.8 us)
Async XLA Ops:
  1.9 18.9 %all-to-all-start.1 = ((bf16[8,16,768]{2,1,0:T(8,128)(2,1)}), bf16[8,16,768]{2,1,0:T(8,128)(2,1)S(1)}, u32[]{:S(2)}, u32[]{:S(2)}) async-start(bf16[8,16,768]{2,1,0:T(8,128)(2,1)} %get-tuple-element.18), calls=%async_computation.1 | async-start | bytes 393216 | tf_op jit(solution)/shard_map/all_to_all | solution.py:178
  10.4 5.2 %collective-permute-start = (bf16[8,64,128]{2,1,0:T(8,128)(2,1)S(1)}, bf16[8,64,128]{2,1,0:T(8,128)(2,1)S(1)}, u32[]{:S(2)}, u32[]{:S(2)}) collective-permute-start(bf16[8,64,128]{2,1,0:T(8,128)(2,1)S(1)} %get-tuple-element.15), channel_id=1, source_target_pairs={{0,8},{8,0},{16,24},{24,16},{1,9},{9,1},{17,25},{25,17},{2,10},{10... | collective-permute-start | bytes 393224 | tf_op jit(solution)/shard_map/ppermute | solution.py:152
  10.9 7.6 %collective-permute-start.1 = (bf16[8,64,128]{2,1,0:T(8,128)(2,1)S(1)}, bf16[8,64,128]{2,1,0:T(8,128)(2,1)S(1)}, u32[]{:S(2)}, u32[]{:S(2)}) collective-permute-start(bf16[8,64,128]{2,1,0:T(8,128)(2,1)S(1)} %get-tuple-element.16), channel_id=1, source_target_pairs={{0,24},{8,16},{16,8},{24,0},{1,25},{9,17},{17,9},{25,1},{2,26},{10... | collective-permute-start | bytes 393224 | tf_op jit(solution)/shard_map/ppermute | solution.py:152
  13.3 6.5 %collective-permute-start.2 = (bf16[8,64,128]{2,1,0:T(8,128)(2,1)S(1)}, bf16[8,64,128]{2,1,0:T(8,128)(2,1)S(1)}, u32[]{:S(2)}, u32[]{:S(2)}) collective-permute-start(bf16[8,64,128]{2,1,0:T(8,128)(2,1)S(1)} %get-tuple-element.17), channel_id=1, source_target_pairs={{0,16},{8,24},{16,0},{24,8},{1,17},{9,25},{17,1},{25,9},{2,18},{10... | collective-permute-start | bytes 393224 | tf_op jit(solution)/shard_map/ppermute | solution.py:152
  20.9 23.6 %all-to-all-start = ((bf16[8,4,64,128]{3,2,1,0:T(8,128)(2,1)}), bf16[8,4,64,128]{3,2,1,0:T(8,128)(2,1)S(1)}, u32[]{:S(2)}, u32[]{:S(2)}) async-start(bf16[8,4,64,128]{3,2,1,0:T(8,128)(2,1)} %pad_maximum_fusion), calls=%async_computation | async-start | bytes 1048576 | tf_op jit(solution)/shard_map/all_to_all | solution.py:179
  27.8 6.9 %collective-permute-start.4 = (bf16[8,16,768]{2,1,0:T(8,128)(2,1)S(1)}, bf16[8,16,768]{2,1,0:T(8,128)(2,1)S(1)}, u32[]{:S(2)}, u32[]{:S(2)}) collective-permute-start(bf16[8,16,768]{2,1,0:T(8,128)(2,1)S(1)} %all-to-all-done.1.refs_0_), channel_id=1, source_target_pairs={{0,6},{2,4},{4,2},{6,0},{1,7},{3,5},{5,3},{7,1},{8,14},{10,12},{12... | collective-permute-start | bytes 589832 | tf_op jit(solution)/shard_map/ppermute | solution.py:152
  30.6 6.7 %collective-permute-start.3 = (bf16[8,16,768]{2,1,0:T(8,128)(2,1)S(1)}, bf16[8,16,768]{2,1,0:T(8,128)(2,1)S(1)}, u32[]{:S(2)}, u32[]{:S(2)}) collective-permute-start(bf16[8,16,768]{2,1,0:T(8,128)(2,1)S(1)} %all-to-all-done.1.refs_0_), channel_id=1, source_target_pairs={{0,2},{2,0},{4,6},{6,4},{1,3},{3,1},{5,7},{7,5},{8,10},{10,8},{12,... | collective-permute-start | bytes 589832 | tf_op jit(solution)/shard_map/ppermute | solution.py:152
  30.8 12.4 %collective-permute-start.7 = (bf16[8,16,768]{2,1,0:T(8,128)(2,1)S(1)}, bf16[8,16,768]{2,1,0:T(8,128)(2,1)S(1)}, u32[]{:S(2)}, u32[]{:S(2)}) collective-permute-start(bf16[8,16,768]{2,1,0:T(8,128)(2,1)S(1)} %all-to-all-done.1.refs_0_), channel_id=1, source_target_pairs={{0,1},{1,0},{2,3},{3,2},{4,5},{5,4},{6,7},{7,6},{8,9},{9,8},{10,11... | collective-permute-start | bytes 589832 | tf_op jit(solution)/shard_map/ppermute | solution.py:152
  34.7 4.7 %collective-permute-start.5 = (bf16[4,16,768]{2,1,0:T(8,128)(2,1)S(1)}, bf16[4,16,768]{2,1,0:T(8,128)(2,1)S(1)}, u32[]{:S(2)}, u32[]{:S(2)}) collective-permute-start(bf16[4,16,768]{2,1,0:T(8,128)(2,1)S(1)} %slice.32), channel_id=1, source_target_pairs={{0,2},{2,0},{4,6},{6,4},{1,3},{3,1},{5,7},{7,5},{8,10},{10,8},{12,... | collective-permute-start | bytes 294920 | tf_op jit(solution)/shard_map/ppermute | solution.py:152
  37.3 5.9 %collective-permute-start.6 = (bf16[4,16,768]{2,1,0:T(8,128)(2,1)S(1)}, bf16[4,16,768]{2,1,0:T(8,128)(2,1)S(1)}, u32[]{:S(2)}, u32[]{:S(2)}) collective-permute-start(bf16[4,16,768]{2,1,0:T(8,128)(2,1)S(1)} %slice.33), channel_id=1, source_target_pairs={{0,6},{2,4},{4,2},{6,0},{1,7},{3,5},{5,3},{7,1},{8,14},{10,12},{12... | collective-permute-start | bytes 294920 | tf_op jit(solution)/shard_map/ppermute | solution.py:152
  37.7 5.5 %collective-permute-start.9 = (bf16[8,16,768]{2,1,0:T(8,128)(2,1)S(1)}, bf16[8,16,768]{2,1,0:T(8,128)(2,1)S(1)}, u32[]{:S(2)}, u32[]{:S(2)}) collective-permute-start(bf16[8,16,768]{2,1,0:T(8,128)(2,1)S(1)} %collective-permute-done.4.refs_2_), channel_id=1, source_target_pairs={{0,1},{1,0},{2,3},{3,2},{4,5},{5,4},{6,7},{7,6},{8,9},{9,8},{10,11... | collective-permute-start | bytes 589832 | tf_op jit(solution)/shard_map/ppermute | solution.py:152
  37.7 6.8 %collective-permute-start.8 = (bf16[8,16,768]{2,1,0:T(8,128)(2,1)S(1)}, bf16[8,16,768]{2,1,0:T(8,128)(2,1)S(1)}, u32[]{:S(2)}, u32[]{:S(2)}) collective-permute-start(bf16[8,16,768]{2,1,0:T(8,128)(2,1)S(1)} %collective-permute-done.3.refs_1_), channel_id=1, source_target_pairs={{0,1},{1,0},{2,3},{3,2},{4,5},{5,4},{6,7},{7,6},{8,9},{9,8},{10,11... | collective-permute-start | bytes 589832 | tf_op jit(solution)/shard_map/ppermute | solution.py:152
  39.4 3.8 %collective-permute-start.10 = (bf16[4,16,768]{2,1,0:T(8,128)(2,1)S(1)}, bf16[4,16,768]{2,1,0:T(8,128)(2,1)S(1)}, u32[]{:S(2)}, u32[]{:S(2)}) collective-permute-start(bf16[4,16,768]{2,1,0:T(8,128)(2,1)S(1)} %collective-permute-done.5.refs_3_), channel_id=1, source_target_pairs={{0,1},{1,0},{2,3},{3,2},{4,5},{5,4},{6,7},{7,6},{8,9},{9,8},{10,11... | collective-permute-start | bytes 294920 | tf_op jit(solution)/shard_map/ppermute | solution.py:152
  43.2 1.3 %collective-permute-start.11 = (bf16[4,16,768]{2,1,0:T(8,128)(2,1)S(1)}, bf16[4,16,768]{2,1,0:T(8,128)(2,1)S(1)}, u32[]{:S(2)}, u32[]{:S(2)}) collective-permute-start(bf16[4,16,768]{2,1,0:T(8,128)(2,1)S(1)} %collective-permute-done.6.refs_4_), channel_id=1, source_target_pairs={{0,1},{1,0},{2,3},{3,2},{4,5},{5,4},{6,7},{7,6},{8,9},{9,8},{10,11... | collective-permute-start | bytes 294920 | tf_op jit(solution)/shard_map/ppermute | solution.py:152
  45.2 11.3 %collective-permute-start.12 = (bf16[256,768]{1,0:T(8,128)(2,1)S(1)}, bf16[256,768]{1,0:T(8,128)(2,1)S(1)}, u32[]{:S(2)}, u32[]{:S(2)}) collective-permute-start(bf16[256,768]{1,0:T(8,128)(2,1)S(1)} %grad.1.grad_ref), channel_id=1, source_target_pairs={{0,2},{2,0},{4,6},{6,4},{1,3},{3,1},{5,7},{7,5},{8,10},{10,8},{12,... | collective-permute-start | bytes 1179656 | tf_op jit(solution)/shard_map/ppermute | solution.py:152
  45.6 12.1 %collective-permute-start.13 = (bf16[256,768]{1,0:T(8,128)(2,1)S(1)}, bf16[256,768]{1,0:T(8,128)(2,1)S(1)}, u32[]{:S(2)}, u32[]{:S(2)}) collective-permute-start(bf16[256,768]{1,0:T(8,128)(2,1)S(1)} %grad.1.grad_ref), channel_id=1, source_target_pairs={{0,6},{2,4},{4,2},{6,0},{1,7},{3,5},{5,3},{7,1},{8,14},{10,12},{12... | collective-permute-start | bytes 1179656 | tf_op jit(solution)/shard_map/ppermute | solution.py:152
  58.8 10.4 %collective-permute-start.16 = (f32[768,768]{1,0:T(8,128)S(1)}, f32[768,768]{1,0:T(8,128)S(1)}, u32[]{:S(2)}, u32[]{:S(2)}) collective-permute-start(f32[768,768]{1,0:T(8,128)S(1)} %add_add_fusion.1), channel_id=1, source_target_pairs={{0,1},{1,0},{2,3},{3,2},{4,5},{5,4},{6,7},{7,6},{8,9},{9,8},{10,11... | collective-permute-start | bytes 7077896 | tf_op jit(solution)/shard_map/ppermute | solution.py:152
  58.9 7.4 %collective-permute-start.14 = (bf16[128,768]{1,0:T(8,128)(2,1)S(1)}, bf16[128,768]{1,0:T(8,128)(2,1)S(1)}, u32[]{:S(2)}, u32[]{:S(2)}) collective-permute-start(bf16[128,768]{1,0:T(8,128)(2,1)S(1)} %slice.34), channel_id=1, source_target_pairs={{0,2},{2,0},{4,6},{6,4},{1,3},{3,1},{5,7},{7,5},{8,10},{10,8},{12,... | collective-permute-start | bytes 589832 | tf_op jit(solution)/shard_map/ppermute | solution.py:152
  59.5 8.3 %collective-permute-start.15 = (bf16[128,768]{1,0:T(8,128)(2,1)S(1)}, bf16[128,768]{1,0:T(8,128)(2,1)S(1)}, u32[]{:S(2)}, u32[]{:S(2)}) collective-permute-start(bf16[128,768]{1,0:T(8,128)(2,1)S(1)} %slice.35), channel_id=1, source_target_pairs={{0,6},{2,4},{4,2},{6,0},{1,7},{3,5},{5,3},{7,1},{8,14},{10,12},{12... | collective-permute-start | bytes 589832 | tf_op jit(solution)/shard_map/ppermute | solution.py:152
  66.3 2.5 %collective-permute-start.17 = (bf16[128,768]{1,0:T(8,128)(2,1)S(1)}, bf16[128,768]{1,0:T(8,128)(2,1)S(1)}, u32[]{:S(2)}, u32[]{:S(2)}) collective-permute-start(bf16[128,768]{1,0:T(8,128)(2,1)S(1)} %collective-permute-done.14), channel_id=1, source_target_pairs={{0,1},{1,0},{2,3},{3,2},{4,5},{5,4},{6,7},{7,6},{8,9},{9,8},{10,11... | collective-permute-start | bytes 589832 | tf_op jit(solution)/shard_map/ppermute | solution.py:152
  67.8 1.4 %collective-permute-start.18 = (bf16[128,768]{1,0:T(8,128)(2,1)S(1)}, bf16[128,768]{1,0:T(8,128)(2,1)S(1)}, u32[]{:S(2)}, u32[]{:S(2)}) collective-permute-start(bf16[128,768]{1,0:T(8,128)(2,1)S(1)} %collective-permute-done.15), channel_id=1, source_target_pairs={{0,1},{1,0},{2,3},{3,2},{4,5},{5,4},{6,7},{7,6},{8,9},{9,8},{10,11... | collective-permute-start | bytes 589832 | tf_op jit(solution)/shard_map/ppermute | solution.py:152
  74.8 13.7 %collective-permute-start.19 = (bf16[1,64,768]{2,1,0:T(8,128)(2,1)S(1)}, bf16[1,64,768]{2,1,0:T(8,128)(2,1)S(1)}, u32[]{:S(2)}, u32[]{:S(2)}) collective-permute-start(bf16[1,64,768]{2,1,0:T(8,128)(2,1)S(1)} %get-tuple-element.19), channel_id=1, source_target_pairs={{0,24},{8,16},{16,8},{24,0},{1,25},{9,17},{17,9},{25,1},{2,26},{10... | collective-permute-start | bytes 294920 | tf_op jit(solution)/shard_map/ppermute | solution.py:152
  76.0 12.5 %collective-permute-start.20 = (bf16[1,64,768]{2,1,0:T(8,128)(2,1)S(1)}, bf16[1,64,768]{2,1,0:T(8,128)(2,1)S(1)}, u32[]{:S(2)}, u32[]{:S(2)}) collective-permute-start(bf16[1,64,768]{2,1,0:T(8,128)(2,1)S(1)} %get-tuple-element.20), channel_id=1, source_target_pairs={{0,16},{8,24},{16,0},{24,8},{1,17},{9,25},{17,1},{25,9},{2,18},{10... | collective-permute-start | bytes 294920 | tf_op jit(solution)/shard_map/ppermute | solution.py:152
  78.7 5.0 %collective-permute-start.29 = (bf16[1,64,768]{2,1,0:T(8,128)(2,1)S(1)}, bf16[1,64,768]{2,1,0:T(8,128)(2,1)S(1)}, u32[]{:S(2)}, u32[]{:S(2)}) collective-permute-start(bf16[1,64,768]{2,1,0:T(8,128)(2,1)S(1)} %get-tuple-element.22), channel_id=1, source_target_pairs={{0,8},{8,0},{16,24},{24,16},{1,9},{9,1},{17,25},{25,17},{2,10},{10... | collective-permute-start | bytes 294920 | tf_op jit(solution)/shard_map/ppermute | solution.py:152
  83.7 7.8 %collective-permute-start.34 = (bf16[2,64,768]{2,1,0:T(8,128)(2,1)S(1)}, bf16[2,64,768]{2,1,0:T(8,128)(2,1)S(1)}, u32[]{:S(2)}, u32[]{:S(2)}) collective-permute-start(bf16[2,64,768]{2,1,0:T(8,128)(2,1)S(1)} %constant_dynamic-update-slice_fusion.2.refs_0_), channel_id=1, source_target_pairs={{0,32},{32,0},{64,96},{96,64},{128,160},{160,128},{192,224},{224,1... | collective-permute-start | bytes 589832 | tf_op jit(solution)/shard_map/ppermute | solution.py:152
  85.8 9.0 %collective-permute-start.30 = (bf16[2,64,768]{2,1,0:T(8,128)(2,1)S(1)}, bf16[2,64,768]{2,1,0:T(8,128)(2,1)S(1)}, u32[]{:S(2)}, u32[]{:S(2)}) collective-permute-start(bf16[2,64,768]{2,1,0:T(8,128)(2,1)S(1)} %constant_dynamic-update-slice_fusion.2.refs_0_), channel_id=1, source_target_pairs={{0,224},{32,64},{64,32},{96,128},{128,96},{160,192},{192,160},{224... | collective-permute-start | bytes 589832 | tf_op jit(solution)/shard_map/ppermute | solution.py:152
  88.5 6.8 %collective-permute-start.25 = (bf16[2,64,768]{2,1,0:T(8,128)(2,1)S(1)}, bf16[2,64,768]{2,1,0:T(8,128)(2,1)S(1)}, u32[]{:S(2)}, u32[]{:S(2)}) collective-permute-start(bf16[2,64,768]{2,1,0:T(8,128)(2,1)S(1)} %constant_dynamic-update-slice_fusion.refs_5_), channel_id=1, source_target_pairs={{0,32},{32,0},{64,96},{96,64},{128,160},{160,128},{192,224},{224,1... | collective-permute-start | bytes 589832 | tf_op jit(solution)/shard_map/ppermute | solution.py:152
  88.9 9.8 %collective-permute-start.21 = (bf16[2,64,768]{2,1,0:T(8,128)(2,1)S(1)}, bf16[2,64,768]{2,1,0:T(8,128)(2,1)S(1)}, u32[]{:S(2)}, u32[]{:S(2)}) collective-permute-start(bf16[2,64,768]{2,1,0:T(8,128)(2,1)S(1)} %constant_dynamic-update-slice_fusion.refs_5_), channel_id=1, source_target_pairs={{0,224},{32,64},{64,32},{96,128},{128,96},{160,192},{192,160},{224... | collective-permute-start | bytes 589832 | tf_op jit(solution)/shard_map/ppermute | solution.py:152
  91.5 11.4 %collective-permute-start.35 = (bf16[2,64,768]{2,1,0:T(8,128)(2,1)S(1)}, bf16[2,64,768]{2,1,0:T(8,128)(2,1)S(1)}, u32[]{:S(2)}, u32[]{:S(2)}) collective-permute-start(bf16[2,64,768]{2,1,0:T(8,128)(2,1)S(1)} %collective-permute-done.34.refs_1_), channel_id=1, source_target_pairs={{0,224},{32,64},{64,32},{96,128},{128,96},{160,192},{192,160},{224... | collective-permute-start | bytes 589832 | tf_op jit(solution)/shard_map/ppermute | solution.py:152
  94.8 8.1 %collective-permute-start.31 = (bf16[2,64,768]{2,1,0:T(8,128)(2,1)S(1)}, bf16[2,64,768]{2,1,0:T(8,128)(2,1)S(1)}, u32[]{:S(2)}, u32[]{:S(2)}) collective-permute-start(bf16[2,64,768]{2,1,0:T(8,128)(2,1)S(1)} %collective-permute-done.30.refs_2_), channel_id=1, source_target_pairs={{0,32},{32,0},{64,96},{96,64},{128,160},{160,128},{192,224},{224,1... | collective-permute-start | bytes 589832 | tf_op jit(solution)/shard_map/ppermute | solution.py:152
  95.3 11.8 %collective-permute-start.26 = (bf16[2,64,768]{2,1,0:T(8,128)(2,1)S(1)}, bf16[2,64,768]{2,1,0:T(8,128)(2,1)S(1)}, u32[]{:S(2)}, u32[]{:S(2)}) collective-permute-start(bf16[2,64,768]{2,1,0:T(8,128)(2,1)S(1)} %collective-permute-done.25.refs_6_), channel_id=1, source_target_pairs={{0,224},{32,64},{64,32},{96,128},{128,96},{160,192},{192,160},{224... | collective-permute-start | bytes 589832 | tf_op jit(solution)/shard_map/ppermute | solution.py:152
  98.7 8.4 %collective-permute-start.22 = (bf16[2,64,768]{2,1,0:T(8,128)(2,1)S(1)}, bf16[2,64,768]{2,1,0:T(8,128)(2,1)S(1)}, u32[]{:S(2)}, u32[]{:S(2)}) collective-permute-start(bf16[2,64,768]{2,1,0:T(8,128)(2,1)S(1)} %collective-permute-done.21.refs_7_), channel_id=1, source_target_pairs={{0,32},{32,0},{64,96},{96,64},{128,160},{160,128},{192,224},{224,1... | collective-permute-start | bytes 589832 | tf_op jit(solution)/shard_map/ppermute | solution.py:152
  102.9 8.1 %collective-permute-start.36 = (bf16[2,64,768]{2,1,0:T(8,128)(2,1)S(1)}, bf16[2,64,768]{2,1,0:T(8,128)(2,1)S(1)}, u32[]{:S(2)}, u32[]{:S(2)}) collective-permute-start(bf16[2,64,768]{2,1,0:T(8,128)(2,1)S(1)} %collective-permute-done.35.refs_4_), channel_id=1, source_target_pairs={{0,32},{32,0},{64,96},{96,64},{128,160},{160,128},{192,224},{224,1... | collective-permute-start | bytes 589832 | tf_op jit(solution)/shard_map/ppermute | solution.py:152
  102.9 10.6 %collective-permute-start.32 = (bf16[2,64,768]{2,1,0:T(8,128)(2,1)S(1)}, bf16[2,64,768]{2,1,0:T(8,128)(2,1)S(1)}, u32[]{:S(2)}, u32[]{:S(2)}) collective-permute-start(bf16[2,64,768]{2,1,0:T(8,128)(2,1)S(1)} %collective-permute-done.31.refs_3_), channel_id=1, source_target_pairs={{0,224},{32,64},{64,32},{96,128},{128,96},{160,192},{192,160},{224... | collective-permute-start | bytes 589832 | tf_op jit(solution)/shard_map/ppermute | solution.py:152
  107.1 7.0 %collective-permute-start.27 = (bf16[2,64,768]{2,1,0:T(8,128)(2,1)S(1)}, bf16[2,64,768]{2,1,0:T(8,128)(2,1)S(1)}, u32[]{:S(2)}, u32[]{:S(2)}) collective-permute-start(bf16[2,64,768]{2,1,0:T(8,128)(2,1)S(1)} %collective-permute-done.26.refs_3_), channel_id=1, source_target_pairs={{0,32},{32,0},{64,96},{96,64},{128,160},{160,128},{192,224},{224,1... | collective-permute-start | bytes 589832 | tf_op jit(solution)/shard_map/ppermute | solution.py:152
  107.1 9.6 %collective-permute-start.23 = (bf16[2,64,768]{2,1,0:T(8,128)(2,1)S(1)}, bf16[2,64,768]{2,1,0:T(8,128)(2,1)S(1)}, u32[]{:S(2)}, u32[]{:S(2)}) collective-permute-start(bf16[2,64,768]{2,1,0:T(8,128)(2,1)S(1)} %collective-permute-done.22.refs_2_), channel_id=1, source_target_pairs={{0,224},{32,64},{64,32},{96,128},{128,96},{160,192},{192,160},{224... | collective-permute-start | bytes 589832 | tf_op jit(solution)/shard_map/ppermute | solution.py:152
  111.0 8.5 %collective-permute-start.37 = (bf16[2,32,768]{2,1,0:T(8,128)(2,1)S(1)}, bf16[2,32,768]{2,1,0:T(8,128)(2,1)S(1)}, u32[]{:S(2)}, u32[]{:S(2)}) collective-permute-start(bf16[2,32,768]{2,1,0:T(8,128)(2,1)S(1)} %slice.39), channel_id=1, source_target_pairs={{0,224},{32,64},{64,32},{96,128},{128,96},{160,192},{192,160},{224... | collective-permute-start | bytes 294920 | tf_op jit(solution)/shard_map/ppermute | solution.py:152
  113.5 5.9 %collective-permute-start.33 = (bf16[2,32,768]{2,1,0:T(8,128)(2,1)S(1)}, bf16[2,32,768]{2,1,0:T(8,128)(2,1)S(1)}, u32[]{:S(2)}, u32[]{:S(2)}) collective-permute-start(bf16[2,32,768]{2,1,0:T(8,128)(2,1)S(1)} %slice.38), channel_id=1, source_target_pairs={{0,32},{32,0},{64,96},{96,64},{128,160},{160,128},{192,224},{224,1... | collective-permute-start | bytes 294920 | tf_op jit(solution)/shard_map/ppermute | solution.py:152
  114.1 6.3 %collective-permute-start.28 = (bf16[2,32,768]{2,1,0:T(8,128)(2,1)S(1)}, bf16[2,32,768]{2,1,0:T(8,128)(2,1)S(1)}, u32[]{:S(2)}, u32[]{:S(2)}) collective-permute-start(bf16[2,32,768]{2,1,0:T(8,128)(2,1)S(1)} %slice.37), channel_id=1, source_target_pairs={{0,224},{32,64},{64,32},{96,128},{128,96},{160,192},{192,160},{224... | collective-permute-start | bytes 294920 | tf_op jit(solution)/shard_map/ppermute | solution.py:152
  116.7 4.7 %collective-permute-start.24 = (bf16[2,32,768]{2,1,0:T(8,128)(2,1)S(1)}, bf16[2,32,768]{2,1,0:T(8,128)(2,1)S(1)}, u32[]{:S(2)}, u32[]{:S(2)}) collective-permute-start(bf16[2,32,768]{2,1,0:T(8,128)(2,1)S(1)} %slice.36), channel_id=1, source_target_pairs={{0,32},{32,0},{64,96},{96,64},{128,160},{160,128},{192,224},{224,1... | collective-permute-start | bytes 294920 | tf_op jit(solution)/shard_map/ppermute | solution.py:152

commit v5 on v4

--- a/solution.py
+++ b/solution.py
@@ -64,6 +64,11 @@
         @pl.when(block >= count_ref[0, NZ * y + plane])
         def _():
             g_out[plane] = jnp.zeros(g_out.shape[1:], g_out.dtype)
+
+
+def join_kernel(*refs):
+    for k in range(NY):
+        refs[NY][:, k] = refs[k][...]
 
 
 def grad_kernel(xt_ref, *refs):
@@ -109,8 +114,9 @@
     half = NEWTON_FIRST * gram + dot(first, gram16)
     gram = NEWTON_FIRST * half + dot(half.astype(jnp.bfloat16), first)
     gram16 = gram.astype(jnp.bfloat16)
-    second = (NEWTON_SECOND * gram + NEWTON_THIRD * dot(gram16, gram16)).astype(jnp.bfloat16)
-    out = NEWTON_FIRST * current + dot(current.astype(jnp.bfloat16), second)
+    once = dot(current.astype(jnp.bfloat16), gram16)
+    twice = dot(once.astype(jnp.bfloat16), gram16)
+    out = NEWTON_FIRST * current + NEWTON_SECOND * once + NEWTON_THIRD * twice
     out = (scale * out).astype(jnp.bfloat16)
     for k in range(NY):
         out_refs[k][...] = out[COLS * k : COLS * (k + 1)].reshape(out_refs[k].shape)
@@ -174,7 +180,14 @@
         far_hbm(g.reshape(NY, NZ, CAP // BLK, BLK, width)),
     )
     sides = [sides[0]] + [move(sides[k], "y", pair(NY, SIDES[k])) for k in range(1, NY)]
-    sides = jnp.stack(sides, axis=1)
+    sides = pl.pallas_call(
+        join_kernel,
+        out_shape=pltpu.VMEM((NZ, NY, COLS, CAP), jnp.bfloat16),
+        in_specs=[VMEM] * NY,
+        out_specs=VMEM,
+        compiler_params=pltpu.CompilerParams(vmem_limit_bytes=1 << 20),
+        name="join",
+    )(*near(*sides))
     own = lax.all_to_all(mine, "z", 0, 0, tiled=True)
     xz = lax.all_to_all(sides, "z", 0, 0, tiled=True)
 

time: 123 us -> 122 us (level)
  transfers between devices with their start and end apart: 40 -> 40, of which waited for: 22 -> 22; matrix products, arithmetic and copies ran while one was open for 2% -> 1% of each run, Pallas kernels for 3% -> 3%
where the time goes in v5:
time: 122 us
  starting transfers between devices  58.3 us (48%)
  waiting for transfers between devices  48.1 us (39%)
  Pallas kernels  12.2 us (10%)
  matrix products  2.55 us (2%)
    ppermute x38, waiting for transfers between devices, move(): return lax.ppermute(value, axis, to)  47.7 us
    ppermute x38, starting transfers between devices, move(): return lax.ppermute(value, axis, to)  42.9 us
    all_to_all x1, starting transfers between devices, body(): own = lax.all_to_all(mine, 'z', 0, 0, tiled=True)  8.48 us
    all_to_all x1, starting transfers between devices, body(): xz = lax.all_to_all(sides, 'z', 0, 0, tiled=True)  6.9 us
    pallas_call x1, Pallas kernels, body(): pl.pallas_call(functools.partial(newton_kernel, math.sqrt(2048)), out_sha...  4.91 us
    pallas_call x4, Pallas kernels, place(): pl.pallas_call(functools.partial(place_kernel, places, n, int(aliased)),...  3.82 us
    dot_general x5, matrix products, gram_of(): lax.dot_general(rows, rows, (((0,), (0,)), ((), ())), preferred_element_t...  2.55 us
  transfers between devices with their start and end apart: 40, of which 22 were waited for; matrix products, arithmetic and copies ran while one was open for 1% of the time, Pallas kernels for 3%

profile of v5, /device:TPU:8, one launch (start us, length us, event | category | flops | bytes accessed | tf_op | source)
XLA Modules:
  0.0 121.6 jit_solution(13147050760429257084)
XLA Ops:
  0.0 1.9 %pack.1 = (bf16[8,64,128]{2,1,0:T(8,128)(2,1)S(1)}, bf16[8,64,128]{2,1,0:T(8,128)(2,1)S(1)}, bf16[8,64,128]{2,1,0:T(8,128)(2,1)S(1)}, bf16[8,64,128]{2,1,0:T(8,128)(2,1)S(1)}, bf16[8,16,768]{2,1,0:T(8,128)(2,1)}) custom-call(s32[1,32]{1,0:T(1,128)} %count_hbm.1, bf16[4,8,64,128]{3,2,1,0:T(8,128)(2,1)} %bitcast.16, bf16[4,8,8,16,768]{4,3,2,1,0:T(8,128)(2,1)} %bitcast.15), custom_call_target="tpu_custom_call" | custom-call | tf_op jit(solution)/shard_map/pack/pallas_call | solution.py:165
  1.9 8.5 %all-to-all-start.1 = ((bf16[8,16,768]{2,1,0:T(8,128)(2,1)}), bf16[8,16,768]{2,1,0:T(8,128)(2,1)S(1)}, u32[]{:S(2)}, u32[]{:S(2)}) async-start(bf16[8,16,768]{2,1,0:T(8,128)(2,1)} %get-tuple-element.18), calls=%async_computation.1 | async-start | bytes 393216 | tf_op jit(solution)/shard_map/all_to_all | solution.py:191
  10.9 2.4 %collective-permute-start.1 = (bf16[8,64,128]{2,1,0:T(8,128)(2,1)S(1)}, bf16[8,64,128]{2,1,0:T(8,128)(2,1)S(1)}, u32[]{:S(2)}, u32[]{:S(2)}) collective-permute-start(bf16[8,64,128]{2,1,0:T(8,128)(2,1)S(1)} %get-tuple-element.16), channel_id=1, source_target_pairs={{0,24},{8,16},{16,8},{24,0},{1,25},{9,17},{17,9},{25,1},{2,26},{10... | collective-permute-start | bytes 393224 | tf_op jit(solution)/shard_map/ppermute | solution.py:158
  13.3 1.2 %collective-permute-start.2 = (bf16[8,64,128]{2,1,0:T(8,128)(2,1)S(1)}, bf16[8,64,128]{2,1,0:T(8,128)(2,1)S(1)}, u32[]{:S(2)}, u32[]{:S(2)}) collective-permute-start(bf16[8,64,128]{2,1,0:T(8,128)(2,1)S(1)} %get-tuple-element.17), channel_id=1, source_target_pairs={{0,16},{8,24},{16,0},{24,8},{1,17},{9,25},{17,1},{25,9},{2,18},{10... | collective-permute-start | bytes 393224 | tf_op jit(solution)/shard_map/ppermute | solution.py:158
  14.5 1.1 collective-permute-done.refs_1_
  15.6 2.9 %collective-permute-done.1.refs_2_ = bf16[8,64,128]{2,1,0:T(8,128)(2,1)S(1)} collective-permute-done((bf16[8,64,128]{2,1,0:T(8,128)(2,1)S(1)}, bf16[8,64,128]{2,1,0:T(8,128)(2,1)S(1)}, u32[]{:S(2)}, u32[]{:S(2)}) %collective-permute-start.1) | collective-permute-done | bytes 131104 | tf_op jit(solution)/shard_map/ppermute | solution.py:158
  18.5 1.3 %collective-permute-done.2.refs_3_ = bf16[8,64,128]{2,1,0:T(8,128)(2,1)S(1)} collective-permute-done((bf16[8,64,128]{2,1,0:T(8,128)(2,1)S(1)}, bf16[8,64,128]{2,1,0:T(8,128)(2,1)S(1)}, u32[]{:S(2)}, u32[]{:S(2)}) %collective-permute-start.2) | collective-permute-done | bytes 131104 | tf_op jit(solution)/shard_map/ppermute | solution.py:158
  19.7 0.8 join.1
  20.9 6.9 %all-to-all-start = ((bf16[8,4,64,128]{3,2,1,0:T(8,128)(2,1)}), bf16[8,4,64,128]{3,2,1,0:T(8,128)(2,1)S(1)}, u32[]{:S(2)}, u32[]{:S(2)}) async-start(bf16[8,4,64,128]{3,2,1,0:T(8,128)(2,1)} %join.1), calls=%async_computation | async-start | bytes 1048576 | tf_op jit(solution)/shard_map/all_to_all | solution.py:192
  27.8 2.8 %collective-permute-start.4 = (bf16[8,16,768]{2,1,0:T(8,128)(2,1)S(1)}, bf16[8,16,768]{2,1,0:T(8,128)(2,1)S(1)}, u32[]{:S(2)}, u32[]{:S(2)}) collective-permute-start(bf16[8,16,768]{2,1,0:T(8,128)(2,1)S(1)} %all-to-all-done.1.refs_0_), channel_id=1, source_target_pairs={{0,6},{2,4},{4,2},{6,0},{1,7},{3,5},{5,3},{7,1},{8,14},{10,12},{12... | collective-permute-start | bytes 589832 | tf_op jit(solution)/shard_map/ppermute | solution.py:158
  30.8 3.9 %collective-permute-done.4.refs_2_ = bf16[8,16,768]{2,1,0:T(8,128)(2,1)S(1)} collective-permute-done((bf16[8,16,768]{2,1,0:T(8,128)(2,1)S(1)}, bf16[8,16,768]{2,1,0:T(8,128)(2,1)S(1)}, u32[]{:S(2)}, u32[]{:S(2)}) %collective-permute-start.4) | collective-permute-done | bytes 196640 | tf_op jit(solution)/shard_map/ppermute | solution.py:158
  35.0 2.2 %collective-permute-done.3.refs_1_ = bf16[8,16,768]{2,1,0:T(8,128)(2,1)S(1)} collective-permute-done((bf16[8,16,768]{2,1,0:T(8,128)(2,1)S(1)}, bf16[8,16,768]{2,1,0:T(8,128)(2,1)S(1)}, u32[]{:S(2)}, u32[]{:S(2)}) %collective-permute-start.3) | collective-permute-done | bytes 196640 | tf_op jit(solution)/shard_map/ppermute | solution.py:158
  38.2 1.2 collective-permute-done.5.refs_3_
  39.4 3.8 %collective-permute-done.6.refs_4_ = bf16[4,16,768]{2,1,0:T(8,128)(2,1)S(1)} collective-permute-done((bf16[4,16,768]{2,1,0:T(8,128)(2,1)S(1)}, bf16[4,16,768]{2,1,0:T(8,128)(2,1)S(1)}, u32[]{:S(2)}, u32[]{:S(2)}) %collective-permute-start.6) | collective-permute-done | bytes 98336 | tf_op jit(solution)/shard_map/ppermute | solution.py:158
  43.2 1.3 %collective-permute-done.11.refs_9_ = bf16[4,16,768]{2,1,0:T(8,128)(2,1)S(1)} collective-permute-done((bf16[4,16,768]{2,1,0:T(8,128)(2,1)S(1)}, bf16[4,16,768]{2,1,0:T(8,128)(2,1)S(1)}, u32[]{:S(2)}, u32[]{:S(2)}) %collective-permute-start.11) | collective-permute-done | bytes 98336 | tf_op jit(solution)/shard_map/ppermute | solution.py:158
  44.4 0.7 grad.1.grad_ref
  45.6 2.1 %collective-permute-start.13 = (bf16[256,768]{1,0:T(8,128)(2,1)S(1)}, bf16[256,768]{1,0:T(8,128)(2,1)S(1)}, u32[]{:S(2)}, u32[]{:S(2)}) collective-permute-start(bf16[256,768]{1,0:T(8,128)(2,1)S(1)} %grad.1.grad_ref), channel_id=1, source_target_pairs={{0,6},{2,4},{4,2},{6,0},{1,7},{3,5},{5,3},{7,1},{8,14},{10,12},{12... | collective-permute-start | bytes 1179656 | tf_op jit(solution)/shard_map/ppermute | solution.py:158
  47.7 8.7 %collective-permute-done.12 = bf16[256,768]{1,0:T(8,128)(2,1)S(1)} collective-permute-done((bf16[256,768]{1,0:T(8,128)(2,1)S(1)}, bf16[256,768]{1,0:T(8,128)(2,1)S(1)}, u32[]{:S(2)}, u32[]{:S(2)}) %collective-permute-start.12) | collective-permute-done | bytes 393248 | tf_op jit(solution)/shard_map/ppermute | solution.py:158
  56.4 0.5 fusion
  56.9 0.8 collective-permute-done.13
  58.2 0.5 add_add_fusion.1
  58.9 0.5 collective-permute-start.14
  59.4 1.0 collective-permute-start.15
  60.4 5.9 %collective-permute-done.14 = bf16[128,768]{1,0:T(8,128)(2,1)S(1)} collective-permute-done((bf16[128,768]{1,0:T(8,128)(2,1)S(1)}, bf16[128,768]{1,0:T(8,128)(2,1)S(1)}, u32[]{:S(2)}, u32[]{:S(2)}) %collective-permute-start.14) | collective-permute-done | bytes 196640 | tf_op jit(solution)/shard_map/ppermute | solution.py:158
  66.3 1.5 %collective-permute-done.15 = bf16[128,768]{1,0:T(8,128)(2,1)S(1)} collective-permute-done((bf16[128,768]{1,0:T(8,128)(2,1)S(1)}, bf16[128,768]{1,0:T(8,128)(2,1)S(1)}, u32[]{:S(2)}, u32[]{:S(2)}) %collective-permute-start.15) | collective-permute-done | bytes 196640 | tf_op jit(solution)/shard_map/ppermute | solution.py:158
  68.2 0.5 add_add_fusion.mine_ref
  69.2 4.9 %newton.1 = (bf16[1,64,768]{2,1,0:T(8,128)(2,1)S(1)}, bf16[1,64,768]{2,1,0:T(8,128)(2,1)S(1)}, bf16[1,64,768]{2,1,0:T(8,128)(2,1)S(1)}, bf16[1,64,768]{2,1,0:T(8,128)(2,1)S(1)}) custom-call(f32[768,768]{1,0:T(8,128)S(1)} %add_add_fusion.mine_ref, f32[768,768]{1,0:T(8,128)S(1)} %collective-permute-done.16.other_ref, ...), custom_call_target="tpu_custom_call" | custom-call | tf_op jit(solution)/shard_map/newton/pallas_call | solution.py:223
  74.1 1.2 collective-permute-start.19
  75.3 2.7 %collective-permute-start.20 = (bf16[1,64,768]{2,1,0:T(8,128)(2,1)S(1)}, bf16[1,64,768]{2,1,0:T(8,128)(2,1)S(1)}, u32[]{:S(2)}, u32[]{:S(2)}) collective-permute-start(bf16[1,64,768]{2,1,0:T(8,128)(2,1)S(1)} %get-tuple-element.20), channel_id=1, source_target_pairs={{0,16},{8,24},{16,0},{24,8},{1,17},{9,25},{17,1},{25,9},{2,18},{10... | collective-permute-start | bytes 294920 | tf_op jit(solution)/shard_map/ppermute | solution.py:158
  78.3 4.7 %collective-permute-done.29 = bf16[1,64,768]{2,1,0:T(8,128)(2,1)S(1)} collective-permute-done((bf16[1,64,768]{2,1,0:T(8,128)(2,1)S(1)}, bf16[1,64,768]{2,1,0:T(8,128)(2,1)S(1)}, u32[]{:S(2)}, u32[]{:S(2)}) %collective-permute-start.29) | collective-permute-done | bytes 98336 | tf_op jit(solution)/shard_map/ppermute | solution.py:158
  83.0 2.1 %collective-permute-start.34 = (bf16[2,64,768]{2,1,0:T(8,128)(2,1)S(1)}, bf16[2,64,768]{2,1,0:T(8,128)(2,1)S(1)}, u32[]{:S(2)}, u32[]{:S(2)}) collective-permute-start(bf16[2,64,768]{2,1,0:T(8,128)(2,1)S(1)} %constant_dynamic-update-slice_fusion.2.refs_0_), channel_id=1, source_target_pairs={{0,32},{32,0},{64,96},{96,64},{128,160},{160,128},{192,224},{224,1... | collective-permute-start | bytes 589832 | tf_op jit(solution)/shard_map/ppermute | solution.py:158
  85.1 2.7 %collective-permute-start.30 = (bf16[2,64,768]{2,1,0:T(8,128)(2,1)S(1)}, bf16[2,64,768]{2,1,0:T(8,128)(2,1)S(1)}, u32[]{:S(2)}, u32[]{:S(2)}) collective-permute-start(bf16[2,64,768]{2,1,0:T(8,128)(2,1)S(1)} %constant_dynamic-update-slice_fusion.2.refs_0_), channel_id=1, source_target_pairs={{0,224},{32,64},{64,32},{96,128},{128,96},{160,192},{192,160},{224... | collective-permute-start | bytes 589832 | tf_op jit(solution)/shard_map/ppermute | solution.py:158
  88.2 2.7 %collective-permute-start.21 = (bf16[2,64,768]{2,1,0:T(8,128)(2,1)S(1)}, bf16[2,64,768]{2,1,0:T(8,128)(2,1)S(1)}, u32[]{:S(2)}, u32[]{:S(2)}) collective-permute-start(bf16[2,64,768]{2,1,0:T(8,128)(2,1)S(1)} %constant_dynamic-update-slice_fusion.refs_5_), channel_id=1, source_target_pairs={{0,224},{32,64},{64,32},{96,128},{128,96},{160,192},{192,160},{224... | collective-permute-start | bytes 589832 | tf_op jit(solution)/shard_map/ppermute | solution.py:158
  90.8 3.3 %collective-permute-start.35 = (bf16[2,64,768]{2,1,0:T(8,128)(2,1)S(1)}, bf16[2,64,768]{2,1,0:T(8,128)(2,1)S(1)}, u32[]{:S(2)}, u32[]{:S(2)}) collective-permute-start(bf16[2,64,768]{2,1,0:T(8,128)(2,1)S(1)} %collective-permute-done.34.refs_1_), channel_id=1, source_target_pairs={{0,224},{32,64},{64,32},{96,128},{128,96},{160,192},{192,160},{224... | collective-permute-start | bytes 589832 | tf_op jit(solution)/shard_map/ppermute | solution.py:158
  94.6 3.2 %collective-permute-start.26 = (bf16[2,64,768]{2,1,0:T(8,128)(2,1)S(1)}, bf16[2,64,768]{2,1,0:T(8,128)(2,1)S(1)}, u32[]{:S(2)}, u32[]{:S(2)}) collective-permute-start(bf16[2,64,768]{2,1,0:T(8,128)(2,1)S(1)} %collective-permute-done.25.refs_6_), channel_id=1, source_target_pairs={{0,224},{32,64},{64,32},{96,128},{128,96},{160,192},{192,160},{224... | collective-permute-start | bytes 589832 | tf_op jit(solution)/shard_map/ppermute | solution.py:158
  98.5 3.7 %collective-permute-done.35.refs_4_ = bf16[2,64,768]{2,1,0:T(8,128)(2,1)S(1)} collective-permute-done((bf16[2,64,768]{2,1,0:T(8,128)(2,1)S(1)}, bf16[2,64,768]{2,1,0:T(8,128)(2,1)S(1)}, u32[]{:S(2)}, u32[]{:S(2)}) %collective-permute-start.35) | collective-permute-done | bytes 196640 | tf_op jit(solution)/shard_map/ppermute | solution.py:158
  102.2 2.7 %collective-permute-start.32 = (bf16[2,64,768]{2,1,0:T(8,128)(2,1)S(1)}, bf16[2,64,768]{2,1,0:T(8,128)(2,1)S(1)}, u32[]{:S(2)}, u32[]{:S(2)}) collective-permute-start(bf16[2,64,768]{2,1,0:T(8,128)(2,1)S(1)} %collective-permute-done.31.refs_3_), channel_id=1, source_target_pairs={{0,224},{32,64},{64,32},{96,128},{128,96},{160,192},{192,160},{224... | collective-permute-start | bytes 589832 | tf_op jit(solution)/shard_map/ppermute | solution.py:158
  105.0 1.5 %collective-permute-done.26.refs_3_ = bf16[2,64,768]{2,1,0:T(8,128)(2,1)S(1)} collective-permute-done((bf16[2,64,768]{2,1,0:T(8,128)(2,1)S(1)}, bf16[2,64,768]{2,1,0:T(8,128)(2,1)S(1)}, u32[]{:S(2)}, u32[]{:S(2)}) %collective-permute-start.26) | collective-permute-done | bytes 196640 | tf_op jit(solution)/shard_map/ppermute | solution.py:158
  106.4 2.7 %collective-permute-start.23 = (bf16[2,64,768]{2,1,0:T(8,128)(2,1)S(1)}, bf16[2,64,768]{2,1,0:T(8,128)(2,1)S(1)}, u32[]{:S(2)}, u32[]{:S(2)}) collective-permute-start(bf16[2,64,768]{2,1,0:T(8,128)(2,1)S(1)} %collective-permute-done.22.refs_2_), channel_id=1, source_target_pairs={{0,224},{32,64},{64,32},{96,128},{128,96},{160,192},{192,160},{224... | collective-permute-start | bytes 589832 | tf_op jit(solution)/shard_map/ppermute | solution.py:158
  109.2 1.1 collective-permute-done.36.refs_0_
  110.3 2.5 %collective-permute-start.37 = (bf16[2,32,768]{2,1,0:T(8,128)(2,1)S(1)}, bf16[2,32,768]{2,1,0:T(8,128)(2,1)S(1)}, u32[]{:S(2)}, u32[]{:S(2)}) collective-permute-start(bf16[2,32,768]{2,1,0:T(8,128)(2,1)S(1)} %slice.39), channel_id=1, source_target_pairs={{0,224},{32,64},{64,32},{96,128},{128,96},{160,192},{192,160},{224... | collective-permute-start | bytes 294920 | tf_op jit(solution)/shard_map/ppermute | solution.py:158
  113.4 2.6 %collective-permute-start.28 = (bf16[2,32,768]{2,1,0:T(8,128)(2,1)S(1)}, bf16[2,32,768]{2,1,0:T(8,128)(2,1)S(1)}, u32[]{:S(2)}, u32[]{:S(2)}) collective-permute-start(bf16[2,32,768]{2,1,0:T(8,128)(2,1)S(1)} %slice.37), channel_id=1, source_target_pairs={{0,224},{32,64},{64,32},{96,128},{128,96},{160,192},{192,160},{224... | collective-permute-start | bytes 294920 | tf_op jit(solution)/shard_map/ppermute | solution.py:158
  116.0 0.5 collective-permute-start.24
  116.5 1.3 %shard_map.37.refs_4_ = bf16[4,8,64,768]{3,2,1,0:T(8,128)(2,1)} custom-call(bf16[2,64,768]{2,1,0:T(8,128)(2,1)S(1)} %constant_dynamic-update-slice_fusion.2.refs_0_, bf16[2,64,768]{2,1,0:T(8,128)(2,1)S(1)} %collective-permute-done.34.refs_1_, bf16[2,64,768]{2,1,0:T(8,128)(2,1)S(1)} %collective-permute-done.30.refs_2_, ...), custom_call_target="tpu_custom_call" | custom-call | tf_op jit(solution)/shard_map/pallas_call | solution.py:146
  117.8 1.0 shard_map.38.refs_4_
  118.8 0.9 shard_map.39.refs_2_
  119.7 1.0 collective-permute-done.24.refs_0_
  120.7 0.7 shard_map.40
  (57 shorter events, 6.8 us)
Async XLA Ops:
  1.9 18.9 %all-to-all-start.1 = ((bf16[8,16,768]{2,1,0:T(8,128)(2,1)}), bf16[8,16,768]{2,1,0:T(8,128)(2,1)S(1)}, u32[]{:S(2)}, u32[]{:S(2)}) async-start(bf16[8,16,768]{2,1,0:T(8,128)(2,1)} %get-tuple-element.18), calls=%async_computation.1 | async-start | bytes 393216 | tf_op jit(solution)/shard_map/all_to_all | solution.py:191
  10.4 5.2 %collective-permute-start = (bf16[8,64,128]{2,1,0:T(8,128)(2,1)S(1)}, bf16[8,64,128]{2,1,0:T(8,128)(2,1)S(1)}, u32[]{:S(2)}, u32[]{:S(2)}) collective-permute-start(bf16[8,64,128]{2,1,0:T(8,128)(2,1)S(1)} %get-tuple-element.15), channel_id=1, source_target_pairs={{0,8},{8,0},{16,24},{24,16},{1,9},{9,1},{17,25},{25,17},{2,10},{10... | collective-permute-start | bytes 393224 | tf_op jit(solution)/shard_map/ppermute | solution.py:158
  10.9 7.6 %collective-permute-start.1 = (bf16[8,64,128]{2,1,0:T(8,128)(2,1)S(1)}, bf16[8,64,128]{2,1,0:T(8,128)(2,1)S(1)}, u32[]{:S(2)}, u32[]{:S(2)}) collective-permute-start(bf16[8,64,128]{2,1,0:T(8,128)(2,1)S(1)} %get-tuple-element.16), channel_id=1, source_target_pairs={{0,24},{8,16},{16,8},{24,0},{1,25},{9,17},{17,9},{25,1},{2,26},{10... | collective-permute-start | bytes 393224 | tf_op jit(solution)/shard_map/ppermute | solution.py:158
  13.3 6.5 %collective-permute-start.2 = (bf16[8,64,128]{2,1,0:T(8,128)(2,1)S(1)}, bf16[8,64,128]{2,1,0:T(8,128)(2,1)S(1)}, u32[]{:S(2)}, u32[]{:S(2)}) collective-permute-start(bf16[8,64,128]{2,1,0:T(8,128)(2,1)S(1)} %get-tuple-element.17), channel_id=1, source_target_pairs={{0,16},{8,24},{16,0},{24,8},{1,17},{9,25},{17,1},{25,9},{2,18},{10... | collective-permute-start | bytes 393224 | tf_op jit(solution)/shard_map/ppermute | solution.py:158
  20.9 23.6 %all-to-all-start = ((bf16[8,4,64,128]{3,2,1,0:T(8,128)(2,1)}), bf16[8,4,64,128]{3,2,1,0:T(8,128)(2,1)S(1)}, u32[]{:S(2)}, u32[]{:S(2)}) async-start(bf16[8,4,64,128]{3,2,1,0:T(8,128)(2,1)} %join.1), calls=%async_computation | async-start | bytes 1048576 | tf_op jit(solution)/shard_map/all_to_all | solution.py:192
  27.8 6.9 %collective-permute-start.4 = (bf16[8,16,768]{2,1,0:T(8,128)(2,1)S(1)}, bf16[8,16,768]{2,1,0:T(8,128)(2,1)S(1)}, u32[]{:S(2)}, u32[]{:S(2)}) collective-permute-start(bf16[8,16,768]{2,1,0:T(8,128)(2,1)S(1)} %all-to-all-done.1.refs_0_), channel_id=1, source_target_pairs={{0,6},{2,4},{4,2},{6,0},{1,7},{3,5},{5,3},{7,1},{8,14},{10,12},{12... | collective-permute-start | bytes 589832 | tf_op jit(solution)/shard_map/ppermute | solution.py:158
  30.6 6.7 %collective-permute-start.3 = (bf16[8,16,768]{2,1,0:T(8,128)(2,1)S(1)}, bf16[8,16,768]{2,1,0:T(8,128)(2,1)S(1)}, u32[]{:S(2)}, u32[]{:S(2)}) collective-permute-start(bf16[8,16,768]{2,1,0:T(8,128)(2,1)S(1)} %all-to-all-done.1.refs_0_), channel_id=1, source_target_pairs={{0,2},{2,0},{4,6},{6,4},{1,3},{3,1},{5,7},{7,5},{8,10},{10,8},{12,... | collective-permute-start | bytes 589832 | tf_op jit(solution)/shard_map/ppermute | solution.py:158
  30.8 12.4 %collective-permute-start.7 = (bf16[8,16,768]{2,1,0:T(8,128)(2,1)S(1)}, bf16[8,16,768]{2,1,0:T(8,128)(2,1)S(1)}, u32[]{:S(2)}, u32[]{:S(2)}) collective-permute-start(bf16[8,16,768]{2,1,0:T(8,128)(2,1)S(1)} %all-to-all-done.1.refs_0_), channel_id=1, source_target_pairs={{0,1},{1,0},{2,3},{3,2},{4,5},{5,4},{6,7},{7,6},{8,9},{9,8},{10,11... | collective-permute-start | bytes 589832 | tf_op jit(solution)/shard_map/ppermute | solution.py:158
  34.7 4.7 %collective-permute-start.5 = (bf16[4,16,768]{2,1,0:T(8,128)(2,1)S(1)}, bf16[4,16,768]{2,1,0:T(8,128)(2,1)S(1)}, u32[]{:S(2)}, u32[]{:S(2)}) collective-permute-start(bf16[4,16,768]{2,1,0:T(8,128)(2,1)S(1)} %slice.32), channel_id=1, source_target_pairs={{0,2},{2,0},{4,6},{6,4},{1,3},{3,1},{5,7},{7,5},{8,10},{10,8},{12,... | collective-permute-start | bytes 294920 | tf_op jit(solution)/shard_map/ppermute | solution.py:158
  37.2 5.9 %collective-permute-start.6 = (bf16[4,16,768]{2,1,0:T(8,128)(2,1)S(1)}, bf16[4,16,768]{2,1,0:T(8,128)(2,1)S(1)}, u32[]{:S(2)}, u32[]{:S(2)}) collective-permute-start(bf16[4,16,768]{2,1,0:T(8,128)(2,1)S(1)} %slice.33), channel_id=1, source_target_pairs={{0,6},{2,4},{4,2},{6,0},{1,7},{3,5},{5,3},{7,1},{8,14},{10,12},{12... | collective-permute-start | bytes 294920 | tf_op jit(solution)/shard_map/ppermute | solution.py:158
  37.7 5.5 %collective-permute-start.9 = (bf16[8,16,768]{2,1,0:T(8,128)(2,1)S(1)}, bf16[8,16,768]{2,1,0:T(8,128)(2,1)S(1)}, u32[]{:S(2)}, u32[]{:S(2)}) collective-permute-start(bf16[8,16,768]{2,1,0:T(8,128)(2,1)S(1)} %collective-permute-done.4.refs_2_), channel_id=1, source_target_pairs={{0,1},{1,0},{2,3},{3,2},{4,5},{5,4},{6,7},{7,6},{8,9},{9,8},{10,11... | collective-permute-start | bytes 589832 | tf_op jit(solution)/shard_map/ppermute | solution.py:158
  37.7 6.8 %collective-permute-start.8 = (bf16[8,16,768]{2,1,0:T(8,128)(2,1)S(1)}, bf16[8,16,768]{2,1,0:T(8,128)(2,1)S(1)}, u32[]{:S(2)}, u32[]{:S(2)}) collective-permute-start(bf16[8,16,768]{2,1,0:T(8,128)(2,1)S(1)} %collective-permute-done.3.refs_1_), channel_id=1, source_target_pairs={{0,1},{1,0},{2,3},{3,2},{4,5},{5,4},{6,7},{7,6},{8,9},{9,8},{10,11... | collective-permute-start | bytes 589832 | tf_op jit(solution)/shard_map/ppermute | solution.py:158
  39.4 3.8 %collective-permute-start.10 = (bf16[4,16,768]{2,1,0:T(8,128)(2,1)S(1)}, bf16[4,16,768]{2,1,0:T(8,128)(2,1)S(1)}, u32[]{:S(2)}, u32[]{:S(2)}) collective-permute-start(bf16[4,16,768]{2,1,0:T(8,128)(2,1)S(1)} %collective-permute-done.5.refs_3_), channel_id=1, source_target_pairs={{0,1},{1,0},{2,3},{3,2},{4,5},{5,4},{6,7},{7,6},{8,9},{9,8},{10,11... | collective-permute-start | bytes 294920 | tf_op jit(solution)/shard_map/ppermute | solution.py:158
  43.1 1.3 %collective-permute-start.11 = (bf16[4,16,768]{2,1,0:T(8,128)(2,1)S(1)}, bf16[4,16,768]{2,1,0:T(8,128)(2,1)S(1)}, u32[]{:S(2)}, u32[]{:S(2)}) collective-permute-start(bf16[4,16,768]{2,1,0:T(8,128)(2,1)S(1)} %collective-permute-done.6.refs_4_), channel_id=1, source_target_pairs={{0,1},{1,0},{2,3},{3,2},{4,5},{5,4},{6,7},{7,6},{8,9},{9,8},{10,11... | collective-permute-start | bytes 294920 | tf_op jit(solution)/shard_map/ppermute | solution.py:158
  45.1 11.3 %collective-permute-start.12 = (bf16[256,768]{1,0:T(8,128)(2,1)S(1)}, bf16[256,768]{1,0:T(8,128)(2,1)S(1)}, u32[]{:S(2)}, u32[]{:S(2)}) collective-permute-start(bf16[256,768]{1,0:T(8,128)(2,1)S(1)} %grad.1.grad_ref), channel_id=1, source_target_pairs={{0,2},{2,0},{4,6},{6,4},{1,3},{3,1},{5,7},{7,5},{8,10},{10,8},{12,... | collective-permute-start | bytes 1179656 | tf_op jit(solution)/shard_map/ppermute | solution.py:158
  45.6 12.1 %collective-permute-start.13 = (bf16[256,768]{1,0:T(8,128)(2,1)S(1)}, bf16[256,768]{1,0:T(8,128)(2,1)S(1)}, u32[]{:S(2)}, u32[]{:S(2)}) collective-permute-start(bf16[256,768]{1,0:T(8,128)(2,1)S(1)} %grad.1.grad_ref), channel_id=1, source_target_pairs={{0,6},{2,4},{4,2},{6,0},{1,7},{3,5},{5,3},{7,1},{8,14},{10,12},{12... | collective-permute-start | bytes 1179656 | tf_op jit(solution)/shard_map/ppermute | solution.py:158
  58.8 10.4 %collective-permute-start.16 = (f32[768,768]{1,0:T(8,128)S(1)}, f32[768,768]{1,0:T(8,128)S(1)}, u32[]{:S(2)}, u32[]{:S(2)}) collective-permute-start(f32[768,768]{1,0:T(8,128)S(1)} %add_add_fusion.1), channel_id=1, source_target_pairs={{0,1},{1,0},{2,3},{3,2},{4,5},{5,4},{6,7},{7,6},{8,9},{9,8},{10,11... | collective-permute-start | bytes 7077896 | tf_op jit(solution)/shard_map/ppermute | solution.py:158
  58.9 7.4 %collective-permute-start.14 = (bf16[128,768]{1,0:T(8,128)(2,1)S(1)}, bf16[128,768]{1,0:T(8,128)(2,1)S(1)}, u32[]{:S(2)}, u32[]{:S(2)}) collective-permute-start(bf16[128,768]{1,0:T(8,128)(2,1)S(1)} %slice.34), channel_id=1, source_target_pairs={{0,2},{2,0},{4,6},{6,4},{1,3},{3,1},{5,7},{7,5},{8,10},{10,8},{12,... | collective-permute-start | bytes 589832 | tf_op jit(solution)/shard_map/ppermute | solution.py:158
  59.4 8.3 %collective-permute-start.15 = (bf16[128,768]{1,0:T(8,128)(2,1)S(1)}, bf16[128,768]{1,0:T(8,128)(2,1)S(1)}, u32[]{:S(2)}, u32[]{:S(2)}) collective-permute-start(bf16[128,768]{1,0:T(8,128)(2,1)S(1)} %slice.35), channel_id=1, source_target_pairs={{0,6},{2,4},{4,2},{6,0},{1,7},{3,5},{5,3},{7,1},{8,14},{10,12},{12... | collective-permute-start | bytes 589832 | tf_op jit(solution)/shard_map/ppermute | solution.py:158
  66.3 2.5 %collective-permute-start.17 = (bf16[128,768]{1,0:T(8,128)(2,1)S(1)}, bf16[128,768]{1,0:T(8,128)(2,1)S(1)}, u32[]{:S(2)}, u32[]{:S(2)}) collective-permute-start(bf16[128,768]{1,0:T(8,128)(2,1)S(1)} %collective-permute-done.14), channel_id=1, source_target_pairs={{0,1},{1,0},{2,3},{3,2},{4,5},{5,4},{6,7},{7,6},{8,9},{9,8},{10,11... | collective-permute-start | bytes 589832 | tf_op jit(solution)/shard_map/ppermute | solution.py:158
  67.7 1.4 %collective-permute-start.18 = (bf16[128,768]{1,0:T(8,128)(2,1)S(1)}, bf16[128,768]{1,0:T(8,128)(2,1)S(1)}, u32[]{:S(2)}, u32[]{:S(2)}) collective-permute-start(bf16[128,768]{1,0:T(8,128)(2,1)S(1)} %collective-permute-done.15), channel_id=1, source_target_pairs={{0,1},{1,0},{2,3},{3,2},{4,5},{5,4},{6,7},{7,6},{8,9},{9,8},{10,11... | collective-permute-start | bytes 589832 | tf_op jit(solution)/shard_map/ppermute | solution.py:158
  74.1 13.7 %collective-permute-start.19 = (bf16[1,64,768]{2,1,0:T(8,128)(2,1)S(1)}, bf16[1,64,768]{2,1,0:T(8,128)(2,1)S(1)}, u32[]{:S(2)}, u32[]{:S(2)}) collective-permute-start(bf16[1,64,768]{2,1,0:T(8,128)(2,1)S(1)} %get-tuple-element.19), channel_id=1, source_target_pairs={{0,24},{8,16},{16,8},{24,0},{1,25},{9,17},{17,9},{25,1},{2,26},{10... | collective-permute-start | bytes 294920 | tf_op jit(solution)/shard_map/ppermute | solution.py:158
  75.3 12.5 %collective-permute-start.20 = (bf16[1,64,768]{2,1,0:T(8,128)(2,1)S(1)}, bf16[1,64,768]{2,1,0:T(8,128)(2,1)S(1)}, u32[]{:S(2)}, u32[]{:S(2)}) collective-permute-start(bf16[1,64,768]{2,1,0:T(8,128)(2,1)S(1)} %get-tuple-element.20), channel_id=1, source_target_pairs={{0,16},{8,24},{16,0},{24,8},{1,17},{9,25},{17,1},{25,9},{2,18},{10... | collective-permute-start | bytes 294920 | tf_op jit(solution)/shard_map/ppermute | solution.py:158
  78.0 5.0 %collective-permute-start.29 = (bf16[1,64,768]{2,1,0:T(8,128)(2,1)S(1)}, bf16[1,64,768]{2,1,0:T(8,128)(2,1)S(1)}, u32[]{:S(2)}, u32[]{:S(2)}) collective-permute-start(bf16[1,64,768]{2,1,0:T(8,128)(2,1)S(1)} %get-tuple-element.22), channel_id=1, source_target_pairs={{0,8},{8,0},{16,24},{24,16},{1,9},{9,1},{17,25},{25,17},{2,10},{10... | collective-permute-start | bytes 294920 | tf_op jit(solution)/shard_map/ppermute | solution.py:158
  83.0 7.8 %collective-permute-start.34 = (bf16[2,64,768]{2,1,0:T(8,128)(2,1)S(1)}, bf16[2,64,768]{2,1,0:T(8,128)(2,1)S(1)}, u32[]{:S(2)}, u32[]{:S(2)}) collective-permute-start(bf16[2,64,768]{2,1,0:T(8,128)(2,1)S(1)} %constant_dynamic-update-slice_fusion.2.refs_0_), channel_id=1, source_target_pairs={{0,32},{32,0},{64,96},{96,64},{128,160},{160,128},{192,224},{224,1... | collective-permute-start | bytes 589832 | tf_op jit(solution)/shard_map/ppermute | solution.py:158
  85.1 9.0 %collective-permute-start.30 = (bf16[2,64,768]{2,1,0:T(8,128)(2,1)S(1)}, bf16[2,64,768]{2,1,0:T(8,128)(2,1)S(1)}, u32[]{:S(2)}, u32[]{:S(2)}) collective-permute-start(bf16[2,64,768]{2,1,0:T(8,128)(2,1)S(1)} %constant_dynamic-update-slice_fusion.2.refs_0_), channel_id=1, source_target_pairs={{0,224},{32,64},{64,32},{96,128},{128,96},{160,192},{192,160},{224... | collective-permute-start | bytes 589832 | tf_op jit(solution)/shard_map/ppermute | solution.py:158
  87.8 6.8 %collective-permute-start.25 = (bf16[2,64,768]{2,1,0:T(8,128)(2,1)S(1)}, bf16[2,64,768]{2,1,0:T(8,128)(2,1)S(1)}, u32[]{:S(2)}, u32[]{:S(2)}) collective-permute-start(bf16[2,64,768]{2,1,0:T(8,128)(2,1)S(1)} %constant_dynamic-update-slice_fusion.refs_5_), channel_id=1, source_target_pairs={{0,32},{32,0},{64,96},{96,64},{128,160},{160,128},{192,224},{224,1... | collective-permute-start | bytes 589832 | tf_op jit(solution)/shard_map/ppermute | solution.py:158
  88.2 9.8 %collective-permute-start.21 = (bf16[2,64,768]{2,1,0:T(8,128)(2,1)S(1)}, bf16[2,64,768]{2,1,0:T(8,128)(2,1)S(1)}, u32[]{:S(2)}, u32[]{:S(2)}) collective-permute-start(bf16[2,64,768]{2,1,0:T(8,128)(2,1)S(1)} %constant_dynamic-update-slice_fusion.refs_5_), channel_id=1, source_target_pairs={{0,224},{32,64},{64,32},{96,128},{128,96},{160,192},{192,160},{224... | collective-permute-start | bytes 589832 | tf_op jit(solution)/shard_map/ppermute | solution.py:158
  90.8 11.4 %collective-permute-start.35 = (bf16[2,64,768]{2,1,0:T(8,128)(2,1)S(1)}, bf16[2,64,768]{2,1,0:T(8,128)(2,1)S(1)}, u32[]{:S(2)}, u32[]{:S(2)}) collective-permute-start(bf16[2,64,768]{2,1,0:T(8,128)(2,1)S(1)} %collective-permute-done.34.refs_1_), channel_id=1, source_target_pairs={{0,224},{32,64},{64,32},{96,128},{128,96},{160,192},{192,160},{224... | collective-permute-start | bytes 589832 | tf_op jit(solution)/shard_map/ppermute | solution.py:158
  94.1 8.1 %collective-permute-start.31 = (bf16[2,64,768]{2,1,0:T(8,128)(2,1)S(1)}, bf16[2,64,768]{2,1,0:T(8,128)(2,1)S(1)}, u32[]{:S(2)}, u32[]{:S(2)}) collective-permute-start(bf16[2,64,768]{2,1,0:T(8,128)(2,1)S(1)} %collective-permute-done.30.refs_2_), channel_id=1, source_target_pairs={{0,32},{32,0},{64,96},{96,64},{128,160},{160,128},{192,224},{224,1... | collective-permute-start | bytes 589832 | tf_op jit(solution)/shard_map/ppermute | solution.py:158
  94.6 11.8 %collective-permute-start.26 = (bf16[2,64,768]{2,1,0:T(8,128)(2,1)S(1)}, bf16[2,64,768]{2,1,0:T(8,128)(2,1)S(1)}, u32[]{:S(2)}, u32[]{:S(2)}) collective-permute-start(bf16[2,64,768]{2,1,0:T(8,128)(2,1)S(1)} %collective-permute-done.25.refs_6_), channel_id=1, source_target_pairs={{0,224},{32,64},{64,32},{96,128},{128,96},{160,192},{192,160},{224... | collective-permute-start | bytes 589832 | tf_op jit(solution)/shard_map/ppermute | solution.py:158
  98.0 8.4 %collective-permute-start.22 = (bf16[2,64,768]{2,1,0:T(8,128)(2,1)S(1)}, bf16[2,64,768]{2,1,0:T(8,128)(2,1)S(1)}, u32[]{:S(2)}, u32[]{:S(2)}) collective-permute-start(bf16[2,64,768]{2,1,0:T(8,128)(2,1)S(1)} %collective-permute-done.21.refs_7_), channel_id=1, source_target_pairs={{0,32},{32,0},{64,96},{96,64},{128,160},{160,128},{192,224},{224,1... | collective-permute-start | bytes 589832 | tf_op jit(solution)/shard_map/ppermute | solution.py:158
  102.2 8.0 %collective-permute-start.36 = (bf16[2,64,768]{2,1,0:T(8,128)(2,1)S(1)}, bf16[2,64,768]{2,1,0:T(8,128)(2,1)S(1)}, u32[]{:S(2)}, u32[]{:S(2)}) collective-permute-start(bf16[2,64,768]{2,1,0:T(8,128)(2,1)S(1)} %collective-permute-done.35.refs_4_), channel_id=1, source_target_pairs={{0,32},{32,0},{64,96},{96,64},{128,160},{160,128},{192,224},{224,1... | collective-permute-start | bytes 589832 | tf_op jit(solution)/shard_map/ppermute | solution.py:158
  102.2 10.6 %collective-permute-start.32 = (bf16[2,64,768]{2,1,0:T(8,128)(2,1)S(1)}, bf16[2,64,768]{2,1,0:T(8,128)(2,1)S(1)}, u32[]{:S(2)}, u32[]{:S(2)}) collective-permute-start(bf16[2,64,768]{2,1,0:T(8,128)(2,1)S(1)} %collective-permute-done.31.refs_3_), channel_id=1, source_target_pairs={{0,224},{32,64},{64,32},{96,128},{128,96},{160,192},{192,160},{224... | collective-permute-start | bytes 589832 | tf_op jit(solution)/shard_map/ppermute | solution.py:158
  106.4 7.0 %collective-permute-start.27 = (bf16[2,64,768]{2,1,0:T(8,128)(2,1)S(1)}, bf16[2,64,768]{2,1,0:T(8,128)(2,1)S(1)}, u32[]{:S(2)}, u32[]{:S(2)}) collective-permute-start(bf16[2,64,768]{2,1,0:T(8,128)(2,1)S(1)} %collective-permute-done.26.refs_3_), channel_id=1, source_target_pairs={{0,32},{32,0},{64,96},{96,64},{128,160},{160,128},{192,224},{224,1... | collective-permute-start | bytes 589832 | tf_op jit(solution)/shard_map/ppermute | solution.py:158
  106.4 9.6 %collective-permute-start.23 = (bf16[2,64,768]{2,1,0:T(8,128)(2,1)S(1)}, bf16[2,64,768]{2,1,0:T(8,128)(2,1)S(1)}, u32[]{:S(2)}, u32[]{:S(2)}) collective-permute-start(bf16[2,64,768]{2,1,0:T(8,128)(2,1)S(1)} %collective-permute-done.22.refs_2_), channel_id=1, source_target_pairs={{0,224},{32,64},{64,32},{96,128},{128,96},{160,192},{192,160},{224... | collective-permute-start | bytes 589832 | tf_op jit(solution)/shard_map/ppermute | solution.py:158
  110.3 8.5 %collective-permute-start.37 = (bf16[2,32,768]{2,1,0:T(8,128)(2,1)S(1)}, bf16[2,32,768]{2,1,0:T(8,128)(2,1)S(1)}, u32[]{:S(2)}, u32[]{:S(2)}) collective-permute-start(bf16[2,32,768]{2,1,0:T(8,128)(2,1)S(1)} %slice.39), channel_id=1, source_target_pairs={{0,224},{32,64},{64,32},{96,128},{128,96},{160,192},{192,160},{224... | collective-permute-start | bytes 294920 | tf_op jit(solution)/shard_map/ppermute | solution.py:158
  112.8 6.0 %collective-permute-start.33 = (bf16[2,32,768]{2,1,0:T(8,128)(2,1)S(1)}, bf16[2,32,768]{2,1,0:T(8,128)(2,1)S(1)}, u32[]{:S(2)}, u32[]{:S(2)}) collective-permute-start(bf16[2,32,768]{2,1,0:T(8,128)(2,1)S(1)} %slice.38), channel_id=1, source_target_pairs={{0,32},{32,0},{64,96},{96,64},{128,160},{160,128},{192,224},{224,1... | collective-permute-start | bytes 294920 | tf_op jit(solution)/shard_map/ppermute | solution.py:158
  113.4 6.3 %collective-permute-start.28 = (bf16[2,32,768]{2,1,0:T(8,128)(2,1)S(1)}, bf16[2,32,768]{2,1,0:T(8,128)(2,1)S(1)}, u32[]{:S(2)}, u32[]{:S(2)}) collective-permute-start(bf16[2,32,768]{2,1,0:T(8,128)(2,1)S(1)} %slice.37), channel_id=1, source_target_pairs={{0,224},{32,64},{64,32},{96,128},{128,96},{160,192},{192,160},{224... | collective-permute-start | bytes 294920 | tf_op jit(solution)/shard_map/ppermute | solution.py:158
  116.0 4.7 %collective-permute-start.24 = (bf16[2,32,768]{2,1,0:T(8,128)(2,1)S(1)}, bf16[2,32,768]{2,1,0:T(8,128)(2,1)S(1)}, u32[]{:S(2)}, u32[]{:S(2)}) collective-permute-start(bf16[2,32,768]{2,1,0:T(8,128)(2,1)S(1)} %slice.36), channel_id=1, source_target_pairs={{0,32},{32,0},{64,96},{96,64},{128,160},{160,128},{192,224},{224,1... | collective-permute-start | bytes 294920 | tf_op jit(solution)/shard_map/ppermute | solution.py:158

commit v6 on v4

--- a/solution.py
+++ b/solution.py
@@ -109,8 +109,9 @@
     half = NEWTON_FIRST * gram + dot(first, gram16)
     gram = NEWTON_FIRST * half + dot(half.astype(jnp.bfloat16), first)
     gram16 = gram.astype(jnp.bfloat16)
-    second = (NEWTON_SECOND * gram + NEWTON_THIRD * dot(gram16, gram16)).astype(jnp.bfloat16)
-    out = NEWTON_FIRST * current + dot(current.astype(jnp.bfloat16), second)
+    once = dot(current.astype(jnp.bfloat16), gram16)
+    twice = dot(once.astype(jnp.bfloat16), gram16)
+    out = NEWTON_FIRST * current + NEWTON_SECOND * once + NEWTON_THIRD * twice
     out = (scale * out).astype(jnp.bfloat16)
     for k in range(NY):
         out_refs[k][...] = out[COLS * k : COLS * (k + 1)].reshape(out_refs[k].shape)

time: 123 us -> 122 us (level)
  no operation moved by 1% of the time
where the time goes in v6:
time: 122 us
  starting transfers between devices  58.4 us (48%)
  waiting for transfers between devices  48 us (39%)
  Pallas kernels  11.3 us (9%)
  matrix products  2.55 us (2%)
    ppermute x38, waiting for transfers between devices, move(): return lax.ppermute(value, axis, to)  47.7 us
    ppermute x38, starting transfers between devices, move(): return lax.ppermute(value, axis, to)  43 us
    all_to_all x1, starting transfers between devices, body(): own = lax.all_to_all(mine, 'z', 0, 0, tiled=True)  8.48 us
    all_to_all x1, starting transfers between devices, body(): xz = lax.all_to_all(sides, 'z', 0, 0, tiled=True)  6.93 us
    pallas_call x1, Pallas kernels, body(): pl.pallas_call(functools.partial(newton_kernel, math.sqrt(2048)), out_sha...  4.91 us
    pallas_call x4, Pallas kernels, place(): pl.pallas_call(functools.partial(place_kernel, places, n, int(aliased)),...  3.82 us
    dot_general x5, matrix products, gram_of(): lax.dot_general(rows, rows, (((0,), (0,)), ((), ())), preferred_element_t...  2.55 us
  transfers between devices with their start and end apart: 40, of which 22 were waited for; matrix products, arithmetic and copies ran while one was open for 2% of the time, Pallas kernels for 3%

profile of v6, /device:TPU:8, one launch (start us, length us, event | category | flops | bytes accessed | tf_op | source)
XLA Modules:
  0.0 121.6 jit_solution(15955805690128205422)
XLA Ops:
  0.0 1.9 %pack.1 = (bf16[8,64,128]{2,1,0:T(8,128)(2,1)S(1)}, bf16[8,64,128]{2,1,0:T(8,128)(2,1)S(1)}, bf16[8,64,128]{2,1,0:T(8,128)(2,1)S(1)}, bf16[8,64,128]{2,1,0:T(8,128)(2,1)S(1)}, bf16[8,16,768]{2,1,0:T(8,128)(2,1)}) custom-call(s32[1,32]{1,0:T(1,128)} %count_hbm.1, bf16[4,8,64,128]{3,2,1,0:T(8,128)(2,1)} %bitcast.21, bf16[4,8,8,16,768]{4,3,2,1,0:T(8,128)(2,1)} %bitcast.20), custom_call_target="tpu_custom_call" | custom-call | tf_op jit(solution)/shard_map/pack/pallas_call | solution.py:160
  1.9 8.5 %all-to-all-start.1 = ((bf16[8,16,768]{2,1,0:T(8,128)(2,1)}), bf16[8,16,768]{2,1,0:T(8,128)(2,1)S(1)}, u32[]{:S(2)}, u32[]{:S(2)}) async-start(bf16[8,16,768]{2,1,0:T(8,128)(2,1)} %get-tuple-element.18), calls=%async_computation.1 | async-start | bytes 393216 | tf_op jit(solution)/shard_map/all_to_all | solution.py:179
  10.9 2.4 %collective-permute-start.1 = (bf16[8,64,128]{2,1,0:T(8,128)(2,1)S(1)}, bf16[8,64,128]{2,1,0:T(8,128)(2,1)S(1)}, u32[]{:S(2)}, u32[]{:S(2)}) collective-permute-start(bf16[8,64,128]{2,1,0:T(8,128)(2,1)S(1)} %get-tuple-element.16), channel_id=1, source_target_pairs={{0,24},{8,16},{16,8},{24,0},{1,25},{9,17},{17,9},{25,1},{2,26},{10... | collective-permute-start | bytes 393224 | tf_op jit(solution)/shard_map/ppermute | solution.py:153
  13.3 1.2 %collective-permute-start.2 = (bf16[8,64,128]{2,1,0:T(8,128)(2,1)S(1)}, bf16[8,64,128]{2,1,0:T(8,128)(2,1)S(1)}, u32[]{:S(2)}, u32[]{:S(2)}) collective-permute-start(bf16[8,64,128]{2,1,0:T(8,128)(2,1)S(1)} %get-tuple-element.17), channel_id=1, source_target_pairs={{0,16},{8,24},{16,0},{24,8},{1,17},{9,25},{17,1},{25,9},{2,18},{10... | collective-permute-start | bytes 393224 | tf_op jit(solution)/shard_map/ppermute | solution.py:153
  14.5 1.1 collective-permute-done
  15.6 2.9 %collective-permute-done.1 = bf16[8,64,128]{2,1,0:T(8,128)(2,1)S(1)} collective-permute-done((bf16[8,64,128]{2,1,0:T(8,128)(2,1)S(1)}, bf16[8,64,128]{2,1,0:T(8,128)(2,1)S(1)}, u32[]{:S(2)}, u32[]{:S(2)}) %collective-permute-start.1) | collective-permute-done | bytes 131104 | tf_op jit(solution)/shard_map/ppermute | solution.py:153
  18.5 1.3 %collective-permute-done.2 = bf16[8,64,128]{2,1,0:T(8,128)(2,1)S(1)} collective-permute-done((bf16[8,64,128]{2,1,0:T(8,128)(2,1)S(1)}, bf16[8,64,128]{2,1,0:T(8,128)(2,1)S(1)}, u32[]{:S(2)}, u32[]{:S(2)}) %collective-permute-start.2) | collective-permute-done | bytes 131104 | tf_op jit(solution)/shard_map/ppermute | solution.py:153
  19.7 0.9 pad_maximum_fusion
  20.9 6.9 %all-to-all-start = ((bf16[8,4,64,128]{3,2,1,0:T(8,128)(2,1)}), bf16[8,4,64,128]{3,2,1,0:T(8,128)(2,1)S(1)}, u32[]{:S(2)}, u32[]{:S(2)}) async-start(bf16[8,4,64,128]{3,2,1,0:T(8,128)(2,1)} %pad_maximum_fusion), calls=%async_computation | async-start | bytes 1048576 | tf_op jit(solution)/shard_map/all_to_all | solution.py:180
  27.8 2.8 %collective-permute-start.4 = (bf16[8,16,768]{2,1,0:T(8,128)(2,1)S(1)}, bf16[8,16,768]{2,1,0:T(8,128)(2,1)S(1)}, u32[]{:S(2)}, u32[]{:S(2)}) collective-permute-start(bf16[8,16,768]{2,1,0:T(8,128)(2,1)S(1)} %all-to-all-done.1.refs_0_), channel_id=1, source_target_pairs={{0,6},{2,4},{4,2},{6,0},{1,7},{3,5},{5,3},{7,1},{8,14},{10,12},{12... | collective-permute-start | bytes 589832 | tf_op jit(solution)/shard_map/ppermute | solution.py:153
  30.8 3.9 %collective-permute-done.4.refs_2_ = bf16[8,16,768]{2,1,0:T(8,128)(2,1)S(1)} collective-permute-done((bf16[8,16,768]{2,1,0:T(8,128)(2,1)S(1)}, bf16[8,16,768]{2,1,0:T(8,128)(2,1)S(1)}, u32[]{:S(2)}, u32[]{:S(2)}) %collective-permute-start.4) | collective-permute-done | bytes 196640 | tf_op jit(solution)/shard_map/ppermute | solution.py:153
  35.1 2.2 %collective-permute-done.3.refs_1_ = bf16[8,16,768]{2,1,0:T(8,128)(2,1)S(1)} collective-permute-done((bf16[8,16,768]{2,1,0:T(8,128)(2,1)S(1)}, bf16[8,16,768]{2,1,0:T(8,128)(2,1)S(1)}, u32[]{:S(2)}, u32[]{:S(2)}) %collective-permute-start.3) | collective-permute-done | bytes 196640 | tf_op jit(solution)/shard_map/ppermute | solution.py:153
  38.2 1.2 collective-permute-done.5.refs_3_
  39.4 3.8 %collective-permute-done.6.refs_4_ = bf16[4,16,768]{2,1,0:T(8,128)(2,1)S(1)} collective-permute-done((bf16[4,16,768]{2,1,0:T(8,128)(2,1)S(1)}, bf16[4,16,768]{2,1,0:T(8,128)(2,1)S(1)}, u32[]{:S(2)}, u32[]{:S(2)}) %collective-permute-start.6) | collective-permute-done | bytes 98336 | tf_op jit(solution)/shard_map/ppermute | solution.py:153
  43.2 1.3 %collective-permute-done.11.refs_9_ = bf16[4,16,768]{2,1,0:T(8,128)(2,1)S(1)} collective-permute-done((bf16[4,16,768]{2,1,0:T(8,128)(2,1)S(1)}, bf16[4,16,768]{2,1,0:T(8,128)(2,1)S(1)}, u32[]{:S(2)}, u32[]{:S(2)}) %collective-permute-start.11) | collective-permute-done | bytes 98336 | tf_op jit(solution)/shard_map/ppermute | solution.py:153
  44.5 0.7 grad.1.grad_ref
  45.6 2.1 %collective-permute-start.13 = (bf16[256,768]{1,0:T(8,128)(2,1)S(1)}, bf16[256,768]{1,0:T(8,128)(2,1)S(1)}, u32[]{:S(2)}, u32[]{:S(2)}) collective-permute-start(bf16[256,768]{1,0:T(8,128)(2,1)S(1)} %grad.1.grad_ref), channel_id=1, source_target_pairs={{0,6},{2,4},{4,2},{6,0},{1,7},{3,5},{5,3},{7,1},{8,14},{10,12},{12... | collective-permute-start | bytes 1179656 | tf_op jit(solution)/shard_map/ppermute | solution.py:153
  47.7 8.7 %collective-permute-done.12 = bf16[256,768]{1,0:T(8,128)(2,1)S(1)} collective-permute-done((bf16[256,768]{1,0:T(8,128)(2,1)S(1)}, bf16[256,768]{1,0:T(8,128)(2,1)S(1)}, u32[]{:S(2)}, u32[]{:S(2)}) %collective-permute-start.12) | collective-permute-done | bytes 393248 | tf_op jit(solution)/shard_map/ppermute | solution.py:153
  56.4 0.5 fusion
  57.0 0.8 collective-permute-done.13
  57.8 0.5 fusion.1
  58.3 0.5 add_add_fusion.1
  58.9 0.5 collective-permute-start.14
  59.5 1.0 collective-permute-start.15
  60.4 5.9 %collective-permute-done.14 = bf16[128,768]{1,0:T(8,128)(2,1)S(1)} collective-permute-done((bf16[128,768]{1,0:T(8,128)(2,1)S(1)}, bf16[128,768]{1,0:T(8,128)(2,1)S(1)}, u32[]{:S(2)}, u32[]{:S(2)}) %collective-permute-start.14) | collective-permute-done | bytes 196640 | tf_op jit(solution)/shard_map/ppermute | solution.py:153
  66.3 1.5 %collective-permute-done.15 = bf16[128,768]{1,0:T(8,128)(2,1)S(1)} collective-permute-done((bf16[128,768]{1,0:T(8,128)(2,1)S(1)}, bf16[128,768]{1,0:T(8,128)(2,1)S(1)}, u32[]{:S(2)}, u32[]{:S(2)}) %collective-permute-start.15) | collective-permute-done | bytes 196640 | tf_op jit(solution)/shard_map/ppermute | solution.py:153
  68.3 0.5 add_add_fusion.mine_ref
  69.2 4.9 %newton.1 = (bf16[1,64,768]{2,1,0:T(8,128)(2,1)S(1)}, bf16[1,64,768]{2,1,0:T(8,128)(2,1)S(1)}, bf16[1,64,768]{2,1,0:T(8,128)(2,1)S(1)}, bf16[1,64,768]{2,1,0:T(8,128)(2,1)S(1)}) custom-call(f32[768,768]{1,0:T(8,128)S(1)} %add_add_fusion.mine_ref, f32[768,768]{1,0:T(8,128)S(1)} %collective-permute-done.16.other_ref, ...), custom_call_target="tpu_custom_call" | custom-call | tf_op jit(solution)/shard_map/newton/pallas_call | solution.py:211
  74.1 1.2 collective-permute-start.19
  75.3 2.7 %collective-permute-start.20 = (bf16[1,64,768]{2,1,0:T(8,128)(2,1)S(1)}, bf16[1,64,768]{2,1,0:T(8,128)(2,1)S(1)}, u32[]{:S(2)}, u32[]{:S(2)}) collective-permute-start(bf16[1,64,768]{2,1,0:T(8,128)(2,1)S(1)} %get-tuple-element.20), channel_id=1, source_target_pairs={{0,16},{8,24},{16,0},{24,8},{1,17},{9,25},{17,1},{25,9},{2,18},{10... | collective-permute-start | bytes 294920 | tf_op jit(solution)/shard_map/ppermute | solution.py:153
  78.3 4.7 %collective-permute-done.29 = bf16[1,64,768]{2,1,0:T(8,128)(2,1)S(1)} collective-permute-done((bf16[1,64,768]{2,1,0:T(8,128)(2,1)S(1)}, bf16[1,64,768]{2,1,0:T(8,128)(2,1)S(1)}, u32[]{:S(2)}, u32[]{:S(2)}) %collective-permute-start.29) | collective-permute-done | bytes 98336 | tf_op jit(solution)/shard_map/ppermute | solution.py:153
  83.0 2.1 %collective-permute-start.34 = (bf16[2,64,768]{2,1,0:T(8,128)(2,1)S(1)}, bf16[2,64,768]{2,1,0:T(8,128)(2,1)S(1)}, u32[]{:S(2)}, u32[]{:S(2)}) collective-permute-start(bf16[2,64,768]{2,1,0:T(8,128)(2,1)S(1)} %constant_dynamic-update-slice_fusion.2.refs_0_), channel_id=1, source_target_pairs={{0,32},{32,0},{64,96},{96,64},{128,160},{160,128},{192,224},{224,1... | collective-permute-start | bytes 589832 | tf_op jit(solution)/shard_map/ppermute | solution.py:153
  85.1 2.7 %collective-permute-start.30 = (bf16[2,64,768]{2,1,0:T(8,128)(2,1)S(1)}, bf16[2,64,768]{2,1,0:T(8,128)(2,1)S(1)}, u32[]{:S(2)}, u32[]{:S(2)}) collective-permute-start(bf16[2,64,768]{2,1,0:T(8,128)(2,1)S(1)} %constant_dynamic-update-slice_fusion.2.refs_0_), channel_id=1, source_target_pairs={{0,224},{32,64},{64,32},{96,128},{128,96},{160,192},{192,160},{224... | collective-permute-start | bytes 589832 | tf_op jit(solution)/shard_map/ppermute | solution.py:153
  88.2 2.7 %collective-permute-start.21 = (bf16[2,64,768]{2,1,0:T(8,128)(2,1)S(1)}, bf16[2,64,768]{2,1,0:T(8,128)(2,1)S(1)}, u32[]{:S(2)}, u32[]{:S(2)}) collective-permute-start(bf16[2,64,768]{2,1,0:T(8,128)(2,1)S(1)} %constant_dynamic-update-slice_fusion.refs_5_), channel_id=1, source_target_pairs={{0,224},{32,64},{64,32},{96,128},{128,96},{160,192},{192,160},{224... | collective-permute-start | bytes 589832 | tf_op jit(solution)/shard_map/ppermute | solution.py:153
  90.9 3.2 %collective-permute-start.35 = (bf16[2,64,768]{2,1,0:T(8,128)(2,1)S(1)}, bf16[2,64,768]{2,1,0:T(8,128)(2,1)S(1)}, u32[]{:S(2)}, u32[]{:S(2)}) collective-permute-start(bf16[2,64,768]{2,1,0:T(8,128)(2,1)S(1)} %collective-permute-done.34.refs_1_), channel_id=1, source_target_pairs={{0,224},{32,64},{64,32},{96,128},{128,96},{160,192},{192,160},{224... | collective-permute-start | bytes 589832 | tf_op jit(solution)/shard_map/ppermute | solution.py:153
  94.6 3.2 %collective-permute-start.26 = (bf16[2,64,768]{2,1,0:T(8,128)(2,1)S(1)}, bf16[2,64,768]{2,1,0:T(8,128)(2,1)S(1)}, u32[]{:S(2)}, u32[]{:S(2)}) collective-permute-start(bf16[2,64,768]{2,1,0:T(8,128)(2,1)S(1)} %collective-permute-done.25.refs_6_), channel_id=1, source_target_pairs={{0,224},{32,64},{64,32},{96,128},{128,96},{160,192},{192,160},{224... | collective-permute-start | bytes 589832 | tf_op jit(solution)/shard_map/ppermute | solution.py:153
  98.5 3.7 %collective-permute-done.35.refs_4_ = bf16[2,64,768]{2,1,0:T(8,128)(2,1)S(1)} collective-permute-done((bf16[2,64,768]{2,1,0:T(8,128)(2,1)S(1)}, bf16[2,64,768]{2,1,0:T(8,128)(2,1)S(1)}, u32[]{:S(2)}, u32[]{:S(2)}) %collective-permute-start.35) | collective-permute-done | bytes 196640 | tf_op jit(solution)/shard_map/ppermute | solution.py:153
  102.2 2.8 %collective-permute-start.32 = (bf16[2,64,768]{2,1,0:T(8,128)(2,1)S(1)}, bf16[2,64,768]{2,1,0:T(8,128)(2,1)S(1)}, u32[]{:S(2)}, u32[]{:S(2)}) collective-permute-start(bf16[2,64,768]{2,1,0:T(8,128)(2,1)S(1)} %collective-permute-done.31.refs_3_), channel_id=1, source_target_pairs={{0,224},{32,64},{64,32},{96,128},{128,96},{160,192},{192,160},{224... | collective-permute-start | bytes 589832 | tf_op jit(solution)/shard_map/ppermute | solution.py:153
  105.0 1.4 %collective-permute-done.26.refs_3_ = bf16[2,64,768]{2,1,0:T(8,128)(2,1)S(1)} collective-permute-done((bf16[2,64,768]{2,1,0:T(8,128)(2,1)S(1)}, bf16[2,64,768]{2,1,0:T(8,128)(2,1)S(1)}, u32[]{:S(2)}, u32[]{:S(2)}) %collective-permute-start.26) | collective-permute-done | bytes 196640 | tf_op jit(solution)/shard_map/ppermute | solution.py:153
  106.5 2.8 %collective-permute-start.23 = (bf16[2,64,768]{2,1,0:T(8,128)(2,1)S(1)}, bf16[2,64,768]{2,1,0:T(8,128)(2,1)S(1)}, u32[]{:S(2)}, u32[]{:S(2)}) collective-permute-start(bf16[2,64,768]{2,1,0:T(8,128)(2,1)S(1)} %collective-permute-done.22.refs_2_), channel_id=1, source_target_pairs={{0,224},{32,64},{64,32},{96,128},{128,96},{160,192},{192,160},{224... | collective-permute-start | bytes 589832 | tf_op jit(solution)/shard_map/ppermute | solution.py:153
  109.2 1.1 collective-permute-done.36.refs_0_
  110.3 2.6 %collective-permute-start.37 = (bf16[2,32,768]{2,1,0:T(8,128)(2,1)S(1)}, bf16[2,32,768]{2,1,0:T(8,128)(2,1)S(1)}, u32[]{:S(2)}, u32[]{:S(2)}) collective-permute-start(bf16[2,32,768]{2,1,0:T(8,128)(2,1)S(1)} %slice.39), channel_id=1, source_target_pairs={{0,224},{32,64},{64,32},{96,128},{128,96},{160,192},{192,160},{224... | collective-permute-start | bytes 294920 | tf_op jit(solution)/shard_map/ppermute | solution.py:153
  113.5 2.6 %collective-permute-start.28 = (bf16[2,32,768]{2,1,0:T(8,128)(2,1)S(1)}, bf16[2,32,768]{2,1,0:T(8,128)(2,1)S(1)}, u32[]{:S(2)}, u32[]{:S(2)}) collective-permute-start(bf16[2,32,768]{2,1,0:T(8,128)(2,1)S(1)} %slice.37), channel_id=1, source_target_pairs={{0,224},{32,64},{64,32},{96,128},{128,96},{160,192},{192,160},{224... | collective-permute-start | bytes 294920 | tf_op jit(solution)/shard_map/ppermute | solution.py:153
  116.6 1.3 %shard_map.37.refs_4_ = bf16[4,8,64,768]{3,2,1,0:T(8,128)(2,1)} custom-call(bf16[2,64,768]{2,1,0:T(8,128)(2,1)S(1)} %constant_dynamic-update-slice_fusion.2.refs_0_, bf16[2,64,768]{2,1,0:T(8,128)(2,1)S(1)} %collective-permute-done.34.refs_1_, bf16[2,64,768]{2,1,0:T(8,128)(2,1)S(1)} %collective-permute-done.30.refs_2_, ...), custom_call_target="tpu_custom_call" | custom-call | tf_op jit(solution)/shard_map/pallas_call | solution.py:141
  117.8 1.0 shard_map.38.refs_4_
  118.8 0.9 shard_map.39.refs_2_
  119.7 1.0 collective-permute-done.24.refs_0_
  120.8 0.7 shard_map.40
  (57 shorter events, 6.8 us)
Async XLA Ops:
  1.9 18.9 %all-to-all-start.1 = ((bf16[8,16,768]{2,1,0:T(8,128)(2,1)}), bf16[8,16,768]{2,1,0:T(8,128)(2,1)S(1)}, u32[]{:S(2)}, u32[]{:S(2)}) async-start(bf16[8,16,768]{2,1,0:T(8,128)(2,1)} %get-tuple-element.18), calls=%async_computation.1 | async-start | bytes 393216 | tf_op jit(solution)/shard_map/all_to_all | solution.py:179
  10.4 5.2 %collective-permute-start = (bf16[8,64,128]{2,1,0:T(8,128)(2,1)S(1)}, bf16[8,64,128]{2,1,0:T(8,128)(2,1)S(1)}, u32[]{:S(2)}, u32[]{:S(2)}) collective-permute-start(bf16[8,64,128]{2,1,0:T(8,128)(2,1)S(1)} %get-tuple-element.15), channel_id=1, source_target_pairs={{0,8},{8,0},{16,24},{24,16},{1,9},{9,1},{17,25},{25,17},{2,10},{10... | collective-permute-start | bytes 393224 | tf_op jit(solution)/shard_map/ppermute | solution.py:153
  10.9 7.6 %collective-permute-start.1 = (bf16[8,64,128]{2,1,0:T(8,128)(2,1)S(1)}, bf16[8,64,128]{2,1,0:T(8,128)(2,1)S(1)}, u32[]{:S(2)}, u32[]{:S(2)}) collective-permute-start(bf16[8,64,128]{2,1,0:T(8,128)(2,1)S(1)} %get-tuple-element.16), channel_id=1, source_target_pairs={{0,24},{8,16},{16,8},{24,0},{1,25},{9,17},{17,9},{25,1},{2,26},{10... | collective-permute-start | bytes 393224 | tf_op jit(solution)/shard_map/ppermute | solution.py:153
  13.3 6.5 %collective-permute-start.2 = (bf16[8,64,128]{2,1,0:T(8,128)(2,1)S(1)}, bf16[8,64,128]{2,1,0:T(8,128)(2,1)S(1)}, u32[]{:S(2)}, u32[]{:S(2)}) collective-permute-start(bf16[8,64,128]{2,1,0:T(8,128)(2,1)S(1)} %get-tuple-element.17), channel_id=1, source_target_pairs={{0,16},{8,24},{16,0},{24,8},{1,17},{9,25},{17,1},{25,9},{2,18},{10... | collective-permute-start | bytes 393224 | tf_op jit(solution)/shard_map/ppermute | solution.py:153
  20.9 23.6 %all-to-all-start = ((bf16[8,4,64,128]{3,2,1,0:T(8,128)(2,1)}), bf16[8,4,64,128]{3,2,1,0:T(8,128)(2,1)S(1)}, u32[]{:S(2)}, u32[]{:S(2)}) async-start(bf16[8,4,64,128]{3,2,1,0:T(8,128)(2,1)} %pad_maximum_fusion), calls=%async_computation | async-start | bytes 1048576 | tf_op jit(solution)/shard_map/all_to_all | solution.py:180
  27.8 6.9 %collective-permute-start.4 = (bf16[8,16,768]{2,1,0:T(8,128)(2,1)S(1)}, bf16[8,16,768]{2,1,0:T(8,128)(2,1)S(1)}, u32[]{:S(2)}, u32[]{:S(2)}) collective-permute-start(bf16[8,16,768]{2,1,0:T(8,128)(2,1)S(1)} %all-to-all-done.1.refs_0_), channel_id=1, source_target_pairs={{0,6},{2,4},{4,2},{6,0},{1,7},{3,5},{5,3},{7,1},{8,14},{10,12},{12... | collective-permute-start | bytes 589832 | tf_op jit(solution)/shard_map/ppermute | solution.py:153
  30.6 6.7 %collective-permute-start.3 = (bf16[8,16,768]{2,1,0:T(8,128)(2,1)S(1)}, bf16[8,16,768]{2,1,0:T(8,128)(2,1)S(1)}, u32[]{:S(2)}, u32[]{:S(2)}) collective-permute-start(bf16[8,16,768]{2,1,0:T(8,128)(2,1)S(1)} %all-to-all-done.1.refs_0_), channel_id=1, source_target_pairs={{0,2},{2,0},{4,6},{6,4},{1,3},{3,1},{5,7},{7,5},{8,10},{10,8},{12,... | collective-permute-start | bytes 589832 | tf_op jit(solution)/shard_map/ppermute | solution.py:153
  30.8 12.4 %collective-permute-start.7 = (bf16[8,16,768]{2,1,0:T(8,128)(2,1)S(1)}, bf16[8,16,768]{2,1,0:T(8,128)(2,1)S(1)}, u32[]{:S(2)}, u32[]{:S(2)}) collective-permute-start(bf16[8,16,768]{2,1,0:T(8,128)(2,1)S(1)} %all-to-all-done.1.refs_0_), channel_id=1, source_target_pairs={{0,1},{1,0},{2,3},{3,2},{4,5},{5,4},{6,7},{7,6},{8,9},{9,8},{10,11... | collective-permute-start | bytes 589832 | tf_op jit(solution)/shard_map/ppermute | solution.py:153
  34.7 4.7 %collective-permute-start.5 = (bf16[4,16,768]{2,1,0:T(8,128)(2,1)S(1)}, bf16[4,16,768]{2,1,0:T(8,128)(2,1)S(1)}, u32[]{:S(2)}, u32[]{:S(2)}) collective-permute-start(bf16[4,16,768]{2,1,0:T(8,128)(2,1)S(1)} %slice.32), channel_id=1, source_target_pairs={{0,2},{2,0},{4,6},{6,4},{1,3},{3,1},{5,7},{7,5},{8,10},{10,8},{12,... | collective-permute-start | bytes 294920 | tf_op jit(solution)/shard_map/ppermute | solution.py:153
  37.3 5.9 %collective-permute-start.6 = (bf16[4,16,768]{2,1,0:T(8,128)(2,1)S(1)}, bf16[4,16,768]{2,1,0:T(8,128)(2,1)S(1)}, u32[]{:S(2)}, u32[]{:S(2)}) collective-permute-start(bf16[4,16,768]{2,1,0:T(8,128)(2,1)S(1)} %slice.33), channel_id=1, source_target_pairs={{0,6},{2,4},{4,2},{6,0},{1,7},{3,5},{5,3},{7,1},{8,14},{10,12},{12... | collective-permute-start | bytes 294920 | tf_op jit(solution)/shard_map/ppermute | solution.py:153
  37.7 5.5 %collective-permute-start.9 = (bf16[8,16,768]{2,1,0:T(8,128)(2,1)S(1)}, bf16[8,16,768]{2,1,0:T(8,128)(2,1)S(1)}, u32[]{:S(2)}, u32[]{:S(2)}) collective-permute-start(bf16[8,16,768]{2,1,0:T(8,128)(2,1)S(1)} %collective-permute-done.4.refs_2_), channel_id=1, source_target_pairs={{0,1},{1,0},{2,3},{3,2},{4,5},{5,4},{6,7},{7,6},{8,9},{9,8},{10,11... | collective-permute-start | bytes 589832 | tf_op jit(solution)/shard_map/ppermute | solution.py:153
  37.7 6.8 %collective-permute-start.8 = (bf16[8,16,768]{2,1,0:T(8,128)(2,1)S(1)}, bf16[8,16,768]{2,1,0:T(8,128)(2,1)S(1)}, u32[]{:S(2)}, u32[]{:S(2)}) collective-permute-start(bf16[8,16,768]{2,1,0:T(8,128)(2,1)S(1)} %collective-permute-done.3.refs_1_), channel_id=1, source_target_pairs={{0,1},{1,0},{2,3},{3,2},{4,5},{5,4},{6,7},{7,6},{8,9},{9,8},{10,11... | collective-permute-start | bytes 589832 | tf_op jit(solution)/shard_map/ppermute | solution.py:153
  39.4 3.8 %collective-permute-start.10 = (bf16[4,16,768]{2,1,0:T(8,128)(2,1)S(1)}, bf16[4,16,768]{2,1,0:T(8,128)(2,1)S(1)}, u32[]{:S(2)}, u32[]{:S(2)}) collective-permute-start(bf16[4,16,768]{2,1,0:T(8,128)(2,1)S(1)} %collective-permute-done.5.refs_3_), channel_id=1, source_target_pairs={{0,1},{1,0},{2,3},{3,2},{4,5},{5,4},{6,7},{7,6},{8,9},{9,8},{10,11... | collective-permute-start | bytes 294920 | tf_op jit(solution)/shard_map/ppermute | solution.py:153
  43.2 1.3 %collective-permute-start.11 = (bf16[4,16,768]{2,1,0:T(8,128)(2,1)S(1)}, bf16[4,16,768]{2,1,0:T(8,128)(2,1)S(1)}, u32[]{:S(2)}, u32[]{:S(2)}) collective-permute-start(bf16[4,16,768]{2,1,0:T(8,128)(2,1)S(1)} %collective-permute-done.6.refs_4_), channel_id=1, source_target_pairs={{0,1},{1,0},{2,3},{3,2},{4,5},{5,4},{6,7},{7,6},{8,9},{9,8},{10,11... | collective-permute-start | bytes 294920 | tf_op jit(solution)/shard_map/ppermute | solution.py:153
  45.2 11.3 %collective-permute-start.12 = (bf16[256,768]{1,0:T(8,128)(2,1)S(1)}, bf16[256,768]{1,0:T(8,128)(2,1)S(1)}, u32[]{:S(2)}, u32[]{:S(2)}) collective-permute-start(bf16[256,768]{1,0:T(8,128)(2,1)S(1)} %grad.1.grad_ref), channel_id=1, source_target_pairs={{0,2},{2,0},{4,6},{6,4},{1,3},{3,1},{5,7},{7,5},{8,10},{10,8},{12,... | collective-permute-start | bytes 1179656 | tf_op jit(solution)/shard_map/ppermute | solution.py:153
  45.6 12.1 %collective-permute-start.13 = (bf16[256,768]{1,0:T(8,128)(2,1)S(1)}, bf16[256,768]{1,0:T(8,128)(2,1)S(1)}, u32[]{:S(2)}, u32[]{:S(2)}) collective-permute-start(bf16[256,768]{1,0:T(8,128)(2,1)S(1)} %grad.1.grad_ref), channel_id=1, source_target_pairs={{0,6},{2,4},{4,2},{6,0},{1,7},{3,5},{5,3},{7,1},{8,14},{10,12},{12... | collective-permute-start | bytes 1179656 | tf_op jit(solution)/shard_map/ppermute | solution.py:153
  58.8 10.4 %collective-permute-start.16 = (f32[768,768]{1,0:T(8,128)S(1)}, f32[768,768]{1,0:T(8,128)S(1)}, u32[]{:S(2)}, u32[]{:S(2)}) collective-permute-start(f32[768,768]{1,0:T(8,128)S(1)} %add_add_fusion.1), channel_id=1, source_target_pairs={{0,1},{1,0},{2,3},{3,2},{4,5},{5,4},{6,7},{7,6},{8,9},{9,8},{10,11... | collective-permute-start | bytes 7077896 | tf_op jit(solution)/shard_map/ppermute | solution.py:153
  58.9 7.4 %collective-permute-start.14 = (bf16[128,768]{1,0:T(8,128)(2,1)S(1)}, bf16[128,768]{1,0:T(8,128)(2,1)S(1)}, u32[]{:S(2)}, u32[]{:S(2)}) collective-permute-start(bf16[128,768]{1,0:T(8,128)(2,1)S(1)} %slice.34), channel_id=1, source_target_pairs={{0,2},{2,0},{4,6},{6,4},{1,3},{3,1},{5,7},{7,5},{8,10},{10,8},{12,... | collective-permute-start | bytes 589832 | tf_op jit(solution)/shard_map/ppermute | solution.py:153
  59.5 8.3 %collective-permute-start.15 = (bf16[128,768]{1,0:T(8,128)(2,1)S(1)}, bf16[128,768]{1,0:T(8,128)(2,1)S(1)}, u32[]{:S(2)}, u32[]{:S(2)}) collective-permute-start(bf16[128,768]{1,0:T(8,128)(2,1)S(1)} %slice.35), channel_id=1, source_target_pairs={{0,6},{2,4},{4,2},{6,0},{1,7},{3,5},{5,3},{7,1},{8,14},{10,12},{12... | collective-permute-start | bytes 589832 | tf_op jit(solution)/shard_map/ppermute | solution.py:153
  66.3 2.5 %collective-permute-start.17 = (bf16[128,768]{1,0:T(8,128)(2,1)S(1)}, bf16[128,768]{1,0:T(8,128)(2,1)S(1)}, u32[]{:S(2)}, u32[]{:S(2)}) collective-permute-start(bf16[128,768]{1,0:T(8,128)(2,1)S(1)} %collective-permute-done.14), channel_id=1, source_target_pairs={{0,1},{1,0},{2,3},{3,2},{4,5},{5,4},{6,7},{7,6},{8,9},{9,8},{10,11... | collective-permute-start | bytes 589832 | tf_op jit(solution)/shard_map/ppermute | solution.py:153
  67.8 1.4 %collective-permute-start.18 = (bf16[128,768]{1,0:T(8,128)(2,1)S(1)}, bf16[128,768]{1,0:T(8,128)(2,1)S(1)}, u32[]{:S(2)}, u32[]{:S(2)}) collective-permute-start(bf16[128,768]{1,0:T(8,128)(2,1)S(1)} %collective-permute-done.15), channel_id=1, source_target_pairs={{0,1},{1,0},{2,3},{3,2},{4,5},{5,4},{6,7},{7,6},{8,9},{9,8},{10,11... | collective-permute-start | bytes 589832 | tf_op jit(solution)/shard_map/ppermute | solution.py:153
  74.1 13.7 %collective-permute-start.19 = (bf16[1,64,768]{2,1,0:T(8,128)(2,1)S(1)}, bf16[1,64,768]{2,1,0:T(8,128)(2,1)S(1)}, u32[]{:S(2)}, u32[]{:S(2)}) collective-permute-start(bf16[1,64,768]{2,1,0:T(8,128)(2,1)S(1)} %get-tuple-element.19), channel_id=1, source_target_pairs={{0,24},{8,16},{16,8},{24,0},{1,25},{9,17},{17,9},{25,1},{2,26},{10... | collective-permute-start | bytes 294920 | tf_op jit(solution)/shard_map/ppermute | solution.py:153
  75.3 12.5 %collective-permute-start.20 = (bf16[1,64,768]{2,1,0:T(8,128)(2,1)S(1)}, bf16[1,64,768]{2,1,0:T(8,128)(2,1)S(1)}, u32[]{:S(2)}, u32[]{:S(2)}) collective-permute-start(bf16[1,64,768]{2,1,0:T(8,128)(2,1)S(1)} %get-tuple-element.20), channel_id=1, source_target_pairs={{0,16},{8,24},{16,0},{24,8},{1,17},{9,25},{17,1},{25,9},{2,18},{10... | collective-permute-start | bytes 294920 | tf_op jit(solution)/shard_map/ppermute | solution.py:153
  78.0 5.0 %collective-permute-start.29 = (bf16[1,64,768]{2,1,0:T(8,128)(2,1)S(1)}, bf16[1,64,768]{2,1,0:T(8,128)(2,1)S(1)}, u32[]{:S(2)}, u32[]{:S(2)}) collective-permute-start(bf16[1,64,768]{2,1,0:T(8,128)(2,1)S(1)} %get-tuple-element.22), channel_id=1, source_target_pairs={{0,8},{8,0},{16,24},{24,16},{1,9},{9,1},{17,25},{25,17},{2,10},{10... | collective-permute-start | bytes 294920 | tf_op jit(solution)/shard_map/ppermute | solution.py:153
  83.0 7.8 %collective-permute-start.34 = (bf16[2,64,768]{2,1,0:T(8,128)(2,1)S(1)}, bf16[2,64,768]{2,1,0:T(8,128)(2,1)S(1)}, u32[]{:S(2)}, u32[]{:S(2)}) collective-permute-start(bf16[2,64,768]{2,1,0:T(8,128)(2,1)S(1)} %constant_dynamic-update-slice_fusion.2.refs_0_), channel_id=1, source_target_pairs={{0,32},{32,0},{64,96},{96,64},{128,160},{160,128},{192,224},{224,1... | collective-permute-start | bytes 589832 | tf_op jit(solution)/shard_map/ppermute | solution.py:153
  85.1 9.0 %collective-permute-start.30 = (bf16[2,64,768]{2,1,0:T(8,128)(2,1)S(1)}, bf16[2,64,768]{2,1,0:T(8,128)(2,1)S(1)}, u32[]{:S(2)}, u32[]{:S(2)}) collective-permute-start(bf16[2,64,768]{2,1,0:T(8,128)(2,1)S(1)} %constant_dynamic-update-slice_fusion.2.refs_0_), channel_id=1, source_target_pairs={{0,224},{32,64},{64,32},{96,128},{128,96},{160,192},{192,160},{224... | collective-permute-start | bytes 589832 | tf_op jit(solution)/shard_map/ppermute | solution.py:153
  87.9 6.8 %collective-permute-start.25 = (bf16[2,64,768]{2,1,0:T(8,128)(2,1)S(1)}, bf16[2,64,768]{2,1,0:T(8,128)(2,1)S(1)}, u32[]{:S(2)}, u32[]{:S(2)}) collective-permute-start(bf16[2,64,768]{2,1,0:T(8,128)(2,1)S(1)} %constant_dynamic-update-slice_fusion.refs_5_), channel_id=1, source_target_pairs={{0,32},{32,0},{64,96},{96,64},{128,160},{160,128},{192,224},{224,1... | collective-permute-start | bytes 589832 | tf_op jit(solution)/shard_map/ppermute | solution.py:153
  88.2 9.8 %collective-permute-start.21 = (bf16[2,64,768]{2,1,0:T(8,128)(2,1)S(1)}, bf16[2,64,768]{2,1,0:T(8,128)(2,1)S(1)}, u32[]{:S(2)}, u32[]{:S(2)}) collective-permute-start(bf16[2,64,768]{2,1,0:T(8,128)(2,1)S(1)} %constant_dynamic-update-slice_fusion.refs_5_), channel_id=1, source_target_pairs={{0,224},{32,64},{64,32},{96,128},{128,96},{160,192},{192,160},{224... | collective-permute-start | bytes 589832 | tf_op jit(solution)/shard_map/ppermute | solution.py:153
  90.9 11.4 %collective-permute-start.35 = (bf16[2,64,768]{2,1,0:T(8,128)(2,1)S(1)}, bf16[2,64,768]{2,1,0:T(8,128)(2,1)S(1)}, u32[]{:S(2)}, u32[]{:S(2)}) collective-permute-start(bf16[2,64,768]{2,1,0:T(8,128)(2,1)S(1)} %collective-permute-done.34.refs_1_), channel_id=1, source_target_pairs={{0,224},{32,64},{64,32},{96,128},{128,96},{160,192},{192,160},{224... | collective-permute-start | bytes 589832 | tf_op jit(solution)/shard_map/ppermute | solution.py:153
  94.1 8.1 %collective-permute-start.31 = (bf16[2,64,768]{2,1,0:T(8,128)(2,1)S(1)}, bf16[2,64,768]{2,1,0:T(8,128)(2,1)S(1)}, u32[]{:S(2)}, u32[]{:S(2)}) collective-permute-start(bf16[2,64,768]{2,1,0:T(8,128)(2,1)S(1)} %collective-permute-done.30.refs_2_), channel_id=1, source_target_pairs={{0,32},{32,0},{64,96},{96,64},{128,160},{160,128},{192,224},{224,1... | collective-permute-start | bytes 589832 | tf_op jit(solution)/shard_map/ppermute | solution.py:153
  94.6 11.8 %collective-permute-start.26 = (bf16[2,64,768]{2,1,0:T(8,128)(2,1)S(1)}, bf16[2,64,768]{2,1,0:T(8,128)(2,1)S(1)}, u32[]{:S(2)}, u32[]{:S(2)}) collective-permute-start(bf16[2,64,768]{2,1,0:T(8,128)(2,1)S(1)} %collective-permute-done.25.refs_6_), channel_id=1, source_target_pairs={{0,224},{32,64},{64,32},{96,128},{128,96},{160,192},{192,160},{224... | collective-permute-start | bytes 589832 | tf_op jit(solution)/shard_map/ppermute | solution.py:153
  98.0 8.4 %collective-permute-start.22 = (bf16[2,64,768]{2,1,0:T(8,128)(2,1)S(1)}, bf16[2,64,768]{2,1,0:T(8,128)(2,1)S(1)}, u32[]{:S(2)}, u32[]{:S(2)}) collective-permute-start(bf16[2,64,768]{2,1,0:T(8,128)(2,1)S(1)} %collective-permute-done.21.refs_7_), channel_id=1, source_target_pairs={{0,32},{32,0},{64,96},{96,64},{128,160},{160,128},{192,224},{224,1... | collective-permute-start | bytes 589832 | tf_op jit(solution)/shard_map/ppermute | solution.py:153
  102.2 8.1 %collective-permute-start.36 = (bf16[2,64,768]{2,1,0:T(8,128)(2,1)S(1)}, bf16[2,64,768]{2,1,0:T(8,128)(2,1)S(1)}, u32[]{:S(2)}, u32[]{:S(2)}) collective-permute-start(bf16[2,64,768]{2,1,0:T(8,128)(2,1)S(1)} %collective-permute-done.35.refs_4_), channel_id=1, source_target_pairs={{0,32},{32,0},{64,96},{96,64},{128,160},{160,128},{192,224},{224,1... | collective-permute-start | bytes 589832 | tf_op jit(solution)/shard_map/ppermute | solution.py:153
  102.2 10.6 %collective-permute-start.32 = (bf16[2,64,768]{2,1,0:T(8,128)(2,1)S(1)}, bf16[2,64,768]{2,1,0:T(8,128)(2,1)S(1)}, u32[]{:S(2)}, u32[]{:S(2)}) collective-permute-start(bf16[2,64,768]{2,1,0:T(8,128)(2,1)S(1)} %collective-permute-done.31.refs_3_), channel_id=1, source_target_pairs={{0,224},{32,64},{64,32},{96,128},{128,96},{160,192},{192,160},{224... | collective-permute-start | bytes 589832 | tf_op jit(solution)/shard_map/ppermute | solution.py:153
  106.5 7.0 %collective-permute-start.27 = (bf16[2,64,768]{2,1,0:T(8,128)(2,1)S(1)}, bf16[2,64,768]{2,1,0:T(8,128)(2,1)S(1)}, u32[]{:S(2)}, u32[]{:S(2)}) collective-permute-start(bf16[2,64,768]{2,1,0:T(8,128)(2,1)S(1)} %collective-permute-done.26.refs_3_), channel_id=1, source_target_pairs={{0,32},{32,0},{64,96},{96,64},{128,160},{160,128},{192,224},{224,1... | collective-permute-start | bytes 589832 | tf_op jit(solution)/shard_map/ppermute | solution.py:153
  106.5 9.6 %collective-permute-start.23 = (bf16[2,64,768]{2,1,0:T(8,128)(2,1)S(1)}, bf16[2,64,768]{2,1,0:T(8,128)(2,1)S(1)}, u32[]{:S(2)}, u32[]{:S(2)}) collective-permute-start(bf16[2,64,768]{2,1,0:T(8,128)(2,1)S(1)} %collective-permute-done.22.refs_2_), channel_id=1, source_target_pairs={{0,224},{32,64},{64,32},{96,128},{128,96},{160,192},{192,160},{224... | collective-permute-start | bytes 589832 | tf_op jit(solution)/shard_map/ppermute | solution.py:153
  110.3 8.5 %collective-permute-start.37 = (bf16[2,32,768]{2,1,0:T(8,128)(2,1)S(1)}, bf16[2,32,768]{2,1,0:T(8,128)(2,1)S(1)}, u32[]{:S(2)}, u32[]{:S(2)}) collective-permute-start(bf16[2,32,768]{2,1,0:T(8,128)(2,1)S(1)} %slice.39), channel_id=1, source_target_pairs={{0,224},{32,64},{64,32},{96,128},{128,96},{160,192},{192,160},{224... | collective-permute-start | bytes 294920 | tf_op jit(solution)/shard_map/ppermute | solution.py:153
  112.9 5.9 %collective-permute-start.33 = (bf16[2,32,768]{2,1,0:T(8,128)(2,1)S(1)}, bf16[2,32,768]{2,1,0:T(8,128)(2,1)S(1)}, u32[]{:S(2)}, u32[]{:S(2)}) collective-permute-start(bf16[2,32,768]{2,1,0:T(8,128)(2,1)S(1)} %slice.38), channel_id=1, source_target_pairs={{0,32},{32,0},{64,96},{96,64},{128,160},{160,128},{192,224},{224,1... | collective-permute-start | bytes 294920 | tf_op jit(solution)/shard_map/ppermute | solution.py:153
  113.5 6.3 %collective-permute-start.28 = (bf16[2,32,768]{2,1,0:T(8,128)(2,1)S(1)}, bf16[2,32,768]{2,1,0:T(8,128)(2,1)S(1)}, u32[]{:S(2)}, u32[]{:S(2)}) collective-permute-start(bf16[2,32,768]{2,1,0:T(8,128)(2,1)S(1)} %slice.37), channel_id=1, source_target_pairs={{0,224},{32,64},{64,32},{96,128},{128,96},{160,192},{192,160},{224... | collective-permute-start | bytes 294920 | tf_op jit(solution)/shard_map/ppermute | solution.py:153
  116.1 4.7 %collective-permute-start.24 = (bf16[2,32,768]{2,1,0:T(8,128)(2,1)S(1)}, bf16[2,32,768]{2,1,0:T(8,128)(2,1)S(1)}, u32[]{:S(2)}, u32[]{:S(2)}) collective-permute-start(bf16[2,32,768]{2,1,0:T(8,128)(2,1)S(1)} %slice.36), channel_id=1, source_target_pairs={{0,32},{32,0},{64,96},{96,64},{128,160},{160,128},{192,224},{224,1... | collective-permute-start | bytes 294920 | tf_op jit(solution)/shard_map/ppermute | solution.py:153
